TPU v7x, 512 devices: a whole 4x8x8 slice. The times are simulated.
512 devices in a mesh: leaf: 256 (over x, z, y), probe: 2 (over core).
Axes of the slice: x: 4, y: 8, z: 8, core: 2. Of those that a mesh axis runs over, the one named last changes fastest.
Arguments:
- features: bfloat16 [8, 786432], P(None, 'leaf'), may hold values from -5 to 5
- probes: bfloat16 [256, 786432], P('probe', 'leaf'), may hold values from -6 to 6
- lengthscale: float32 [8], replicated, may hold values from 1 to 4
- near_blocks: int32 [3072, 10], P('leaf'), may hold values from 0 to 3071, as said below
- leaf_order: int32 [256, 3072], P('leaf'), may hold values from 0 to 3071, each once within a row
Outputs:
- transfer: float32 [4, 65536, 256], P(None, 'leaf', 'probe')
- basis: float32 [786432, 256], P('leaf', 'probe')
Inputs may be any that keep to these rules, and one draw needn't show every extreme that they name: `near_blocks`: row a lists 10 distinct blocks, its first entry is a itself, and all belong to leaves a // 12 - 1 to a // 12 + 1. `leaf_order`: each row is a permutation.
All inputs are finite; a program needn't handle non-finite values.
Results may differ from a plain program's by a relative error of at most 0.0053.
Values may be sent and summed in bfloat16 or wider, within the bound.
No kernel may reach another device: no remote copies, remote signals or barrier semaphores. Data moves between devices by JAX's collectives and lax.ppermute only.
A program may use at most 128 MiB of HBM per device.

v0:
```python
import math

import jax
import jax.numpy as jnp
from jax import lax
from jax.sharding import PartitionSpec as P

LEVELS = 4


root_three = 1.7320508075688772
nugget_var = 2.0


def with_halo(cells, sides, width):
    for axis, dim in sides:
        count = lax.axis_size(axis)
        ends = count - 1
        head = lax.slice_in_dim(cells, 0, width, axis=dim)
        tail = lax.slice_in_dim(cells, cells.shape[dim] - width, cells.shape[dim], axis=dim)
        cells = jnp.concatenate(
            [
                lax.ppermute(tail, axis, [(i, (i + 1) % count) for i in range(ends)]),
                cells,
                lax.ppermute(head, axis, [((i + 1) % count, i) for i in range(ends)]),
            ],
            axis=dim,
        )
    return cells


def from_partner(array, axis, bit):
    return lax.ppermute(array, axis, [(i, i ^ 1 << bit) for i in range(lax.axis_size(axis))])


def lower_solve(lower, right):
    return lax.linalg.triangular_solve(lower, right, left_side=True, lower=True)


def body(features, probes, lengthscale, near_blocks, leaf_order):
    feat_count = features.shape[0]
    half_cols = probes.shape[0]
    leaf_len = features.shape[1]
    blk_count = near_blocks.shape[0]
    block_len = leaf_len // blk_count
    near_count = near_blocks.shape[1]
    ordered = jnp.take(features, leaf_order[0], axis=1)
    stacked = jnp.concatenate([ordered, probes], 0)
    beside_all = with_halo(stacked, (("leaf", 1),), leaf_len)
    first_block = (lax.axis_index("leaf") - 1) * blk_count
    local_ids = (near_blocks - first_block).reshape(-1)
    tiles_all = beside_all.reshape(feat_count + half_cols, 3 * blk_count, block_len)
    picked = jnp.take(tiles_all, local_ids, axis=1)
    picked = picked.reshape(feat_count + half_cols, blk_count, near_count, block_len)
    picked = jnp.moveaxis(picked, 1, 0)
    own_rows = jnp.moveaxis(stacked.reshape(feat_count + half_cols, blk_count, block_len), 1, 0)

    def one_block(inputs):
        own_panel, near_panel = inputs
        row_feat = own_panel[:feat_count].astype(jnp.float32)
        col_feat = near_panel[:feat_count].astype(jnp.float32)
        dist_sq = jnp.zeros((block_len, near_count, block_len), jnp.float32)
        for feature in range(feat_count):
            diff = (row_feat[feature][:, None, None] - col_feat[feature][None]) / lengthscale[
                feature
            ]
            dist_sq = dist_sq + diff * diff
        scaled = root_three * jnp.sqrt(dist_sq)
        kern = ((1.0 + scaled) * jnp.exp(-scaled)).astype(jnp.bfloat16)
        col_probe = near_panel[feat_count:].reshape(half_cols, near_count * block_len)
        total = lax.dot_general(
            kern.reshape(block_len, near_count * block_len),
            col_probe,
            (((1,), (1,)), ((), ())),
            preferred_element_type=jnp.float32,
        )
        return total + nugget_var * own_panel[feat_count:].astype(jnp.float32).T

    sketch = lax.map(one_block, (own_rows, picked)).reshape(leaf_len, half_cols)
    col_start = lax.axis_index("probe") * half_cols
    full_sketch = lax.all_gather(sketch, "probe", axis=1, tiled=True)
    gram = lax.dot_general(
        full_sketch,
        full_sketch,
        (((0,), (0,)), ((), ())),
        precision=lax.Precision.HIGHEST,
        preferred_element_type=jnp.float32,
    )
    grams = [gram]
    for depth in range(LEVELS):
        gram = gram + from_partner(gram, "leaf", depth)
        grams.append(gram)
    factors = [jnp.linalg.cholesky(item) for item in grams]
    pieces = []
    for depth in range(1, LEVELS + 1):
        mixed = lower_solve(factors[depth], factors[depth - 1])
        chosen = lax.dynamic_slice_in_dim(mixed, col_start, half_cols, 0)
        pieces.append(chosen.T)
    transfer = jnp.stack(pieces, 0)
    factor_top = math.sqrt(2**LEVELS * leaf_len)
    solved = lower_solve(factors[LEVELS], full_sketch.T)
    basis = lax.dynamic_slice_in_dim(solved, col_start, half_cols, 0).T * factor_top
    return (transfer, basis)


def solution(mesh):
    in_specs = (P(None, "leaf"), P("probe", "leaf"), P(), P("leaf", None), P("leaf", None))
    out_specs = (P(None, "leaf", "probe"), P("leaf", "probe"))
    return jax.shard_map(body, mesh=mesh, in_specs=in_specs, out_specs=out_specs, check_vma=False)
```

profile of v0, /device:TPU:6, one launch (start us, length us, event | category | flops | bytes accessed | tf_op | source)
XLA Modules:
  0.0 677.5 jit_solution(11529364420537995498)
XLA Ops:
  24.5 12.6 %collective-permute-start.1 = (bf16[136,3072]{1,0:T(8,128)(2,1)S(1)}, bf16[136,3072]{1,0:T(8,128)(2,1)S(1)}, u32[]{:S(2)}, u32[]{:S(2)}) collective-permute-start(bf16[136,3072]{1,0:T(8,128)(2,1)S(1)} %pad_maximum_fusion.1), channel_id=1, source_target_pairs={{2,0},{4,2},{6,4},{8,6},{10,8},{12,10},{14,12},{16,14},{18,16},{20... | collective-permute-start | bytes 2506760 | tf_op jit(solution)/shard_map/ppermute | solution.py:25
  38.7 15.0 %collective-permute-done = bf16[136,3072]{1,0:T(8,128)(2,1)S(1)} collective-permute-done((bf16[136,3072]{1,0:T(8,128)(2,1)S(1)}, bf16[136,3072]{1,0:T(8,128)(2,1)S(1)}, u32[]{:S(2)}, u32[]{:S(2)}) %collective-permute-start) | collective-permute-done | bytes 835616 | tf_op jit(solution)/shard_map/ppermute | solution.py:23
  69.4 248.2 %while.19 = (s32[]{:T(128)}, f32[12,256,128]{2,1,0:T(8,128)}, bf16[12,136,256]{1,2,0:T(8,128)(2,1)}, bf16[12,136,10,256]{3,1,2,0:T(8,128)(2,1)}, f32[8]{0:T(128)S(1)}, /*index=5*/s32[]{:T(128)}, s32[]{:T(128)}, s32[]{}) while((s32[]{:T(128)}, f32[12,256,128]{2,1,0:T(8,128)}, bf16[12,136,256]{1,2,0:T(8,128)(2,1)}, ...), condition=%wide.region_1.2_spmd, body=%wide.region_0.1_spmd.sunk | while | flops 191485952 | bytes 4211381 | solution.py:79
  80.0 10.5 %fusion.102 = f32[12,256,128]{2,1,0:T(8,128)} fusion(f32[12,256,128]{2,1,0:T(8,128)} %get-tuple-element.399, s32[]{:T(128)} %get-tuple-element.398, bf16[128,2560]{0,1:T(8,128)(2,1)S(1)} %bitcast.234, f32[]{:T(128)} %bitcast.210, f32[2560]{0:T(1024)S(1)} %sub.408, f32[256]{0:T(256)S(1)} %get-tuple-element.344, f32[]{:T(128)} %bitcast.211, ...), kind=kOutput, calls=%fused_computation.22.clone.1 | convolution fusion | flops 191463424 | bytes 946692 | tf_op jit(solution)/shard_map/while/body/eval_jaxpr/dot_general | solution.py:71
  100.6 10.5 %fusion.102 = f32[12,256,128]{2,1,0:T(8,128)} fusion(f32[12,256,128]{2,1,0:T(8,128)} %get-tuple-element.399, s32[]{:T(128)} %get-tuple-element.398, bf16[128,2560]{0,1:T(8,128)(2,1)S(1)} %bitcast.234, f32[]{:T(128)} %bitcast.210, f32[2560]{0:T(1024)S(1)} %sub.408, f32[256]{0:T(256)S(1)} %get-tuple-element.344, f32[]{:T(128)} %bitcast.211, ...), kind=kOutput, calls=%fused_computation.22.clone.1 | convolution fusion | flops 191463424 | bytes 946692 | tf_op jit(solution)/shard_map/while/body/eval_jaxpr/dot_general | solution.py:71
  121.2 10.5 %fusion.102 = f32[12,256,128]{2,1,0:T(8,128)} fusion(f32[12,256,128]{2,1,0:T(8,128)} %get-tuple-element.399, s32[]{:T(128)} %get-tuple-element.398, bf16[128,2560]{0,1:T(8,128)(2,1)S(1)} %bitcast.234, f32[]{:T(128)} %bitcast.210, f32[2560]{0:T(1024)S(1)} %sub.408, f32[256]{0:T(256)S(1)} %get-tuple-element.344, f32[]{:T(128)} %bitcast.211, ...), kind=kOutput, calls=%fused_computation.22.clone.1 | convolution fusion | flops 191463424 | bytes 946692 | tf_op jit(solution)/shard_map/while/body/eval_jaxpr/dot_general | solution.py:71
  141.8 10.5 %fusion.102 = f32[12,256,128]{2,1,0:T(8,128)} fusion(f32[12,256,128]{2,1,0:T(8,128)} %get-tuple-element.399, s32[]{:T(128)} %get-tuple-element.398, bf16[128,2560]{0,1:T(8,128)(2,1)S(1)} %bitcast.234, f32[]{:T(128)} %bitcast.210, f32[2560]{0:T(1024)S(1)} %sub.408, f32[256]{0:T(256)S(1)} %get-tuple-element.344, f32[]{:T(128)} %bitcast.211, ...), kind=kOutput, calls=%fused_computation.22.clone.1 | convolution fusion | flops 191463424 | bytes 946692 | tf_op jit(solution)/shard_map/while/body/eval_jaxpr/dot_general | solution.py:71
  162.5 10.5 %fusion.102 = f32[12,256,128]{2,1,0:T(8,128)} fusion(f32[12,256,128]{2,1,0:T(8,128)} %get-tuple-element.399, s32[]{:T(128)} %get-tuple-element.398, bf16[128,2560]{0,1:T(8,128)(2,1)S(1)} %bitcast.234, f32[]{:T(128)} %bitcast.210, f32[2560]{0:T(1024)S(1)} %sub.408, f32[256]{0:T(256)S(1)} %get-tuple-element.344, f32[]{:T(128)} %bitcast.211, ...), kind=kOutput, calls=%fused_computation.22.clone.1 | convolution fusion | flops 191463424 | bytes 946692 | tf_op jit(solution)/shard_map/while/body/eval_jaxpr/dot_general | solution.py:71
  183.1 10.5 %fusion.102 = f32[12,256,128]{2,1,0:T(8,128)} fusion(f32[12,256,128]{2,1,0:T(8,128)} %get-tuple-element.399, s32[]{:T(128)} %get-tuple-element.398, bf16[128,2560]{0,1:T(8,128)(2,1)S(1)} %bitcast.234, f32[]{:T(128)} %bitcast.210, f32[2560]{0:T(1024)S(1)} %sub.408, f32[256]{0:T(256)S(1)} %get-tuple-element.344, f32[]{:T(128)} %bitcast.211, ...), kind=kOutput, calls=%fused_computation.22.clone.1 | convolution fusion | flops 191463424 | bytes 946692 | tf_op jit(solution)/shard_map/while/body/eval_jaxpr/dot_general | solution.py:71
  203.7 10.5 %fusion.102 = f32[12,256,128]{2,1,0:T(8,128)} fusion(f32[12,256,128]{2,1,0:T(8,128)} %get-tuple-element.399, s32[]{:T(128)} %get-tuple-element.398, bf16[128,2560]{0,1:T(8,128)(2,1)S(1)} %bitcast.234, f32[]{:T(128)} %bitcast.210, f32[2560]{0:T(1024)S(1)} %sub.408, f32[256]{0:T(256)S(1)} %get-tuple-element.344, f32[]{:T(128)} %bitcast.211, ...), kind=kOutput, calls=%fused_computation.22.clone.1 | convolution fusion | flops 191463424 | bytes 946692 | tf_op jit(solution)/shard_map/while/body/eval_jaxpr/dot_general | solution.py:71
  224.3 10.5 %fusion.102 = f32[12,256,128]{2,1,0:T(8,128)} fusion(f32[12,256,128]{2,1,0:T(8,128)} %get-tuple-element.399, s32[]{:T(128)} %get-tuple-element.398, bf16[128,2560]{0,1:T(8,128)(2,1)S(1)} %bitcast.234, f32[]{:T(128)} %bitcast.210, f32[2560]{0:T(1024)S(1)} %sub.408, f32[256]{0:T(256)S(1)} %get-tuple-element.344, f32[]{:T(128)} %bitcast.211, ...), kind=kOutput, calls=%fused_computation.22.clone.1 | convolution fusion | flops 191463424 | bytes 946692 | tf_op jit(solution)/shard_map/while/body/eval_jaxpr/dot_general | solution.py:71
  245.0 10.5 %fusion.102 = f32[12,256,128]{2,1,0:T(8,128)} fusion(f32[12,256,128]{2,1,0:T(8,128)} %get-tuple-element.399, s32[]{:T(128)} %get-tuple-element.398, bf16[128,2560]{0,1:T(8,128)(2,1)S(1)} %bitcast.234, f32[]{:T(128)} %bitcast.210, f32[2560]{0:T(1024)S(1)} %sub.408, f32[256]{0:T(256)S(1)} %get-tuple-element.344, f32[]{:T(128)} %bitcast.211, ...), kind=kOutput, calls=%fused_computation.22.clone.1 | convolution fusion | flops 191463424 | bytes 946692 | tf_op jit(solution)/shard_map/while/body/eval_jaxpr/dot_general | solution.py:71
  265.6 10.5 %fusion.102 = f32[12,256,128]{2,1,0:T(8,128)} fusion(f32[12,256,128]{2,1,0:T(8,128)} %get-tuple-element.399, s32[]{:T(128)} %get-tuple-element.398, bf16[128,2560]{0,1:T(8,128)(2,1)S(1)} %bitcast.234, f32[]{:T(128)} %bitcast.210, f32[2560]{0:T(1024)S(1)} %sub.408, f32[256]{0:T(256)S(1)} %get-tuple-element.344, f32[]{:T(128)} %bitcast.211, ...), kind=kOutput, calls=%fused_computation.22.clone.1 | convolution fusion | flops 191463424 | bytes 946692 | tf_op jit(solution)/shard_map/while/body/eval_jaxpr/dot_general | solution.py:71
  286.2 10.5 %fusion.102 = f32[12,256,128]{2,1,0:T(8,128)} fusion(f32[12,256,128]{2,1,0:T(8,128)} %get-tuple-element.399, s32[]{:T(128)} %get-tuple-element.398, bf16[128,2560]{0,1:T(8,128)(2,1)S(1)} %bitcast.234, f32[]{:T(128)} %bitcast.210, f32[2560]{0:T(1024)S(1)} %sub.408, f32[256]{0:T(256)S(1)} %get-tuple-element.344, f32[]{:T(128)} %bitcast.211, ...), kind=kOutput, calls=%fused_computation.22.clone.1 | convolution fusion | flops 191463424 | bytes 946692 | tf_op jit(solution)/shard_map/while/body/eval_jaxpr/dot_general | solution.py:71
  306.8 10.5 %fusion.102 = f32[12,256,128]{2,1,0:T(8,128)} fusion(f32[12,256,128]{2,1,0:T(8,128)} %get-tuple-element.399, s32[]{:T(128)} %get-tuple-element.398, bf16[128,2560]{0,1:T(8,128)(2,1)S(1)} %bitcast.234, f32[]{:T(128)} %bitcast.210, f32[2560]{0:T(1024)S(1)} %sub.408, f32[256]{0:T(256)S(1)} %get-tuple-element.344, f32[]{:T(128)} %bitcast.211, ...), kind=kOutput, calls=%fused_computation.22.clone.1 | convolution fusion | flops 191463424 | bytes 946692 | tf_op jit(solution)/shard_map/while/body/eval_jaxpr/dot_general | solution.py:71
  317.6 16.7 %all-gather.2.cloned.1.call-done = f32[3072,256]{1,0:T(8,128)} async-done(((f32[3072,128]{1,0:T(8,128)}), f32[3072,256]{1,0:T(8,128)}) %all-gather.2.cloned.1.call-update) | async-done | bytes 3145744 | tf_op jit(solution)/shard_map/all_gather | solution.py:81
  345.8 11.7 %cholesky.290 = f32[128,128]{1,0:T(8,128)S(1)} custom-call(f32[128,128]{1,0:T(8,128)S(1)} %cholesky.425), custom_call_target="Cholesky" | custom-call | tf_op jit(solution)/shard_map/jit(cholesky)/cholesky | solution.py:93
  367.9 11.7 %cholesky.307 = f32[128,128]{1,0:T(8,128)S(1)} custom-call(f32[128,128]{1,0:T(8,128)S(1)} %convolution_subtract_fusion.5), custom_call_target="Cholesky" | custom-call | tf_op jit(solution)/shard_map/jit(cholesky)/cholesky | solution.py:93
  387.2 11.7 %cholesky.256 = f32[128,128]{1,0:T(8,128)S(1)} custom-call(f32[128,128]{1,0:T(8,128)S(1)} %cholesky.422), custom_call_target="Cholesky" | custom-call | tf_op jit(solution)/shard_map/jit(cholesky)/cholesky | solution.py:93
  409.3 11.7 %cholesky.273 = f32[128,128]{1,0:T(8,128)S(1)} custom-call(f32[128,128]{1,0:T(8,128)S(1)} %slice_subtract_fusion.3), custom_call_target="Cholesky" | custom-call | tf_op jit(solution)/shard_map/jit(cholesky)/cholesky | solution.py:93
  427.9 19.7 %custom-call.24 = f32[2,128,128]{1,2,0:T(8,128)S(1)} custom-call(f32[2,128,128]{2,1,0:T(8,128)S(1)} %get-tuple-element.66), custom_call_target="InvertDiagBlocksLowerTriangular" | custom-call | tf_op jit(solution)/shard_map/triangular_solve/custom-call.0 | solution.py:37
  453.4 11.7 %cholesky.324 = f32[128,128]{1,0:T(8,128)S(1)} custom-call(f32[128,128]{1,0:T(8,128)S(1)} %cholesky.428), custom_call_target="Cholesky" | custom-call | tf_op jit(solution)/shard_map/jit(cholesky)/cholesky | solution.py:93
  465.1 9.8 %custom-call.25 = f32[1,128,128]{1,2,0:T(8,128)S(1)} custom-call(f32[1,128,128]{2,1,0:T(8,128)S(1)} %get-tuple-element.172), custom_call_target="InvertDiagBlocksLowerTriangular" | custom-call | tf_op jit(solution)/shard_map/jit(cholesky)/cholesky | solution.py:93
  475.5 11.7 %cholesky.341 = f32[128,128]{1,0:T(8,128)S(1)} custom-call(f32[128,128]{1,0:T(8,128)S(1)} %slice_subtract_fusion.2), custom_call_target="Cholesky" | custom-call | tf_op jit(solution)/shard_map/jit(cholesky)/cholesky | solution.py:93
  493.9 19.7 %custom-call.26 = f32[2,128,128]{1,2,0:T(8,128)S(1)} custom-call(f32[2,128,128]{2,1,0:T(8,128)S(1)} %get-tuple-element.67), custom_call_target="InvertDiagBlocksLowerTriangular" | custom-call | tf_op jit(solution)/shard_map/triangular_solve/custom-call.0 | solution.py:37
  519.1 11.7 %cholesky.358 = f32[128,128]{1,0:T(8,128)S(1)} custom-call(f32[128,128]{1,0:T(8,128)S(1)} %cholesky.431), custom_call_target="Cholesky" | custom-call | tf_op jit(solution)/shard_map/jit(cholesky)/cholesky | solution.py:93
  541.2 11.7 %cholesky.375 = f32[128,128]{1,0:T(8,128)S(1)} custom-call(f32[128,128]{1,0:T(8,128)S(1)} %slice_subtract_fusion.1), custom_call_target="Cholesky" | custom-call | tf_op jit(solution)/shard_map/jit(cholesky)/cholesky | solution.py:93
  560.4 19.8 %custom-call.28 = f32[2,128,128]{1,2,0:T(8,128)S(1)} custom-call(f32[2,128,128]{2,1,0:T(8,128)S(1)} %get-tuple-element.68), custom_call_target="InvertDiagBlocksLowerTriangular" | custom-call | tf_op jit(solution)/shard_map/triangular_solve/custom-call.0 | solution.py:37
  587.6 11.7 %cholesky.392 = f32[128,128]{1,0:T(8,128)S(1)} custom-call(f32[128,128]{1,0:T(8,128)S(1)} %cholesky.434), custom_call_target="Cholesky" | custom-call | tf_op jit(solution)/shard_map/jit(cholesky)/cholesky | solution.py:93
  601.4 11.3 %custom-call.29 = f32[1,128,128]{1,2,0:T(8,128)} custom-call(f32[1,128,128]{2,1,0:T(8,128)} %get-tuple-element.176), custom_call_target="InvertDiagBlocksLowerTriangular" | custom-call | tf_op jit(solution)/shard_map/jit(cholesky)/cholesky | solution.py:93
  615.5 13.2 %cholesky.409 = f32[128,128]{1,0:T(8,128)} custom-call(f32[128,128]{1,0:T(8,128)} %slice_subtract_fusion), custom_call_target="Cholesky" | custom-call | tf_op jit(solution)/shard_map/jit(cholesky)/cholesky | solution.py:93
  638.5 21.3 %custom-call.30 = f32[2,128,128]{1,2,0:T(8,128)} custom-call(f32[2,128,128]{2,1,0:T(8,128)} %get-tuple-element.69), custom_call_target="InvertDiagBlocksLowerTriangular" | custom-call | tf_op jit(solution)/shard_map/triangular_solve/custom-call.0 | solution.py:37
  (380 shorter events, 280.1 us)
Async XLA Ops:
  7.2 13.8 %copy-start.1 = (bf16[128,3072]{1,0:T(8,128)(2,1)S(1)}, bf16[128,3072]{1,0:T(8,128)(2,1)}, u32[]{:S(2)}) copy-start(bf16[128,3072]{1,0:T(8,128)(2,1)} %param.11) | copy-start | bytes 2359300
  7.2 327.1 %all-gather.2.cloned.1.call-start = ((), (), s32[]{:S(2)}) async-start(), calls=%async_computation | async-start | bytes 4718592 | tf_op jit(solution)/shard_map/all_gather | solution.py:81
  20.7 17.9 %copy-start.13 = (s32[12,10]{1,0:T(8,128)S(1)}, s32[12,10]{1,0:T(8,128)}, u32[]{:S(2)}) copy-start(s32[12,10]{1,0:T(8,128)} %param.13) | copy-start | bytes 1444
  21.0 32.7 %collective-permute-start = (bf16[136,3072]{1,0:T(8,128)(2,1)S(1)}, bf16[136,3072]{1,0:T(8,128)(2,1)S(1)}, u32[]{:S(2)}, u32[]{:S(2)}) collective-permute-start(bf16[136,3072]{1,0:T(8,128)(2,1)S(1)} %pad_maximum_fusion.1), channel_id=1, source_target_pairs={{0,2},{2,4},{4,6},{6,8},{8,10},{10,12},{12,14},{14,16},{16,18},{18... | collective-permute-start | bytes 2506760 | tf_op jit(solution)/shard_map/ppermute | solution.py:23
  24.5 30.4 %collective-permute-start.1 = (bf16[136,3072]{1,0:T(8,128)(2,1)S(1)}, bf16[136,3072]{1,0:T(8,128)(2,1)S(1)}, u32[]{:S(2)}, u32[]{:S(2)}) collective-permute-start(bf16[136,3072]{1,0:T(8,128)(2,1)S(1)} %pad_maximum_fusion.1), channel_id=1, source_target_pairs={{2,0},{4,2},{6,4},{8,6},{10,8},{12,10},{14,12},{16,14},{18,16},{20... | collective-permute-start | bytes 2506760 | tf_op jit(solution)/shard_map/ppermute | solution.py:25
  62.0 7.4 %copy-start.4 = (f32[8]{0:T(128)S(1)}, f32[8]{0:T(128)}, u32[]{:S(2)}) copy-start(f32[8]{0:T(128)} %param.12) | copy-start | bytes 100
  342.4 39.9 %collective-permute-start.2 = (f32[256,256]{0,1:T(8,128)S(1)}, f32[256,256]{0,1:T(8,128)S(1)}, u32[]{:S(2)}, u32[]{:S(2)}) collective-permute-start(f32[256,256]{0,1:T(8,128)S(1)} %copy.25), channel_id=1, source_target_pairs={{0,2},{2,0},{4,6},{6,4},{8,10},{10,8},{12,14},{14,12},{16,18},{18,... | collective-permute-start | bytes 786440 | tf_op jit(solution)/shard_map/ppermute | solution.py:33
  382.3 66.2 %collective-permute-start.3 = (f32[256,256]{0,1:T(8,128)S(1)}, f32[256,256]{0,1:T(8,128)S(1)}, u32[]{:S(2)}, u32[]{:S(2)}) collective-permute-start(f32[256,256]{0,1:T(8,128)S(1)} %add.128), channel_id=1, source_target_pairs={{0,4},{2,6},{4,0},{6,2},{8,12},{10,14},{12,8},{14,10},{16,20},{18,... | collective-permute-start | bytes 786440 | tf_op jit(solution)/shard_map/ppermute | solution.py:33
  448.5 66.8 %collective-permute-start.4 = (f32[256,256]{0,1:T(8,128)S(1)}, f32[256,256]{0,1:T(8,128)S(1)}, u32[]{:S(2)}, u32[]{:S(2)}) collective-permute-start(f32[256,256]{0,1:T(8,128)S(1)} %add.130), channel_id=1, source_target_pairs={{0,8},{2,10},{4,12},{6,14},{8,0},{10,2},{12,4},{14,6},{16,24},{18,... | collective-permute-start | bytes 786440 | tf_op jit(solution)/shard_map/ppermute | solution.py:33
  515.3 67.8 %collective-permute-start.5 = (f32[256,256]{0,1:T(8,128)S(1)}, f32[256,256]{0,1:T(8,128)}, u32[]{:S(2)}, u32[]{:S(2)}) collective-permute-start(f32[256,256]{0,1:T(8,128)S(1)} %add.131), channel_id=1, source_target_pairs={{0,16},{2,18},{4,20},{6,22},{8,24},{10,26},{12,28},{14,30},{16,0},... | collective-permute-start | bytes 786440 | tf_op jit(solution)/shard_map/ppermute | solution.py:33
  580.2 0.7 copy-start.12
  581.1 78.7 %copy-start = (f32[3072,256]{1,0:T(8,128)S(1)}, f32[3072,256]{1,0:T(8,128)}, u32[]{:S(2)}) copy-start(f32[3072,256]{1,0:T(8,128)} %all-gather.2.cloned.1.call-done) | copy-start | bytes 9437188
  586.8 0.7 copy-start.5
  599.3 0.6 copy-start.11
  629.5 2.4 copy-start.2
  662.1 2.7 copy-start.6
  666.7 1.7 copy-start.3
  666.7 1.7 copy-start.7
  666.7 2.6 copy-start.8
  666.8 2.6 copy-start.9
  666.8 2.6 copy-start.10
Sparse Core Ops, SparseCore 0:
  317.7 16.5 all-gather.1
where the time goes:
time: 691 us; the launch traced here: 678 us
  other arithmetic  286 us (41%)
  local copies, waits for them, and re-layouts  152 us (22%)
  matrix products  151 us (22%)
  waiting for transfers between devices  32.9 us (5%)
  starting transfers between devices  32.4 us (5%)
  between operations  21.2 us (3%)
    another operation x35, other arithmetic, body(): factors = [jnp.linalg.cholesky(item) for item in grams]  177 us
    dot_general x12, matrix products, one_block(): lax.dot_general(kern.reshape(block_len, near_count * block_len), col_prob...  127 us
    another operation x9, other arithmetic, lower_solve(): return lax.linalg.triangular_solve(lower, right, left_side=True, lower=True)  82.3 us
    slice x12, local copies, waits for them, and re-layouts, one_block(): col_feat[feature][None]  61.8 us
    another operation x29, local copies, waits for them, and re-layouts, lower_solve(): return lax.linalg.triangular_solve(lower, right, left_side=True, lower=True)  17.4 us
    all_gather x1, waiting for transfers between devices, body(): full_sketch = lax.all_gather(sketch, 'probe', axis=1, tiled=True)  16.7 us
    ppermute x4, starting transfers between devices, from_partner(): lax.ppermute(array, axis, [(i, i ^ 1 << bit) for i in range(lax.axis_size...  16.3 us
    ppermute x1, waiting for transfers between devices, with_halo(): lax.ppermute(tail, axis, [(i, (i + 1) % count) for i in range(ends)])  15 us
  transfers between devices with their start and end apart: 7, of which 3 were waited for; matrix products, arithmetic and copies ran while one was open for 32% of the time, Pallas kernels for 0%

commit v1 on v0

v1 whole, which is shorter than its diff:
```python
import math

import jax
import jax.numpy as jnp
from jax import lax
from jax.experimental import pallas as pl
from jax.experimental.pallas import tpu as pltpu
from jax.sharding import PartitionSpec as P

LEVELS = 4
LANES = 128
ROWS = 8
LOG2_E = 1.4426950408889634
LN_2 = 0.6931471805599453
NUGGET = 2.0
TINY = 1e-20
HI = lax.Precision.HIGHEST
F32 = jnp.float32
BF16 = jnp.bfloat16
VMEM_BYTES = 48 << 20


def call(kernel, out_shape, **kwargs):
    return pl.pallas_call(
        kernel,
        out_shape=out_shape,
        compiler_params=pltpu.CompilerParams(vmem_limit_bytes=VMEM_BYTES),
        **kwargs,
    )


def dot(a, b, ca, cb, precision=HI):
    return lax.dot_general(
        a, b, (((ca,), (cb,)), ((), ())), precision=precision, preferred_element_type=F32
    )


def dot16(a, b, ca, cb):
    return lax.dot_general(a, b, (((ca,), (cb,)), ((), ())), preferred_element_type=F32)


def halves(x):
    hi = x.astype(BF16)
    return hi, (x - hi.astype(F32)).astype(BF16)


def thirds(x):
    hi = x.astype(BF16).astype(F32)
    rest = x - hi
    mid = rest.astype(BF16).astype(F32)
    return hi, mid, rest - mid


def order_kernel(feat, order, out):
    chunks = feat.shape[1] // LANES
    pieces = [feat[:, c * LANES : (c + 1) * LANES].astype(F32) for c in range(chunks)]

    def one(q, carry):
        at = pl.multiple_of(q * LANES, LANES)
        index = jnp.broadcast_to(order[:, pl.ds(at, LANES)], (ROWS, LANES))
        low, high = index & (LANES - 1), index >> 7
        total = jnp.zeros((ROWS, LANES), F32)
        for c in range(chunks):
            total = jnp.where(high == c, jnp.take_along_axis(pieces[c], low, axis=1), total)
        out[:, pl.ds(at, LANES)] = total.astype(BF16)
        return carry

    lax.fori_loop(0, chunks, one, 0)


def order_features(features, leaf_order):
    return call(order_kernel, jax.ShapeDtypeStruct(features.shape, BF16))(features, leaf_order)


def tile_kernel(ids, own, left, right, scale, out, rows_t, cols):
    step = pl.program_id(0)
    leaf = own.shape[1]
    near = ids.shape[1]
    block = rows_t.shape[0] // pl.num_programs(0)

    @pl.when(step == 0)
    def _():
        weight = (3.0 * LOG2_E * LOG2_E) / (scale[...] * scale[...])
        for n, ref in enumerate((left, own, right)):
            x = ref[...].astype(F32)
            norm = jnp.sum(x * x * weight, 0, keepdims=True)
            norms = thirds(norm)
            ones = jnp.ones_like(norm)
            zeros = jnp.zeros((2, leaf), F32)
            cols[:, n * leaf : (n + 1) * leaf] = jnp.concatenate(
                [x, x, x, *norms, ones, ones, ones, zeros], 0
            ).astype(BF16)
            if n == 1:
                parts = thirds(-2.0 * weight * x)
                rows_t[...] = jnp.concatenate(
                    [*parts, ones, ones, ones, *norms, zeros], 0
                ).T.astype(BF16)

    mine = rows_t[pl.ds(pl.multiple_of(step * block, block), block), :]
    for j in range(near):
        at = pl.multiple_of(ids[step, j] * block, block)
        dist = dot16(mine, cols[:, pl.ds(at, block)], 1, 0)
        dist = jnp.maximum(dist, TINY)
        root = dist * lax.rsqrt(dist)
        kern = (1.0 + LN_2 * root) * jnp.exp2(-root)
        if j == 0:
            here = lax.broadcasted_iota(jnp.int32, (block, block), 0)
            there = lax.broadcasted_iota(jnp.int32, (block, block), 1)
            kern = jnp.where(here == there, kern + NUGGET, kern)
        out[0, :, j * block : (j + 1) * block] = kern.astype(BF16)


def kernel_tiles(ids, own, left, right, scale):
    leaf = own.shape[1]
    blocks, near = ids.shape
    block = leaf // blocks
    whole = pl.BlockSpec(memory_space=pltpu.VMEM)
    return call(
        tile_kernel,
        jax.ShapeDtypeStruct((blocks, block, near * block), BF16),
        grid_spec=pltpu.PrefetchScalarGridSpec(
            num_scalar_prefetch=1,
            grid=(blocks,),
            in_specs=[whole] * 4,
            out_specs=pl.BlockSpec((1, block, near * block), lambda i, ids: (i, 0, 0)),
            scratch_shapes=[pltpu.VMEM((leaf, 32), BF16), pltpu.VMEM((32, 3 * leaf), BF16)],
        ),
    )(ids, own, left, right, scale)


def sketch_kernel(ids, tiles, left, own, right, out, panel):
    step = pl.program_id(0)
    near = ids.shape[1]
    leaf = own.shape[1]
    block = tiles.shape[1]

    @pl.when(step == 0)
    def _():
        for n, ref in enumerate((left, own, right)):
            panel[:, n * leaf : (n + 1) * leaf] = ref[...]

    total = jnp.zeros(out.shape, F32)
    for j in range(near):
        at = pl.multiple_of(ids[step, j] * block, block)
        total += dot16(tiles[0, :, j * block : (j + 1) * block], panel[:, pl.ds(at, block)], 1, 1)
    out[...] = total


def sketch_rows(ids, tiles, left, own, right):
    half, leaf = own.shape
    blocks, block, width = tiles.shape
    whole = pl.BlockSpec(memory_space=pltpu.VMEM)
    return call(
        sketch_kernel,
        jax.ShapeDtypeStruct((leaf, half), F32),
        grid_spec=pltpu.PrefetchScalarGridSpec(
            num_scalar_prefetch=1,
            grid=(blocks,),
            in_specs=[pl.BlockSpec((1, block, width), lambda i, ids: (i, 0, 0))] + [whole] * 3,
            out_specs=pl.BlockSpec((block, half), lambda i, ids: (i, 0)),
            scratch_shapes=[pltpu.VMEM((half, 3 * leaf), BF16)],
        ),
    )(ids, tiles, left, own, right)


def gram_kernel(me, own, other, out):
    @pl.when(pl.program_id(0) == 0)
    def _():
        out[...] = jnp.zeros_like(out)

    def add(first, second):
        a0, a1 = halves(first)
        b0, b1 = halves(second)
        n = a0.shape[1]
        out[0:n] += dot16(a0, a0, 0, 0) + (dot16(a0, a1, 0, 0) + dot16(a1, a0, 0, 0))
        out[n : 2 * n] += dot16(b0, a0, 0, 0) + (dot16(b0, a1, 0, 0) + dot16(b1, a0, 0, 0))
        out[2 * n :] += dot16(b0, b0, 0, 0) + (dot16(b0, b1, 0, 0) + dot16(b1, b0, 0, 0))

    @pl.when(me[0] == 0)
    def _():
        add(own[...], other[...])

    @pl.when(me[0] == 1)
    def _():
        add(other[...], own[...])


def gram_blocks(me, own, other):
    leaf, half = own.shape
    steps = 4
    rows = pl.BlockSpec((leaf // steps, half), lambda i, me: (i, 0))
    return call(
        gram_kernel,
        jax.ShapeDtypeStruct((3 * half, half), F32),
        grid_spec=pltpu.PrefetchScalarGridSpec(
            num_scalar_prefetch=1,
            grid=(steps,),
            in_specs=[rows, rows],
            out_specs=pl.BlockSpec((3 * half, half), lambda i, me: (0, 0)),
        ),
    )(me, own, other)


def outer_sum(a, b):
    a0, a1, a2 = thirds(a)
    b0, b1, b2 = thirds(b)
    left = jnp.concatenate([a0, a0, a1, a0, a1, a2], 0).astype(BF16)
    right = jnp.concatenate([b0, b1, b0, b2, b1, b0], 0).astype(BF16)
    return dot16(left, right, 0, 0)


def eliminate(panels, units, diags):
    count = range(len(panels))
    tile = (ROWS, LANES)
    full = [[[None] * ROWS for _ in range(ROWS)] for _ in count]
    for m in range(ROWS):
        cols = [jnp.broadcast_to(diags[l][:, m : m + 1], tile) for l in count]
        for i in range(m, ROWS):
            for l in count:
                full[l][i][m] = jnp.broadcast_to(cols[l][i : i + 1, :], tile)
    rows = [[jnp.broadcast_to(panels[l][i : i + 1, :], tile) for i in range(ROWS)] for l in count]
    unit = [[jnp.broadcast_to(units[l][i : i + 1, :], tile) for i in range(ROWS)] for l in count]
    for k in range(ROWS):
        inv = [lax.rsqrt(full[l][k][k]) for l in count]
        low = [[None] * ROWS for _ in count]
        for i in range(k + 1, ROWS):
            for l in count:
                low[l][i] = full[l][i][k] * inv[l]
        for j in range(k + 1, ROWS):
            for i in range(j, ROWS):
                for l in count:
                    full[l][i][j] = full[l][i][j] - low[l][i] * low[l][j]
        for l in count:
            rows[l][k] = rows[l][k] * inv[l]
            unit[l][k] = unit[l][k] * inv[l]
        for i in range(k + 1, ROWS):
            for l in count:
                rows[l][i] = rows[l][i] - low[l][i] * rows[l][k]
                unit[l][i] = unit[l][i] - low[l][i] * unit[l][k]
    sub = lax.broadcasted_iota(jnp.int32, tile, 0)
    outs, invs = [], []
    for l in count:
        out, inv = rows[l][0], unit[l][0]
        for i in range(1, ROWS):
            out = jnp.where(sub == i, rows[l][i], out)
            inv = jnp.where(sub == i, unit[l][i], inv)
        outs.append(out)
        invs.append(inv)
    return outs, invs


def factor_block(work, ups, invs, base):
    count = range(work.shape[0])
    tile = (ROWS, LANES)
    lane = lax.broadcasted_iota(jnp.int32, tile, 1)
    sub = lax.broadcasted_iota(jnp.int32, tile, 0)
    lane_all = lax.broadcasted_iota(jnp.int32, (LANES, LANES), 1)
    span = slice(base, base + LANES)

    def step(j, carry):
        at = pl.multiple_of(j * ROWS, ROWS)
        here = (lane >= at) & (lane < at + ROWS)
        unit = jnp.where(lane - at == sub, 1.0, 0.0)
        panels = [work[l, pl.ds(at, ROWS), :] for l in count]
        diags = [pltpu.roll(panel, LANES - at, 1) for panel in panels]
        outs, units = eliminate(panels, [unit] * len(panels), diags)
        fulls = [jnp.where(here, units[l], outs[l]) for l in count]
        lefts = [jnp.where(lane >= at + ROWS, outs[l], 0.0) for l in count]
        sums = [outer_sum(lefts[l], fulls[l]) for l in count]
        gone = (lane_all >= at) & (lane_all < at + ROWS)
        rests = [jnp.where(gone, 0.0, work[l]) - sums[l] for l in count]
        for l in count:
            ups[l, pl.ds(base + at, ROWS), span] = jnp.where(lane >= at, outs[l], 0.0)
            invs[l, pl.ds(base + at, ROWS), span] = jnp.where(lane < at + ROWS, fulls[l], 0.0)
            work[l] = rests[l]
        return carry

    lax.fori_loop(0, LANES // ROWS, step, 0)


def factor(grams, work, ups, invs):
    n = LANES
    blank = jnp.zeros((n, n), F32)
    count = range(work.shape[0])
    for l in count:
        work[l] = grams(l, 0)
    factor_block(work, ups, invs, 0)
    for l in count:
        side = dot(invs[l, 0:n, 0:n], grams(l, 1), 1, 1)
        ups[l, 0:n, n : 2 * n] = side
        ups[l, n : 2 * n, 0:n] = blank
        invs[l, 0:n, n : 2 * n] = blank
        work[l] = grams(l, 2) - dot(side, side, 0, 0)
    factor_block(work, ups, invs, n)
    for l in count:
        down = dot(ups[l, 0:n, n : 2 * n], invs[l, 0:n, 0:n], 0, 0)
        invs[l, n : 2 * n, 0:n] = -dot(invs[l, n : 2 * n, n : 2 * n], down, 1, 0)


def factor_kernel(me, *refs):
    count = LEVELS + 1
    grams, (transfer, weight, work, ups, invs) = refs[:count], refs[count:]
    factor(lambda l, b: grams[l][b * LANES : (b + 1) * LANES, :], work, ups, invs)
    cols = pl.ds(pl.multiple_of(me[0] * LANES, LANES), LANES)
    for l in range(LEVELS):
        transfer[l] = dot(ups[l], invs[l + 1, cols, :], 1, 1)
    weight[...] = invs[LEVELS, cols, :]


def factors(me, grams):
    n = 2 * LANES
    count = len(grams)
    whole = pl.BlockSpec(memory_space=pltpu.VMEM)
    return call(
        factor_kernel,
        (
            jax.ShapeDtypeStruct((LEVELS, n, LANES), F32),
            jax.ShapeDtypeStruct((LANES, n), F32),
        ),
        grid_spec=pltpu.PrefetchScalarGridSpec(
            num_scalar_prefetch=1,
            grid=(1,),
            in_specs=[whole] * count,
            out_specs=[whole] * 2,
            scratch_shapes=[
                pltpu.VMEM((count, LANES, LANES), F32),
                pltpu.VMEM((count, n, n), F32),
                pltpu.VMEM((count, n, n), F32),
            ],
        ),
    )(me, *grams)


def basis_kernel(me, own, other, weight, out):
    n = LANES
    scale = math.sqrt(2**LEVELS * own.shape[0] * pl.num_programs(0))
    mine = pl.ds(pl.multiple_of(me[0] * n, n), n)
    rest = pl.ds(pl.multiple_of((1 - me[0]) * n, n), n)
    total = None
    for ref, cols in ((own, mine), (other, rest)):
        a0, a1 = halves(ref[...])
        b0, b1 = halves(weight[:, cols] * scale)
        part = dot16(a0, b0, 1, 1) + (dot16(a0, b1, 1, 1) + dot16(a1, b0, 1, 1))
        total = part if total is None else total + part
    out[...] = total


def basis_rows(me, own, other, weight):
    leaf, half = own.shape
    steps = 4
    rows = pl.BlockSpec((leaf // steps, half), lambda i, me: (i, 0))
    return call(
        basis_kernel,
        jax.ShapeDtypeStruct((leaf, half), F32),
        grid_spec=pltpu.PrefetchScalarGridSpec(
            num_scalar_prefetch=1,
            grid=(steps,),
            in_specs=[rows, rows, pl.BlockSpec((half, 2 * half), lambda i, me: (0, 0))],
            out_specs=rows,
        ),
    )(me, own, other, weight)


def beside(array, shift):
    count = lax.axis_size("leaf")
    pairs = [(i, i + shift) for i in range(count) if 0 <= i + shift < count]
    return lax.ppermute(array, "leaf", pairs)


def sibling(array, bit):
    return lax.ppermute(array, "leaf", [(i, i ^ 1 << bit) for i in range(lax.axis_size("leaf"))])


def other_core(array):
    return lax.ppermute(array, "probe", [(0, 1), (1, 0)])


def body(features, probes, lengthscale, near_blocks, leaf_order):
    blocks = near_blocks.shape[0]
    me = lax.axis_index("probe").astype(jnp.int32)[None]
    ids = near_blocks - (lax.axis_index("leaf") - 1) * blocks
    ordered = order_features(features, leaf_order)
    before = beside(ordered, 1)
    after = beside(ordered, -1)
    probes_before = beside(probes, 1)
    probes_after = beside(probes, -1)
    tiles = kernel_tiles(ids, ordered, before, after, lengthscale[:, None])
    own = sketch_rows(ids, tiles, probes_before, probes, probes_after)
    other = other_core(own)
    gram = gram_blocks(me, own, other)
    grams = [gram]
    for depth in range(LEVELS):
        gram = gram + sibling(gram, depth)
        grams.append(gram)
    transfer, weight = factors(me, grams)
    basis = basis_rows(me, own, other, weight)
    return transfer, basis


def solution(mesh):
    in_specs = (P(None, "leaf"), P("probe", "leaf"), P(), P("leaf", None), P("leaf", None))
    out_specs = (P(None, "leaf", "probe"), P("leaf", "probe"))
    return jax.shard_map(body, mesh=mesh, in_specs=in_specs, out_specs=out_specs, check_vma=False)
```

time: 691 us -> 145 us (0.21); the launches traced: 678 us -> 145 us
  other arithmetic: 286 us -> 0.79 us
  matrix products: 151 us -> 0 us
  local copies, waits for them, and re-layouts: 152 us -> 2.23 us
  Pallas kernels: 0 us -> 63.1 us
  between operations: 21.2 us -> 0.77 us
  waiting for transfers between devices: 32.9 us -> 46.4 us
    another operation x47 -> x0, other arithmetic: 260 us -> none  [the longest x35 177 us: body(): factors = [jnp.linalg.cholesky(item) for item in grams]]
    dot_general x13 -> x0, matrix products: 134 us -> none  [the longest x12 127 us: one_block(): lax.dot_general(kern.reshape(block_len, near_count * block_len), col_prob...]
    slice x60 -> x0, local copies, waits for them, and re-layouts: 100 us -> none  [the longest x12 61.8 us: one_block(): col_feat[feature][None]]
    pallas_call x0 -> x6, Pallas kernels: none -> 63.1 us  [the longest x1 27.4 us: factors(): call(factor_kernel, (jax.ShapeDtypeStruct((LEVELS, n, LANES), F32), jax.S...]
    ppermute x6 -> x9, waiting for transfers between devices: 16.2 us -> 46.4 us  [the longest x4 35.9 us: sibling(): lax.ppermute(array, 'leaf', [(i, i ^ 1 << bit) for i in range(lax.axis_si...]
    another operation x39 -> x0, local copies, waits for them, and re-layouts: 18.3 us -> none  [the longest x29 17.4 us: lower_solve(): return lax.linalg.triangular_solve(lower, right, left_side=True, lower=True)]
    all_gather x1 -> x0, waiting for transfers between devices: 16.7 us -> none  [body(): full_sketch = lax.all_gather(sketch, 'probe', axis=1, tiled=True)]
    another operation x25 -> x0, matrix products: 16.3 us -> none  [the longest x15 11.7 us: lower_solve(): return lax.linalg.triangular_solve(lower, right, left_side=True, lower=True)]
  transfers between devices with their start and end apart: 7 -> 9, of which waited for: 3 -> 6; matrix products, arithmetic and copies ran while one was open for 32% -> 1% of each run, Pallas kernels for 0% -> 12%
where the time goes in v1:
time: 145 us
  Pallas kernels  63.1 us (44%)
  waiting for transfers between devices  46.4 us (32%)
  starting transfers between devices  31.5 us (22%)
  local copies, waits for them, and re-layouts  2.23 us (2%)
    ppermute x4, waiting for transfers between devices, sibling(): lax.ppermute(array, 'leaf', [(i, i ^ 1 << bit) for i in range(lax.axis_si...  35.9 us
    pallas_call x1, Pallas kernels, factors(): call(factor_kernel, (jax.ShapeDtypeStruct((LEVELS, n, LANES), F32), jax.S...  27.4 us
    ppermute x4, starting transfers between devices, beside(): return lax.ppermute(array, 'leaf', pairs)  21.9 us
    pallas_call x1, Pallas kernels, kernel_tiles(): call(tile_kernel, jax.ShapeDtypeStruct((blocks, block, near * block), BF1...  15 us
    pallas_call x1, Pallas kernels, sketch_rows(): call(sketch_kernel, jax.ShapeDtypeStruct((leaf, half), F32), grid_spec=pl...  12.9 us
    ppermute x4, starting transfers between devices, sibling(): lax.ppermute(array, 'leaf', [(i, i ^ 1 << bit) for i in range(lax.axis_si...  7.68 us
    ppermute x4, waiting for transfers between devices, beside(): return lax.ppermute(array, 'leaf', pairs)  7.06 us
    ppermute x1, waiting for transfers between devices, other_core(): return lax.ppermute(array, 'probe', [(0, 1), (1, 0)])  3.37 us
  transfers between devices with their start and end apart: 9, of which 6 were waited for; matrix products, arithmetic and copies ran while one was open for 1% of the time, Pallas kernels for 12%

profile of v1, /device:TPU:6, one launch (start us, length us, event | category | flops | bytes accessed | tf_op | source)
XLA Modules:
  0.0 144.8 jit_solution(8452825319140986879)
XLA Ops:
  0.6 3.5 %collective-permute-start.2 = (bf16[128,3072]{1,0:T(8,128)(2,1)}, bf16[128,3072]{1,0:T(8,128)(2,1)S(1)}, u32[]{:S(2)}, u32[]{:S(2)}) collective-permute-start(bf16[128,3072]{1,0:T(8,128)(2,1)} %own.1), channel_id=1, source_target_pairs={{0,2},{2,4},{4,6},{6,8},{8,10},{10,12},{12,14},{14,16},{16,18},{18... | collective-permute-start | bytes 2359304 | tf_op jit(solution)/shard_map/ppermute | solution.py:367
  4.1 12.6 %collective-permute-start.3 = (bf16[128,3072]{1,0:T(8,128)(2,1)}, bf16[128,3072]{1,0:T(8,128)(2,1)S(1)}, u32[]{:S(2)}, u32[]{:S(2)}) collective-permute-start(bf16[128,3072]{1,0:T(8,128)(2,1)} %own.1), channel_id=1, source_target_pairs={{2,0},{4,2},{6,4},{8,6},{10,8},{12,10},{14,12},{16,14},{18,16},{20... | collective-permute-start | bytes 2359304 | tf_op jit(solution)/shard_map/ppermute | solution.py:367
  16.7 0.0 copy-start.1
  16.7 0.8 copy-done.1
  17.5 0.0 copy-start.2
  17.5 0.7 copy-done.2
  18.2 2.2 %shard_map.68.own = bf16[8,3072]{1,0:T(8,128)(2,1)S(1)} custom-call(bf16[8,3072]{1,0:T(8,128)(2,1)S(1)} %copy-done.1, s32[1,3072]{1,0:T(1,128)S(1)} %copy-done.2), custom_call_target="tpu_custom_call" | custom-call | tf_op jit(solution)/shard_map/pallas_call | solution.py:72
  20.4 3.9 %collective-permute-start.1 = (bf16[8,3072]{1,0:T(8,128)(2,1)S(1)}, bf16[8,3072]{1,0:T(8,128)(2,1)S(1)}, u32[]{:S(2)}, u32[]{:S(2)}) collective-permute-start(bf16[8,3072]{1,0:T(8,128)(2,1)S(1)} %shard_map.68.own), channel_id=1, source_target_pairs={{2,0},{4,2},{6,4},{8,6},{10,8},{12,10},{14,12},{16,14},{18,16},{20... | collective-permute-start | bytes 147464 | tf_op jit(solution)/shard_map/ppermute | solution.py:367
  24.3 1.9 %collective-permute-start = (bf16[8,3072]{1,0:T(8,128)(2,1)S(1)}, bf16[8,3072]{1,0:T(8,128)(2,1)S(1)}, u32[]{:S(2)}, u32[]{:S(2)}) collective-permute-start(bf16[8,3072]{1,0:T(8,128)(2,1)S(1)} %shard_map.68.own), channel_id=1, source_target_pairs={{0,2},{2,4},{4,6},{6,8},{8,10},{10,12},{12,14},{14,16},{16,18},{18... | collective-permute-start | bytes 147464 | tf_op jit(solution)/shard_map/ppermute | solution.py:367
  26.2 0.7 broadcast_subtract_fusion.ids
  26.9 0.7 copy.7.scale
  27.7 0.0 copy-start
  27.7 7.1 %collective-permute-done.1.right = bf16[8,3072]{1,0:T(8,128)(2,1)S(1)} collective-permute-done((bf16[8,3072]{1,0:T(8,128)(2,1)S(1)}, bf16[8,3072]{1,0:T(8,128)(2,1)S(1)}, u32[]{:S(2)}, u32[]{:S(2)}) %collective-permute-start.1) | collective-permute-done | bytes 49184 | tf_op jit(solution)/shard_map/ppermute | solution.py:367
  34.7 0.0 collective-permute-done.left
  34.7 15.0 %shard_map.69.tiles = bf16[12,256,2560]{2,1,0:T(8,128)(2,1)} custom-call(s32[12,10]{1,0:T(8,128)S(1)} %broadcast_subtract_fusion.ids, bf16[8,3072]{1,0:T(8,128)(2,1)S(1)} %shard_map.68.own, bf16[8,3072]{1,0:T(8,128)(2,1)S(1)} %collective-permute-done.left, bf16[8,3072]{1,0:T(8,128)(2,1)S(1)} %collective-permute-done.1.right, f32[8,1]{1,0:T(8,128)S(1)} %copy.7.scale), custom_call_target="tpu_custom_call" | custom-call | tf_op jit(solution)/shard_map/pallas_call | solution.py:118
  49.7 0.0 collective-permute-done.2.left
  49.7 0.0 collective-permute-done.3.right
  49.7 0.0 copy-done
  49.7 12.9 %shard_map.70.own = f32[3072,128]{1,0:T(8,128)S(1)} custom-call(s32[12,10]{1,0:T(8,128)S(1)} %broadcast_subtract_fusion.ids, bf16[12,256,2560]{2,1,0:T(8,128)(2,1)} %shard_map.69.tiles, bf16[128,3072]{1,0:T(8,128)(2,1)S(1)} %collective-permute-done.2.left, bf16[128,3072]{1,0:T(8,128)(2,1)S(1)} %copy-done, bf16[128,3072]{1,0:T(8,128)(2,1)S(1)} %collective-permute-done.3.right), custom_call_target="tpu_custom_call" | custom-call | tf_op jit(solution)/shard_map/pallas_call | solution.py:153
  62.6 1.9 %collective-permute-start.4 = (f32[3072,128]{1,0:T(8,128)S(1)}, f32[3072,128]{1,0:T(8,128)S(1)}, u32[]{:S(2)}, u32[]{:S(2)}) collective-permute-start(f32[3072,128]{1,0:T(8,128)S(1)} %shard_map.70.own), channel_id=1, source_target_pairs={{0,1},{1,0},{2,3},{3,2},{4,5},{5,4},{6,7},{7,6},{8,9},{9,8},{10,11... | collective-permute-start | bytes 4718600 | tf_op jit(solution)/shard_map/ppermute | solution.py:375
  64.5 3.4 %collective-permute-done.4.other = f32[3072,128]{1,0:T(8,128)S(1)} collective-permute-done((f32[3072,128]{1,0:T(8,128)S(1)}, f32[3072,128]{1,0:T(8,128)S(1)}, u32[]{:S(2)}, u32[]{:S(2)}) %collective-permute-start.4) | collective-permute-done | bytes 1572896 | tf_op jit(solution)/shard_map/ppermute | solution.py:375
  67.9 2.8 %shard_map.71.refs_0_ = f32[384,128]{1,0:T(8,128)S(1)} custom-call(s32[1]{0:T(128)} %bitcast.me, f32[3072,128]{1,0:T(8,128)S(1)} %shard_map.70.own, f32[3072,128]{1,0:T(8,128)S(1)} %collective-permute-done.4.other), custom_call_target="tpu_custom_call" | custom-call | tf_op jit(solution)/shard_map/pallas_call | solution.py:192
  70.7 1.9 %collective-permute-start.5 = (f32[384,128]{1,0:T(8,128)S(1)}, f32[384,128]{1,0:T(8,128)S(1)}, u32[]{:S(2)}, u32[]{:S(2)}) collective-permute-start(f32[384,128]{1,0:T(8,128)S(1)} %shard_map.71.refs_0_), channel_id=1, source_target_pairs={{0,2},{2,0},{4,6},{6,4},{8,10},{10,8},{12,14},{14,12},{16,18},{18,... | collective-permute-start | bytes 589832 | tf_op jit(solution)/shard_map/ppermute | solution.py:371
  72.6 6.9 %collective-permute-done.5 = f32[384,128]{1,0:T(8,128)S(1)} collective-permute-done((f32[384,128]{1,0:T(8,128)S(1)}, f32[384,128]{1,0:T(8,128)S(1)}, u32[]{:S(2)}, u32[]{:S(2)}) %collective-permute-start.5) | collective-permute-done | bytes 196640 | tf_op jit(solution)/shard_map/ppermute | solution.py:371
  79.5 1.9 %collective-permute-start.6 = (f32[384,128]{1,0:T(8,128)S(1)}, f32[384,128]{1,0:T(8,128)S(1)}, u32[]{:S(2)}, u32[]{:S(2)}) collective-permute-start(f32[384,128]{1,0:T(8,128)S(1)} %add.13.refs_1_), channel_id=1, source_target_pairs={{0,4},{2,6},{4,0},{6,2},{8,12},{10,14},{12,8},{14,10},{16,20},{18,... | collective-permute-start | bytes 589832 | tf_op jit(solution)/shard_map/ppermute | solution.py:371
  81.5 11.2 %collective-permute-done.6 = f32[384,128]{1,0:T(8,128)S(1)} collective-permute-done((f32[384,128]{1,0:T(8,128)S(1)}, f32[384,128]{1,0:T(8,128)S(1)}, u32[]{:S(2)}, u32[]{:S(2)}) %collective-permute-start.6) | collective-permute-done | bytes 196640 | tf_op jit(solution)/shard_map/ppermute | solution.py:371
  92.7 1.9 %collective-permute-start.7 = (f32[384,128]{1,0:T(8,128)S(1)}, f32[384,128]{1,0:T(8,128)S(1)}, u32[]{:S(2)}, u32[]{:S(2)}) collective-permute-start(f32[384,128]{1,0:T(8,128)S(1)} %add.14.refs_2_), channel_id=1, source_target_pairs={{0,8},{2,10},{4,12},{6,14},{8,0},{10,2},{12,4},{14,6},{16,24},{18,... | collective-permute-start | bytes 589832 | tf_op jit(solution)/shard_map/ppermute | solution.py:371
  94.6 12.1 %collective-permute-done.7 = f32[384,128]{1,0:T(8,128)S(1)} collective-permute-done((f32[384,128]{1,0:T(8,128)S(1)}, f32[384,128]{1,0:T(8,128)S(1)}, u32[]{:S(2)}, u32[]{:S(2)}) %collective-permute-start.7) | collective-permute-done | bytes 196640 | tf_op jit(solution)/shard_map/ppermute | solution.py:371
  106.7 1.9 %collective-permute-start.8 = (f32[384,128]{1,0:T(8,128)S(1)}, f32[384,128]{1,0:T(8,128)S(1)}, u32[]{:S(2)}, u32[]{:S(2)}) collective-permute-start(f32[384,128]{1,0:T(8,128)S(1)} %add.15.refs_3_), channel_id=1, source_target_pairs={{0,16},{2,18},{4,20},{6,22},{8,24},{10,26},{12,28},{14,30},{16,0},... | collective-permute-start | bytes 589832 | tf_op jit(solution)/shard_map/ppermute | solution.py:371
  108.7 5.7 %collective-permute-done.8 = f32[384,128]{1,0:T(8,128)S(1)} collective-permute-done((f32[384,128]{1,0:T(8,128)S(1)}, f32[384,128]{1,0:T(8,128)S(1)}, u32[]{:S(2)}, u32[]{:S(2)}) %collective-permute-start.8) | collective-permute-done | bytes 196640 | tf_op jit(solution)/shard_map/ppermute | solution.py:371
  114.4 27.4 %shard_map.72 = (f32[4,256,128]{2,1,0:T(8,128)}, f32[128,256]{1,0:T(8,128)S(1)}) custom-call(s32[1]{0:T(128)} %bitcast.me, f32[384,128]{1,0:T(8,128)S(1)} %shard_map.71.refs_0_, f32[384,128]{1,0:T(8,128)S(1)} %add.13.refs_1_, f32[384,128]{1,0:T(8,128)S(1)} %add.14.refs_2_, f32[384,128]{1,0:T(8,128)S(1)} %add.15.refs_3_, f32[384,128]{1,0:T(8,128)S(1)} %add.16.refs_4_), custom_call_target="tpu_custom_call" | custom-call | tf_op jit(solution)/shard_map/pallas_call | solution.py:314
  141.8 3.0 %shard_map.73 = f32[3072,128]{1,0:T(8,128)} custom-call(s32[1]{0:T(128)} %bitcast.me, f32[3072,128]{1,0:T(8,128)S(1)} %shard_map.70.own, f32[3072,128]{1,0:T(8,128)S(1)} %collective-permute-done.4.other, f32[128,256]{1,0:T(8,128)S(1)} %get-tuple-element.5.weight), custom_call_target="tpu_custom_call" | custom-call | tf_op jit(solution)/shard_map/pallas_call | solution.py:352
  (4 shorter events, 0.1 us)
Async XLA Ops:
  0.6 49.1 %collective-permute-start.2 = (bf16[128,3072]{1,0:T(8,128)(2,1)}, bf16[128,3072]{1,0:T(8,128)(2,1)S(1)}, u32[]{:S(2)}, u32[]{:S(2)}) collective-permute-start(bf16[128,3072]{1,0:T(8,128)(2,1)} %own.1), channel_id=1, source_target_pairs={{0,2},{2,4},{4,6},{6,8},{8,10},{10,12},{12,14},{14,16},{16,18},{18... | collective-permute-start | bytes 2359304 | tf_op jit(solution)/shard_map/ppermute | solution.py:367
  4.1 45.6 %collective-permute-start.3 = (bf16[128,3072]{1,0:T(8,128)(2,1)}, bf16[128,3072]{1,0:T(8,128)(2,1)S(1)}, u32[]{:S(2)}, u32[]{:S(2)}) collective-permute-start(bf16[128,3072]{1,0:T(8,128)(2,1)} %own.1), channel_id=1, source_target_pairs={{2,0},{4,2},{6,4},{8,6},{10,8},{12,10},{14,12},{16,14},{18,16},{20... | collective-permute-start | bytes 2359304 | tf_op jit(solution)/shard_map/ppermute | solution.py:367
  16.7 0.8 copy-start.1
  17.5 0.7 copy-start.2
  20.4 14.4 %collective-permute-start.1 = (bf16[8,3072]{1,0:T(8,128)(2,1)S(1)}, bf16[8,3072]{1,0:T(8,128)(2,1)S(1)}, u32[]{:S(2)}, u32[]{:S(2)}) collective-permute-start(bf16[8,3072]{1,0:T(8,128)(2,1)S(1)} %shard_map.68.own), channel_id=1, source_target_pairs={{2,0},{4,2},{6,4},{8,6},{10,8},{12,10},{14,12},{16,14},{18,16},{20... | collective-permute-start | bytes 147464 | tf_op jit(solution)/shard_map/ppermute | solution.py:367
  24.3 10.4 %collective-permute-start = (bf16[8,3072]{1,0:T(8,128)(2,1)S(1)}, bf16[8,3072]{1,0:T(8,128)(2,1)S(1)}, u32[]{:S(2)}, u32[]{:S(2)}) collective-permute-start(bf16[8,3072]{1,0:T(8,128)(2,1)S(1)} %shard_map.68.own), channel_id=1, source_target_pairs={{0,2},{2,4},{4,6},{6,8},{8,10},{10,12},{12,14},{14,16},{16,18},{18... | collective-permute-start | bytes 147464 | tf_op jit(solution)/shard_map/ppermute | solution.py:367
  27.7 22.1 %copy-start = (bf16[128,3072]{1,0:T(8,128)(2,1)S(1)}, bf16[128,3072]{1,0:T(8,128)(2,1)}, u32[]{:S(2)}) copy-start(bf16[128,3072]{1,0:T(8,128)(2,1)} %own.1) | copy-start | bytes 2359300
  62.6 5.3 %collective-permute-start.4 = (f32[3072,128]{1,0:T(8,128)S(1)}, f32[3072,128]{1,0:T(8,128)S(1)}, u32[]{:S(2)}, u32[]{:S(2)}) collective-permute-start(f32[3072,128]{1,0:T(8,128)S(1)} %shard_map.70.own), channel_id=1, source_target_pairs={{0,1},{1,0},{2,3},{3,2},{4,5},{5,4},{6,7},{7,6},{8,9},{9,8},{10,11... | collective-permute-start | bytes 4718600 | tf_op jit(solution)/shard_map/ppermute | solution.py:375
  70.7 8.8 %collective-permute-start.5 = (f32[384,128]{1,0:T(8,128)S(1)}, f32[384,128]{1,0:T(8,128)S(1)}, u32[]{:S(2)}, u32[]{:S(2)}) collective-permute-start(f32[384,128]{1,0:T(8,128)S(1)} %shard_map.71.refs_0_), channel_id=1, source_target_pairs={{0,2},{2,0},{4,6},{6,4},{8,10},{10,8},{12,14},{14,12},{16,18},{18,... | collective-permute-start | bytes 589832 | tf_op jit(solution)/shard_map/ppermute | solution.py:371
  79.5 13.1 %collective-permute-start.6 = (f32[384,128]{1,0:T(8,128)S(1)}, f32[384,128]{1,0:T(8,128)S(1)}, u32[]{:S(2)}, u32[]{:S(2)}) collective-permute-start(f32[384,128]{1,0:T(8,128)S(1)} %add.13.refs_1_), channel_id=1, source_target_pairs={{0,4},{2,6},{4,0},{6,2},{8,12},{10,14},{12,8},{14,10},{16,20},{18,... | collective-permute-start | bytes 589832 | tf_op jit(solution)/shard_map/ppermute | solution.py:371
  92.7 14.0 %collective-permute-start.7 = (f32[384,128]{1,0:T(8,128)S(1)}, f32[384,128]{1,0:T(8,128)S(1)}, u32[]{:S(2)}, u32[]{:S(2)}) collective-permute-start(f32[384,128]{1,0:T(8,128)S(1)} %add.14.refs_2_), channel_id=1, source_target_pairs={{0,8},{2,10},{4,12},{6,14},{8,0},{10,2},{12,4},{14,6},{16,24},{18,... | collective-permute-start | bytes 589832 | tf_op jit(solution)/shard_map/ppermute | solution.py:371
  106.7 7.7 %collective-permute-start.8 = (f32[384,128]{1,0:T(8,128)S(1)}, f32[384,128]{1,0:T(8,128)S(1)}, u32[]{:S(2)}, u32[]{:S(2)}) collective-permute-start(f32[384,128]{1,0:T(8,128)S(1)} %add.15.refs_3_), channel_id=1, source_target_pairs={{0,16},{2,18},{4,20},{6,22},{8,24},{10,26},{12,28},{14,30},{16,0},... | collective-permute-start | bytes 589832 | tf_op jit(solution)/shard_map/ppermute | solution.py:371

commit v2 on v1

v2 whole, which is shorter than its diff:
```python
import math

import jax
import jax.numpy as jnp
from jax import lax
from jax.experimental import pallas as pl
from jax.experimental.pallas import tpu as pltpu
from jax.sharding import PartitionSpec as P

LEVELS = 4
LANES = 128
ROWS = 8
LOG2_E = 1.4426950408889634
LN_2 = 0.6931471805599453
NUGGET = 2.0
TINY = 1e-20
HI = lax.Precision.HIGHEST
F32 = jnp.float32
BF16 = jnp.bfloat16
VMEM_BYTES = 14 << 20


def call(kernel, out_shape, **kwargs):
    return pl.pallas_call(
        kernel,
        out_shape=out_shape,
        compiler_params=pltpu.CompilerParams(vmem_limit_bytes=VMEM_BYTES),
        **kwargs,
    )


def dot(a, b, ca, cb, precision=HI):
    return lax.dot_general(
        a, b, (((ca,), (cb,)), ((), ())), precision=precision, preferred_element_type=F32
    )


def dot16(a, b, ca, cb):
    return lax.dot_general(a, b, (((ca,), (cb,)), ((), ())), preferred_element_type=F32)


def halves(x):
    hi = x.astype(BF16)
    return hi, (x - hi.astype(F32)).astype(BF16)


def thirds(x):
    hi = x.astype(BF16).astype(F32)
    rest = x - hi
    mid = rest.astype(BF16).astype(F32)
    return hi, mid, rest - mid


def order_kernel(feat, order, out):
    chunks = feat.shape[1] // LANES
    pieces = [feat[:, c * LANES : (c + 1) * LANES].astype(F32) for c in range(chunks)]

    def one(q, carry):
        at = pl.multiple_of(q * LANES, LANES)
        index = jnp.broadcast_to(order[:, pl.ds(at, LANES)], (ROWS, LANES))
        low, high = index & (LANES - 1), index >> 7
        total = jnp.zeros((ROWS, LANES), F32)
        for c in range(chunks):
            total = jnp.where(high == c, jnp.take_along_axis(pieces[c], low, axis=1), total)
        out[:, pl.ds(at, LANES)] = total.astype(BF16)
        return carry

    lax.fori_loop(0, chunks, one, 0)


def order_features(features, leaf_order):
    return call(order_kernel, jax.ShapeDtypeStruct(features.shape, BF16))(features, leaf_order)


SHIFT = 6
SLOTS = 128
WIDE = 4


def column_pieces(x, weight):
    norm = jnp.sum(x * x * weight, 0, keepdims=True)
    ones = jnp.ones_like(norm)
    zeros = jnp.zeros((2, x.shape[1]), F32)
    return jnp.concatenate([x, x, x, *thirds(norm), ones, ones, ones, zeros], 0).astype(BF16)


def row_pieces(x, weight):
    norm = jnp.sum(x * x * weight, 0, keepdims=True)
    ones = jnp.ones_like(norm)
    zeros = jnp.zeros((2, x.shape[1]), F32)
    return jnp.concatenate(
        [*thirds(-2.0 * weight * x), ones, ones, ones, *thirds(norm), zeros], 0
    ).T.astype(BF16)


def weights(scale):
    return (3.0 * LOG2_E * LOG2_E) / (scale[...] * scale[...])


def load_columns(cols, panel, feats, probes, weight, blocks):
    leaf = feats[0].shape[1]
    block = leaf // blocks
    for n, (feat, probe) in enumerate(zip(feats, probes)):
        pieces = column_pieces(feat[...].astype(F32), weight)
        for b in range(blocks):
            span = slice(b * block, (b + 1) * block)
            cols[n * blocks + b] = pieces[:, span]
            panel[n * blocks + b] = probe[:, span]
    last = len(feats) * blocks
    cols[last] = jnp.zeros(cols.shape[1:], BF16)
    panel[last] = jnp.zeros(panel.shape[1:], BF16)


def run_tasks(tasks, count, slot_of, rows_t, cols, panel, out):
    block = cols.shape[2]

    def some(t, carry):
        parts = []
        for u in range(WIDE):
            code = tasks[t * WIDE + u]
            at = pl.ds(pl.multiple_of((code >> SHIFT) * block, block), block)
            slot = slot_of(code & ((1 << SHIFT) - 1))
            dist = jnp.maximum(dot16(rows_t[at, :], cols[slot], 1, 0), TINY)
            root = dist * lax.rsqrt(dist)
            kern = (1.0 + LN_2 * root) * jnp.exp2(-root)
            parts.append((at, dot16(kern.astype(BF16), panel[slot], 1, 1)))
        for at, part in parts:
            out[at, :] += part
        return carry

    lax.fori_loop(0, (count + (WIDE - 1)) // WIDE, some, 0)


def near_kernel(ids, feat, scale, probes, out, rows_t, far, tasks, cols, panel):
    blocks, near = ids.shape
    block = feat.shape[1] // blocks

    def scan(a, counts):
        mine, rest = counts
        for j in range(near):
            listed = ids[a, j]
            code = (a << SHIFT) + listed
            inside = jnp.where((listed >= blocks) & (listed < 2 * blocks), 1, 0)
            tasks[mine] = code
            far[rest] = code
            mine = mine + inside
            rest = rest + (1 - inside)
        return mine, rest

    mine, rest = lax.fori_loop(0, blocks, scan, (jnp.int32(0), jnp.int32(0)))
    for u in range(WIDE):
        tasks[mine + u] = 2 * blocks
        far[rest + u] = 3 * blocks
    far[SLOTS - 1] = rest

    weight = weights(scale)
    rows_t[...] = row_pieces(feat[...].astype(F32), weight)
    load_columns(cols, panel, [feat], [probes], weight, blocks)
    here = lax.broadcasted_iota(jnp.int32, (block, block), 0)
    there = lax.broadcasted_iota(jnp.int32, (block, block), 1)
    nugget = jnp.where(here == there, NUGGET, 0.0).astype(BF16)
    for b in range(blocks):
        out[b * block : (b + 1) * block, :] = dot16(nugget, panel[b], 1, 1)
    run_tasks(tasks, mine, lambda listed: listed - blocks, rows_t, cols, panel, out)


def near_part(ids, feat, scale, probes):
    half, leaf = probes.shape
    blocks = ids.shape[0]
    block = leaf // blocks
    whole = pl.BlockSpec(memory_space=pltpu.VMEM)
    return call(
        near_kernel,
        (
            pltpu.VMEM((leaf, half), F32),
            pltpu.VMEM((leaf, 32), BF16),
            jax.ShapeDtypeStruct((SLOTS,), jnp.int32),
        ),
        grid_spec=pltpu.PrefetchScalarGridSpec(
            num_scalar_prefetch=1,
            grid=(1,),
            in_specs=[whole] * 3,
            out_specs=[whole, whole, pl.BlockSpec(memory_space=pltpu.SMEM)],
            scratch_shapes=[
                pltpu.SMEM((SLOTS,), jnp.int32),
                pltpu.VMEM((blocks + 1, 32, block), BF16),
                pltpu.VMEM((blocks + 1, half, block), BF16),
            ],
        ),
    )(ids, feat, scale, probes)


def far_kernel(far, part, rows_t, left, right, scale, before, after, out, cols, panel):
    blocks = (cols.shape[0] - 1) // 2
    load_columns(cols, panel, [left, right], [before, after], weights(scale), blocks)
    out[...] = part[...]
    run_tasks(
        far,
        far[SLOTS - 1],
        lambda listed: jnp.where(listed < blocks, listed, listed - blocks),
        rows_t,
        cols,
        panel,
        out,
    )


def far_part(far, part, rows_t, left, right, scale, before, after, blocks):
    half, leaf = before.shape
    block = leaf // blocks
    whole = pl.BlockSpec(memory_space=pltpu.VMEM)
    return call(
        far_kernel,
        pltpu.VMEM((leaf, half), F32),
        grid_spec=pltpu.PrefetchScalarGridSpec(
            num_scalar_prefetch=1,
            grid=(1,),
            in_specs=[whole] * 7,
            out_specs=whole,
            scratch_shapes=[
                pltpu.VMEM((2 * blocks + 1, 32, block), BF16),
                pltpu.VMEM((2 * blocks + 1, half, block), BF16),
            ],
        ),
    )(far, part, rows_t, left, right, scale, before, after)


def gram_kernel(me, own, other, out):
    n = own.shape[1]

    @pl.when(pl.program_id(0) == 0)
    def _():
        out[...] = jnp.zeros_like(out)

    def product(a, b):
        return dot16(a[0], b[0], 0, 0) + (dot16(a[0], b[1], 0, 0) + dot16(a[1], b[0], 0, 0))

    mine = halves(own[...])
    out[0:n] += product(mine, mine)

    @pl.when(me[0] == 0)
    def _():
        out[n:] += product(halves(other[:, : n // 2]), halves(own[...]))

    @pl.when(me[0] == 1)
    def _():
        out[n:] += product(halves(own[:, n // 2 :]), halves(other[...]))


def gram_blocks(me, own, other):
    leaf, half = own.shape
    steps = 4
    height = half + half // 2
    rows = pl.BlockSpec((leaf // steps, half), lambda i, me: (i, 0))
    return call(
        gram_kernel,
        jax.ShapeDtypeStruct((height, half), F32),
        grid_spec=pltpu.PrefetchScalarGridSpec(
            num_scalar_prefetch=1,
            grid=(steps,),
            in_specs=[rows, rows],
            out_specs=pl.BlockSpec((height, half), lambda i, me: (0, 0)),
        ),
    )(me, own, other)


TILE = (ROWS, LANES)


def row_of(x, k):
    return jnp.broadcast_to(x[k : k + 1, :], TILE)


def columns(panel, at):
    return [
        jnp.take_along_axis(panel, jnp.full(TILE, at + m, jnp.int32), axis=1)
        for m in range(ROWS)
    ]


def outer_sum(a, b):
    a0, a1, a2 = thirds(a)
    b0, b1, b2 = thirds(b)
    left = jnp.concatenate([a0, a0, a1, a0, a1, a2], 0).astype(BF16)
    right = jnp.concatenate([b0, b1, b0, b2, b1, b0], 0).astype(BF16)
    return dot16(left, right, 0, 0)


def eliminate(panels, nexts, at):
    count = range(len(panels))
    lane = lax.broadcasted_iota(jnp.int32, TILE, 1)
    sub = lax.broadcasted_iota(jnp.int32, TILE, 0)
    here = (lane >= at) & (lane < at + ROWS)
    unit = jnp.where(lane - at == sub, 1.0, 0.0)
    cols = [columns(panels[l], at) for l in count]
    rows = [jnp.where(here, unit, panels[l]) for l in count]
    lows = [jnp.zeros(TILE, F32) for l in count]
    below = [columns(panel, at) for panel in nexts]
    nexts = [jnp.where(here, 0.0, panel) for panel in nexts]
    for k in range(ROWS):
        inv = [lax.rsqrt(row_of(cols[l][k], k)) for l in count]
        low = [jnp.where(sub >= k, cols[l][k] * inv[l], 0.0) for l in count]
        for l in count:
            lead = row_of(rows[l], k) * inv[l]
            rows[l] = jnp.where(sub == k, lead, rows[l] - low[l] * lead)
            lows[l] = jnp.where(lane == at + k, low[l], lows[l])
            if nexts:
                below[l][k] = below[l][k] * inv[l]
                nexts[l] = nexts[l] - below[l][k] * lead
        for m in range(k + 1, ROWS):
            for l in count:
                one = row_of(low[l], m)
                cols[l][m] = cols[l][m] - low[l] * one
                if nexts:
                    below[l][m] = below[l][m] - below[l][k] * one
    return rows, lows, nexts


def factor_block(work, ups, invs, base):
    count = range(work.shape[0])
    lane = lax.broadcasted_iota(jnp.int32, TILE, 1)
    lane_all = lax.broadcasted_iota(jnp.int32, (LANES, LANES), 1)
    span = slice(base, base + LANES)
    pair = 2 * ROWS

    def step(j, carry):
        at = pl.multiple_of(j * pair, pair)
        mid, end = at + ROWS, at + pair
        both = [work[l, pl.ds(at, pair), :] for l in count]
        first, low_first, second = eliminate(
            [b[:ROWS] for b in both], [b[ROWS:] for b in both], at
        )
        second, low_second, _ = eliminate(second, [], mid)
        lefts, rights = [], []
        for l in count:
            lefts.append(
                jnp.concatenate([jnp.where(lane >= end, x[l], 0.0) for x in (first, second)], 0)
            )
            rights.append(
                jnp.concatenate(
                    [jnp.where((lane >= mid) & (lane < end), 0.0, first[l]), second[l]], 0
                )
            )
        sums = [outer_sum(lefts[l], rights[l]) for l in count]
        gone = (lane_all >= at) & (lane_all < end)
        rests = [jnp.where(gone, 0.0, work[l]) - sums[l] for l in count]
        for l in count:
            for x, low, p in ((first, low_first, at), (second, low_second, mid)):
                to = pl.ds(pl.multiple_of(base + p, ROWS), ROWS)
                ups[l, to, span] = jnp.where(lane >= p + ROWS, x[l], low[l])
                invs[l, to, span] = jnp.where(lane < p + ROWS, x[l], 0.0)
            work[l] = rests[l]
        return carry

    lax.fori_loop(0, LANES // pair, step, 0)


def straighten(ups, l, base):
    n = LANES
    block = ups[l, base : base + n, base : base + n]
    row = lax.broadcasted_iota(jnp.int32, (n, n), 0)
    col = lax.broadcasted_iota(jnp.int32, (n, n), 1)
    ups[l, base : base + n, base : base + n] = jnp.where(row >> 3 == col >> 3, block.T, block)


def factor(grams, work, ups, invs):
    n = LANES
    blank = jnp.zeros((n, n), F32)
    count = range(work.shape[0])
    for l in count:
        work[l] = grams(l, 0)
    factor_block(work, ups, invs, 0)
    sides = [dot(invs[l, 0:n, 0:n], grams(l, 1), 1, 1) for l in count]
    for l in count:
        ups[l, 0:n, n : 2 * n] = sides[l]
        ups[l, n : 2 * n, 0:n] = blank
        invs[l, 0:n, n : 2 * n] = blank
    squares = [dot(sides[l], sides[l], 0, 0) for l in count]
    for l in count:
        work[l] = grams(l, 2) - squares[l]
    factor_block(work, ups, invs, n)
    downs = [dot(ups[l, 0:n, n : 2 * n], invs[l, 0:n, 0:n], 0, 0) for l in count]
    downs = [dot(invs[l, n : 2 * n, n : 2 * n], downs[l], 1, 0) for l in count]
    for l in count:
        invs[l, n : 2 * n, 0:n] = -downs[l]
        straighten(ups, l, 0)
        straighten(ups, l, n)


def factor_kernel(me, mine, theirs, transfer, weight, pieces, work, ups, invs):
    n = LANES
    height = n + n // 2
    pieces[me[0]] = mine[...]
    pieces[1 - me[0]] = theirs[...]

    def gram(l, b):
        at = l * height
        if b == 1:
            return jnp.concatenate([pieces[p, at + n : at + height, :] for p in range(2)], 0)
        return pieces[b // 2, at : at + n, :]

    factor(gram, work, ups, invs)
    cols = pl.ds(pl.multiple_of(me[0] * n, n), n)
    for l in range(LEVELS):
        transfer[l] = dot(ups[l], invs[l + 1, cols, :], 1, 1)
    weight[...] = invs[LEVELS, cols, :]


def factors(me, mine, theirs):
    n = 2 * LANES
    count = LEVELS + 1
    whole = pl.BlockSpec(memory_space=pltpu.VMEM)
    return call(
        factor_kernel,
        (
            jax.ShapeDtypeStruct((LEVELS, n, LANES), F32),
            jax.ShapeDtypeStruct((LANES, n), F32),
        ),
        grid_spec=pltpu.PrefetchScalarGridSpec(
            num_scalar_prefetch=1,
            grid=(1,),
            in_specs=[whole] * 2,
            out_specs=[whole] * 2,
            scratch_shapes=[
                pltpu.VMEM((2, *mine.shape), F32),
                pltpu.VMEM((count, LANES, LANES), F32),
                pltpu.VMEM((count, n, n), F32),
                pltpu.VMEM((count, n, n), F32),
            ],
        ),
    )(me, mine, theirs)


def basis_kernel(me, own, other, weight, out):
    n = LANES
    scale = math.sqrt(2**LEVELS * own.shape[0] * pl.num_programs(0))
    mine = pl.ds(pl.multiple_of(me[0] * n, n), n)
    rest = pl.ds(pl.multiple_of((1 - me[0]) * n, n), n)
    total = None
    for ref, cols in ((own, mine), (other, rest)):
        a0, a1 = halves(ref[...])
        b0, b1 = halves(weight[:, cols] * scale)
        part = dot16(a0, b0, 1, 1) + (dot16(a0, b1, 1, 1) + dot16(a1, b0, 1, 1))
        total = part if total is None else total + part
    out[...] = total


def basis_rows(me, own, other, weight):
    leaf, half = own.shape
    steps = 4
    rows = pl.BlockSpec((leaf // steps, half), lambda i, me: (i, 0))
    return call(
        basis_kernel,
        jax.ShapeDtypeStruct((leaf, half), F32),
        grid_spec=pltpu.PrefetchScalarGridSpec(
            num_scalar_prefetch=1,
            grid=(steps,),
            in_specs=[rows, rows, pl.BlockSpec((half, 2 * half), lambda i, me: (0, 0))],
            out_specs=rows,
        ),
    )(me, own, other, weight)


def beside(array, shift):
    count = lax.axis_size("leaf")
    pairs = [(i, i + shift) for i in range(count) if 0 <= i + shift < count]
    return lax.ppermute(array, "leaf", pairs)


def sibling(array, bit):
    return lax.ppermute(array, "leaf", [(i, i ^ 1 << bit) for i in range(lax.axis_size("leaf"))])


def other_core(array):
    return lax.ppermute(array, "probe", [(0, 1), (1, 0)])


def body(features, probes, lengthscale, near_blocks, leaf_order):
    blocks = near_blocks.shape[0]
    me = lax.axis_index("probe").astype(jnp.int32)[None]
    ids = near_blocks - (lax.axis_index("leaf") - 1) * blocks
    scale = lengthscale[:, None]
    probes_before = beside(probes, 1)
    probes_after = beside(probes, -1)
    ordered = order_features(features, leaf_order)
    before = beside(ordered, 1)
    after = beside(ordered, -1)
    part, rows_t, far = near_part(ids, ordered, scale, probes)
    own = far_part(far, part, rows_t, before, after, scale, probes_before, probes_after, blocks)
    other = other_core(own)
    gram = gram_blocks(me, own, other)
    grams = [gram]
    for depth in range(LEVELS):
        gram = gram + sibling(gram, depth)
        grams.append(gram)
    mine = jnp.concatenate(grams, 0)
    transfer, weight = factors(me, mine, other_core(mine))
    basis = basis_rows(me, own, other, weight)
    return transfer, basis


def solution(mesh):
    in_specs = (P(None, "leaf"), P("probe", "leaf"), P(), P("leaf", None), P("leaf", None))
    out_specs = (P(None, "leaf", "probe"), P("leaf", "probe"))
    return jax.shard_map(body, mesh=mesh, in_specs=in_specs, out_specs=out_specs, check_vma=False)
```

time: 145 us -> 121 us (0.83)
  Pallas kernels: 63.1 us -> 46.1 us
  waiting for transfers between devices: 46.4 us -> 31.2 us
  starting transfers between devices: 31.5 us -> 37.6 us
    pallas_call x1, Pallas kernels: 27.4 us -> 14.8 us  [factors(): call(factor_kernel, (jax.ShapeDtypeStruct((LEVELS, n, LANES), F32), jax.S...]
    ppermute x4, waiting for transfers between devices: 35.9 us -> 26 us  [sibling(): lax.ppermute(array, 'leaf', [(i, i ^ 1 << bit) for i in range(lax.axis_si...]
    ppermute x4, waiting for transfers between devices: 7.06 us -> 0.01 us  [beside(): return lax.ppermute(array, 'leaf', pairs)]
    pallas_call x3, Pallas kernels: 30.6 us -> 26.2 us  [the longest x1 12.5 us: far_part(): call(far_kernel, pltpu.VMEM((leaf, half), F32), grid_spec=pltpu.PrefetchS...]
    ppermute x4, starting transfers between devices: 21.9 us -> 26.1 us  [beside(): return lax.ppermute(array, 'leaf', pairs)]
    ppermute x1 -> x2, starting transfers between devices: 1.92 us -> 3.84 us  [other_core(): return lax.ppermute(array, 'probe', [(0, 1), (1, 0)])]
    ppermute x1 -> x2, waiting for transfers between devices: 3.37 us -> 5.2 us  [other_core(): return lax.ppermute(array, 'probe', [(0, 1), (1, 0)])]
  transfers between devices with their start and end apart: 9 -> 10, of which waited for: 6 -> 6; matrix products, arithmetic and copies ran while one was open for 1% -> 1% of each run, Pallas kernels for 12% -> 11%
where the time goes in v2:
time: 121 us; the launch traced here: 120 us
  Pallas kernels  46.1 us (38%)
  starting transfers between devices  37.6 us (31%)
  waiting for transfers between devices  31.2 us (26%)
  local copies, waits for them, and re-layouts  3.37 us (3%)
    ppermute x4, starting transfers between devices, beside(): return lax.ppermute(array, 'leaf', pairs)  26.1 us
    ppermute x4, waiting for transfers between devices, sibling(): lax.ppermute(array, 'leaf', [(i, i ^ 1 << bit) for i in range(lax.axis_si...  26 us
    pallas_call x1, Pallas kernels, factors(): call(factor_kernel, (jax.ShapeDtypeStruct((LEVELS, n, LANES), F32), jax.S...  14.8 us
    pallas_call x1, Pallas kernels, far_part(): call(far_kernel, pltpu.VMEM((leaf, half), F32), grid_spec=pltpu.PrefetchS...  12.5 us
    pallas_call x1, Pallas kernels, near_part(): call(near_kernel, (pltpu.VMEM((leaf, half), F32), pltpu.VMEM((leaf, 32),...  10.8 us
    ppermute x4, starting transfers between devices, sibling(): lax.ppermute(array, 'leaf', [(i, i ^ 1 << bit) for i in range(lax.axis_si...  7.68 us
    ppermute x2, waiting for transfers between devices, other_core(): return lax.ppermute(array, 'probe', [(0, 1), (1, 0)])  5.2 us
    ppermute x2, starting transfers between devices, other_core(): return lax.ppermute(array, 'probe', [(0, 1), (1, 0)])  3.84 us
  transfers between devices with their start and end apart: 10, of which 6 were waited for; matrix products, arithmetic and copies ran while one was open for 1% of the time, Pallas kernels for 11%

profile of v2, /device:TPU:6, one launch (start us, length us, event | category | flops | bytes accessed | tf_op | source)
XLA Modules:
  0.0 119.8 jit_solution(11593037962525755055)
XLA Ops:
  0.6 14.1 %collective-permute-start.3 = (bf16[128,3072]{1,0:T(8,128)(2,1)}, bf16[128,3072]{1,0:T(8,128)(2,1)S(1)}, u32[]{:S(2)}, u32[]{:S(2)}) collective-permute-start(bf16[128,3072]{1,0:T(8,128)(2,1)} %probes.1), channel_id=1, source_target_pairs={{2,0},{4,2},{6,4},{8,6},{10,8},{12,10},{14,12},{16,14},{18,16},{20... | collective-permute-start | bytes 2359304 | tf_op jit(solution)/shard_map/ppermute | solution.py:467
  14.8 1.9 %collective-permute-start.2 = (bf16[128,3072]{1,0:T(8,128)(2,1)}, bf16[128,3072]{1,0:T(8,128)(2,1)S(1)}, u32[]{:S(2)}, u32[]{:S(2)}) collective-permute-start(bf16[128,3072]{1,0:T(8,128)(2,1)} %probes.1), channel_id=1, source_target_pairs={{0,2},{2,4},{4,6},{6,8},{8,10},{10,12},{12,14},{14,16},{16,18},{18... | collective-permute-start | bytes 2359304 | tf_op jit(solution)/shard_map/ppermute | solution.py:467
  16.7 0.0 copy-start.1
  16.7 0.8 copy-done.1
  17.5 0.7 copy-done.2
  18.2 2.2 %shard_map.68.feat = bf16[8,3072]{1,0:T(8,128)(2,1)S(1)} custom-call(bf16[8,3072]{1,0:T(8,128)(2,1)S(1)} %copy-done.1, s32[1,3072]{1,0:T(1,128)S(1)} %copy-done.2), custom_call_target="tpu_custom_call" | custom-call | tf_op jit(solution)/shard_map/pallas_call | solution.py:72
  20.4 8.1 %collective-permute-start.1 = (bf16[8,3072]{1,0:T(8,128)(2,1)S(1)}, bf16[8,3072]{1,0:T(8,128)(2,1)S(1)}, u32[]{:S(2)}, u32[]{:S(2)}) collective-permute-start(bf16[8,3072]{1,0:T(8,128)(2,1)S(1)} %shard_map.68.feat), channel_id=1, source_target_pairs={{2,0},{4,2},{6,4},{8,6},{10,8},{12,10},{14,12},{16,14},{18,16},{20... | collective-permute-start | bytes 147464 | tf_op jit(solution)/shard_map/ppermute | solution.py:467
  28.5 1.9 %collective-permute-start = (bf16[8,3072]{1,0:T(8,128)(2,1)S(1)}, bf16[8,3072]{1,0:T(8,128)(2,1)S(1)}, u32[]{:S(2)}, u32[]{:S(2)}) collective-permute-start(bf16[8,3072]{1,0:T(8,128)(2,1)S(1)} %shard_map.68.feat), channel_id=1, source_target_pairs={{0,2},{2,4},{4,6},{6,8},{8,10},{10,12},{12,14},{14,16},{16,18},{18... | collective-permute-start | bytes 147464 | tf_op jit(solution)/shard_map/ppermute | solution.py:467
  30.5 0.7 broadcast_subtract_fusion.ids
  31.2 0.7 copy.7.scale
  31.9 1.1 copy-done
  33.0 10.8 %shard_map.69 = (f32[3072,128]{1,0:T(8,128)S(1)}, bf16[3072,32]{1,0:T(8,128)(2,1)S(1)}, s32[128]{0:T(128)S(1)}) custom-call(s32[12,10]{1,0:T(8,128)S(1)} %broadcast_subtract_fusion.ids, bf16[8,3072]{1,0:T(8,128)(2,1)S(1)} %shard_map.68.feat, f32[8,1]{1,0:T(8,128)S(1)} %copy.7.scale, bf16[128,3072]{1,0:T(8,128)(2,1)S(1)} %copy-done), custom_call_target="tpu_custom_call" | custom-call | tf_op jit(solution)/shard_map/pallas_call | solution.py:172
  43.9 0.0 collective-permute-done.1.right
  43.9 0.0 collective-permute-done.left
  43.9 0.0 collective-permute-done.3.after
  43.9 0.0 collective-permute-done.2.before
  43.9 12.5 %shard_map.70.own = f32[3072,128]{1,0:T(8,128)S(1)} custom-call(s32[128]{0:T(128)S(1)} %get-tuple-element.7.far, f32[3072,128]{1,0:T(8,128)S(1)} %get-tuple-element.8.part, bf16[3072,32]{1,0:T(8,128)(2,1)S(1)} %get-tuple-element.9.rows_t, bf16[8,3072]{1,0:T(8,128)(2,1)S(1)} %collective-permute-done.left, bf16[8,3072]{1,0:T(8,128)(2,1)S(1)} %collective-permute-done.1.right, ...), custom_call_target="tpu_custom_call" | custom-call | tf_op jit(solution)/shard_map/pallas_call | solution.py:212
  56.4 1.9 %collective-permute-start.4 = (f32[3072,128]{1,0:T(8,128)S(1)}, f32[3072,128]{1,0:T(8,128)S(1)}, u32[]{:S(2)}, u32[]{:S(2)}) collective-permute-start(f32[3072,128]{1,0:T(8,128)S(1)} %shard_map.70.own), channel_id=1, source_target_pairs={{0,1},{1,0},{2,3},{3,2},{4,5},{5,4},{6,7},{7,6},{8,9},{9,8},{10,11... | collective-permute-start | bytes 4718600 | tf_op jit(solution)/shard_map/ppermute | solution.py:475
  58.3 3.4 %collective-permute-done.4.other = f32[3072,128]{1,0:T(8,128)S(1)} collective-permute-done((f32[3072,128]{1,0:T(8,128)S(1)}, f32[3072,128]{1,0:T(8,128)S(1)}, u32[]{:S(2)}, u32[]{:S(2)}) %collective-permute-start.4) | collective-permute-done | bytes 1572896 | tf_op jit(solution)/shard_map/ppermute | solution.py:475
  61.7 2.8 %shard_map.71 = f32[192,128]{1,0:T(8,128)S(1)} custom-call(s32[1]{0:T(128)} %bitcast.me, f32[3072,128]{1,0:T(8,128)S(1)} %shard_map.70.own, f32[3072,128]{1,0:T(8,128)S(1)} %collective-permute-done.4.other), custom_call_target="tpu_custom_call" | custom-call | tf_op jit(solution)/shard_map/pallas_call | solution.py:255
  64.6 1.9 %collective-permute-start.5 = (f32[192,128]{1,0:T(8,128)S(1)}, f32[192,128]{1,0:T(8,128)S(1)}, u32[]{:S(2)}, u32[]{:S(2)}) collective-permute-start(f32[192,128]{1,0:T(8,128)S(1)} %shard_map.71), channel_id=1, source_target_pairs={{0,2},{2,0},{4,6},{6,4},{8,10},{10,8},{12,14},{14,12},{16,18},{18,... | collective-permute-start | bytes 294920 | tf_op jit(solution)/shard_map/ppermute | solution.py:471
  66.5 5.3 %collective-permute-done.5 = f32[192,128]{1,0:T(8,128)S(1)} collective-permute-done((f32[192,128]{1,0:T(8,128)S(1)}, f32[192,128]{1,0:T(8,128)S(1)}, u32[]{:S(2)}, u32[]{:S(2)}) %collective-permute-start.5) | collective-permute-done | bytes 98336 | tf_op jit(solution)/shard_map/ppermute | solution.py:471
  71.8 1.9 %collective-permute-start.6 = (f32[192,128]{1,0:T(8,128)S(1)}, f32[192,128]{1,0:T(8,128)S(1)}, u32[]{:S(2)}, u32[]{:S(2)}) collective-permute-start(f32[192,128]{1,0:T(8,128)S(1)} %get-tuple-element.17), channel_id=1, source_target_pairs={{0,4},{2,6},{4,0},{6,2},{8,12},{10,14},{12,8},{14,10},{16,20},{18,... | collective-permute-start | bytes 294920 | tf_op jit(solution)/shard_map/ppermute | solution.py:471
  73.8 7.5 %collective-permute-done.6 = f32[192,128]{1,0:T(8,128)S(1)} collective-permute-done((f32[192,128]{1,0:T(8,128)S(1)}, f32[192,128]{1,0:T(8,128)S(1)}, u32[]{:S(2)}, u32[]{:S(2)}) %collective-permute-start.6) | collective-permute-done | bytes 98336 | tf_op jit(solution)/shard_map/ppermute | solution.py:471
  81.3 1.9 %collective-permute-start.7 = (f32[192,128]{1,0:T(8,128)S(1)}, f32[192,128]{1,0:T(8,128)S(1)}, u32[]{:S(2)}, u32[]{:S(2)}) collective-permute-start(f32[192,128]{1,0:T(8,128)S(1)} %get-tuple-element.15), channel_id=1, source_target_pairs={{0,8},{2,10},{4,12},{6,14},{8,0},{10,2},{12,4},{14,6},{16,24},{18,... | collective-permute-start | bytes 294920 | tf_op jit(solution)/shard_map/ppermute | solution.py:471
  83.2 8.6 %collective-permute-done.7 = f32[192,128]{1,0:T(8,128)S(1)} collective-permute-done((f32[192,128]{1,0:T(8,128)S(1)}, f32[192,128]{1,0:T(8,128)S(1)}, u32[]{:S(2)}, u32[]{:S(2)}) %collective-permute-start.7) | collective-permute-done | bytes 98336 | tf_op jit(solution)/shard_map/ppermute | solution.py:471
  91.8 1.9 %collective-permute-start.8 = (f32[192,128]{1,0:T(8,128)S(1)}, f32[192,128]{1,0:T(8,128)S(1)}, u32[]{:S(2)}, u32[]{:S(2)}) collective-permute-start(f32[192,128]{1,0:T(8,128)S(1)} %get-tuple-element.13), channel_id=1, source_target_pairs={{0,16},{2,18},{4,20},{6,22},{8,24},{10,26},{12,28},{14,30},{16,0},... | collective-permute-start | bytes 294920 | tf_op jit(solution)/shard_map/ppermute | solution.py:471
  93.7 4.6 %collective-permute-done.8 = f32[192,128]{1,0:T(8,128)S(1)} collective-permute-done((f32[192,128]{1,0:T(8,128)S(1)}, f32[192,128]{1,0:T(8,128)S(1)}, u32[]{:S(2)}, u32[]{:S(2)}) %collective-permute-start.8) | collective-permute-done | bytes 98336 | tf_op jit(solution)/shard_map/ppermute | solution.py:471
  98.3 1.9 %collective-permute-start.9 = (f32[960,128]{1,0:T(8,128)S(1)}, f32[960,128]{1,0:T(8,128)S(1)}, u32[]{:S(2)}, u32[]{:S(2)}) collective-permute-start(f32[960,128]{1,0:T(8,128)S(1)} %add_dynamic-update-slice_fusion.mine), channel_id=1, source_target_pairs={{0,1},{1,0},{2,3},{3,2},{4,5},{5,4},{6,7},{7,6},{8,9},{9,8},{10,11... | collective-permute-start | bytes 1474568 | tf_op jit(solution)/shard_map/ppermute | solution.py:475
  100.3 1.8 %collective-permute-done.9.theirs = f32[960,128]{1,0:T(8,128)S(1)} collective-permute-done((f32[960,128]{1,0:T(8,128)S(1)}, f32[960,128]{1,0:T(8,128)S(1)}, u32[]{:S(2)}, u32[]{:S(2)}) %collective-permute-start.9) | collective-permute-done | bytes 491552 | tf_op jit(solution)/shard_map/ppermute | solution.py:475
  102.1 14.8 %shard_map.72 = (f32[4,256,128]{2,1,0:T(8,128)}, f32[128,256]{1,0:T(8,128)S(1)}) custom-call(s32[1]{0:T(128)} %bitcast.me, f32[960,128]{1,0:T(8,128)S(1)} %add_dynamic-update-slice_fusion.mine, f32[960,128]{1,0:T(8,128)S(1)} %collective-permute-done.9.theirs), custom_call_target="tpu_custom_call" | custom-call | tf_op jit(solution)/shard_map/pallas_call | solution.py:413
  116.9 3.0 %shard_map.73 = f32[3072,128]{1,0:T(8,128)} custom-call(s32[1]{0:T(128)} %bitcast.me, f32[3072,128]{1,0:T(8,128)S(1)} %shard_map.70.own, f32[3072,128]{1,0:T(8,128)S(1)} %collective-permute-done.4.other, f32[128,256]{1,0:T(8,128)S(1)} %get-tuple-element.11.weight), custom_call_target="tpu_custom_call" | custom-call | tf_op jit(solution)/shard_map/pallas_call | solution.py:452
  (7 shorter events, 0.1 us)
Async XLA Ops:
  0.6 43.3 %collective-permute-start.3 = (bf16[128,3072]{1,0:T(8,128)(2,1)}, bf16[128,3072]{1,0:T(8,128)(2,1)S(1)}, u32[]{:S(2)}, u32[]{:S(2)}) collective-permute-start(bf16[128,3072]{1,0:T(8,128)(2,1)} %probes.1), channel_id=1, source_target_pairs={{2,0},{4,2},{6,4},{8,6},{10,8},{12,10},{14,12},{16,14},{18,16},{20... | collective-permute-start | bytes 2359304 | tf_op jit(solution)/shard_map/ppermute | solution.py:467
  14.8 29.1 %collective-permute-start.2 = (bf16[128,3072]{1,0:T(8,128)(2,1)}, bf16[128,3072]{1,0:T(8,128)(2,1)S(1)}, u32[]{:S(2)}, u32[]{:S(2)}) collective-permute-start(bf16[128,3072]{1,0:T(8,128)(2,1)} %probes.1), channel_id=1, source_target_pairs={{0,2},{2,4},{4,6},{6,8},{8,10},{10,12},{12,14},{14,16},{16,18},{18... | collective-permute-start | bytes 2359304 | tf_op jit(solution)/shard_map/ppermute | solution.py:467
  16.7 0.8 copy-start.1
  17.5 0.7 copy-start.2
  20.4 23.5 %collective-permute-start.1 = (bf16[8,3072]{1,0:T(8,128)(2,1)S(1)}, bf16[8,3072]{1,0:T(8,128)(2,1)S(1)}, u32[]{:S(2)}, u32[]{:S(2)}) collective-permute-start(bf16[8,3072]{1,0:T(8,128)(2,1)S(1)} %shard_map.68.feat), channel_id=1, source_target_pairs={{2,0},{4,2},{6,4},{8,6},{10,8},{12,10},{14,12},{16,14},{18,16},{20... | collective-permute-start | bytes 147464 | tf_op jit(solution)/shard_map/ppermute | solution.py:467
  28.5 15.4 %collective-permute-start = (bf16[8,3072]{1,0:T(8,128)(2,1)S(1)}, bf16[8,3072]{1,0:T(8,128)(2,1)S(1)}, u32[]{:S(2)}, u32[]{:S(2)}) collective-permute-start(bf16[8,3072]{1,0:T(8,128)(2,1)S(1)} %shard_map.68.feat), channel_id=1, source_target_pairs={{0,2},{2,4},{4,6},{6,8},{8,10},{10,12},{12,14},{14,16},{16,18},{18... | collective-permute-start | bytes 147464 | tf_op jit(solution)/shard_map/ppermute | solution.py:467
  31.9 1.1 copy-start
  56.4 5.3 %collective-permute-start.4 = (f32[3072,128]{1,0:T(8,128)S(1)}, f32[3072,128]{1,0:T(8,128)S(1)}, u32[]{:S(2)}, u32[]{:S(2)}) collective-permute-start(f32[3072,128]{1,0:T(8,128)S(1)} %shard_map.70.own), channel_id=1, source_target_pairs={{0,1},{1,0},{2,3},{3,2},{4,5},{5,4},{6,7},{7,6},{8,9},{9,8},{10,11... | collective-permute-start | bytes 4718600 | tf_op jit(solution)/shard_map/ppermute | solution.py:475
  64.6 7.3 %collective-permute-start.5 = (f32[192,128]{1,0:T(8,128)S(1)}, f32[192,128]{1,0:T(8,128)S(1)}, u32[]{:S(2)}, u32[]{:S(2)}) collective-permute-start(f32[192,128]{1,0:T(8,128)S(1)} %shard_map.71), channel_id=1, source_target_pairs={{0,2},{2,0},{4,6},{6,4},{8,10},{10,8},{12,14},{14,12},{16,18},{18,... | collective-permute-start | bytes 294920 | tf_op jit(solution)/shard_map/ppermute | solution.py:471
  71.8 9.4 %collective-permute-start.6 = (f32[192,128]{1,0:T(8,128)S(1)}, f32[192,128]{1,0:T(8,128)S(1)}, u32[]{:S(2)}, u32[]{:S(2)}) collective-permute-start(f32[192,128]{1,0:T(8,128)S(1)} %get-tuple-element.17), channel_id=1, source_target_pairs={{0,4},{2,6},{4,0},{6,2},{8,12},{10,14},{12,8},{14,10},{16,20},{18,... | collective-permute-start | bytes 294920 | tf_op jit(solution)/shard_map/ppermute | solution.py:471
  81.3 10.5 %collective-permute-start.7 = (f32[192,128]{1,0:T(8,128)S(1)}, f32[192,128]{1,0:T(8,128)S(1)}, u32[]{:S(2)}, u32[]{:S(2)}) collective-permute-start(f32[192,128]{1,0:T(8,128)S(1)} %get-tuple-element.15), channel_id=1, source_target_pairs={{0,8},{2,10},{4,12},{6,14},{8,0},{10,2},{12,4},{14,6},{16,24},{18,... | collective-permute-start | bytes 294920 | tf_op jit(solution)/shard_map/ppermute | solution.py:471
  91.8 6.5 %collective-permute-start.8 = (f32[192,128]{1,0:T(8,128)S(1)}, f32[192,128]{1,0:T(8,128)S(1)}, u32[]{:S(2)}, u32[]{:S(2)}) collective-permute-start(f32[192,128]{1,0:T(8,128)S(1)} %get-tuple-element.13), channel_id=1, source_target_pairs={{0,16},{2,18},{4,20},{6,22},{8,24},{10,26},{12,28},{14,30},{16,0},... | collective-permute-start | bytes 294920 | tf_op jit(solution)/shard_map/ppermute | solution.py:471
  98.3 3.8 %collective-permute-start.9 = (f32[960,128]{1,0:T(8,128)S(1)}, f32[960,128]{1,0:T(8,128)S(1)}, u32[]{:S(2)}, u32[]{:S(2)}) collective-permute-start(f32[960,128]{1,0:T(8,128)S(1)} %add_dynamic-update-slice_fusion.mine), channel_id=1, source_target_pairs={{0,1},{1,0},{2,3},{3,2},{4,5},{5,4},{6,7},{7,6},{8,9},{9,8},{10,11... | collective-permute-start | bytes 1474568 | tf_op jit(solution)/shard_map/ppermute | solution.py:475

commit v3 on v2

--- a/solution.py
+++ b/solution.py
@@ -10,6 +10,7 @@
 LEVELS = 4
 LANES = 128
 ROWS = 8
+TILE = (ROWS, LANES)
 LOG2_E = 1.4426950408889634
 LN_2 = 0.6931471805599453
 NUGGET = 2.0
@@ -73,7 +74,7 @@
 
 
 SHIFT = 6
-SLOTS = 128
+SLOTS = 160
 WIDE = 4
 
 
@@ -94,7 +95,12 @@
 
 
 def weights(scale):
-    return (3.0 * LOG2_E * LOG2_E) / (scale[...] * scale[...])
+    count = scale.shape[0]
+    row = lax.broadcasted_iota(jnp.int32, (count, 1), 0)
+    held = jnp.full((count, 1), scale[0], F32)
+    for f in range(1, count):
+        held = jnp.where(row == f, scale[f], held)
+    return (3.0 * LOG2_E * LOG2_E) / (held * held)
 
 
 def load_columns(cols, panel, feats, probes, weight, blocks):
@@ -111,34 +117,47 @@
     panel[last] = jnp.zeros(panel.shape[1:], BF16)
 
 
-def run_tasks(tasks, count, slot_of, rows_t, cols, panel, out):
+def run_tasks(tasks, count, slot_of, rows_t, cols, panel, out, kerns):
     block = cols.shape[2]
 
-    def some(t, carry):
-        parts = []
-        for u in range(WIDE):
-            code = tasks[t * WIDE + u]
-            at = pl.ds(pl.multiple_of((code >> SHIFT) * block, block), block)
-            slot = slot_of(code & ((1 << SHIFT) - 1))
-            dist = jnp.maximum(dot16(rows_t[at, :], cols[slot], 1, 0), TINY)
-            root = dist * lax.rsqrt(dist)
-            kern = (1.0 + LN_2 * root) * jnp.exp2(-root)
-            parts.append((at, dot16(kern.astype(BF16), panel[slot], 1, 1)))
-        for at, part in parts:
-            out[at, :] += part
+    def where_of(n):
+        code = tasks[n]
+        at = pl.ds(pl.multiple_of((code >> SHIFT) * block, block), block)
+        return at, slot_of(code & ((1 << SHIFT) - 1))
+
+    def product(n, kern):
+        at, slot = where_of(n)
+        return at, dot16(kern, panel[slot], 1, 1)
+
+    def some(i, carry):
+        for half in range(2):
+            group = 2 * i + half
+            last = jnp.maximum(group - 1, 0)
+            for u in range(WIDE):
+                to, part = product(last * WIDE + u, kerns[1 - half][u])
+                at, slot = where_of(group * WIDE + u)
+                dist = jnp.maximum(dot16(rows_t[at, :], cols[slot], 1, 0), TINY)
+                root = dist * lax.rsqrt(dist)
+                kerns[half][u] = ((1.0 + LN_2 * root) * jnp.exp2(-root)).astype(BF16)
+                out[to, :] += part
         return carry
 
-    lax.fori_loop(0, (count + (WIDE - 1)) // WIDE, some, 0)
-
-
-def near_kernel(ids, feat, scale, probes, out, rows_t, far, tasks, cols, panel):
-    blocks, near = ids.shape
+    kerns[1][...] = jnp.zeros_like(kerns[1])
+    pairs = (count + (2 * WIDE - 1)) // (2 * WIDE)
+    lax.fori_loop(0, pairs, some, 0)
+    for u in range(WIDE):
+        to, part = product(jnp.maximum(2 * pairs - 1, 0) * WIDE + u, kerns[1][u])
+        out[to, :] += part
+
+
+def near_kernel(near_blocks, first, scale, feat, probes, out, rows_t, far, tasks, cols, panel, k0, k1):
+    blocks, near = near_blocks.shape
     block = feat.shape[1] // blocks
 
     def scan(a, counts):
         mine, rest = counts
         for j in range(near):
-            listed = ids[a, j]
+            listed = near_blocks[a, j] - first[0]
             code = (a << SHIFT) + listed
             inside = jnp.where((listed >= blocks) & (listed < 2 * blocks), 1, 0)
             tasks[mine] = code
@@ -148,7 +167,7 @@
         return mine, rest
 
     mine, rest = lax.fori_loop(0, blocks, scan, (jnp.int32(0), jnp.int32(0)))
-    for u in range(WIDE):
+    for u in range(2 * WIDE):
         tasks[mine + u] = 2 * blocks
         far[rest + u] = 3 * blocks
     far[SLOTS - 1] = rest
@@ -161,12 +180,12 @@
     nugget = jnp.where(here == there, NUGGET, 0.0).astype(BF16)
     for b in range(blocks):
         out[b * block : (b + 1) * block, :] = dot16(nugget, panel[b], 1, 1)
-    run_tasks(tasks, mine, lambda listed: listed - blocks, rows_t, cols, panel, out)
-
-
-def near_part(ids, feat, scale, probes):
+    run_tasks(tasks, mine, lambda listed: listed - blocks, rows_t, cols, panel, out, (k0, k1))
+
+
+def near_part(near_blocks, first, scale, feat, probes):
     half, leaf = probes.shape
-    blocks = ids.shape[0]
+    blocks = near_blocks.shape[0]
     block = leaf // blocks
     whole = pl.BlockSpec(memory_space=pltpu.VMEM)
     return call(
@@ -177,20 +196,21 @@
             jax.ShapeDtypeStruct((SLOTS,), jnp.int32),
         ),
         grid_spec=pltpu.PrefetchScalarGridSpec(
-            num_scalar_prefetch=1,
+            num_scalar_prefetch=3,
             grid=(1,),
-            in_specs=[whole] * 3,
+            in_specs=[whole] * 2,
             out_specs=[whole, whole, pl.BlockSpec(memory_space=pltpu.SMEM)],
             scratch_shapes=[
                 pltpu.SMEM((SLOTS,), jnp.int32),
                 pltpu.VMEM((blocks + 1, 32, block), BF16),
                 pltpu.VMEM((blocks + 1, half, block), BF16),
+                *[pltpu.VMEM((WIDE, block, block), BF16)] * 2,
             ],
         ),
-    )(ids, feat, scale, probes)
-
-
-def far_kernel(far, part, rows_t, left, right, scale, before, after, out, cols, panel):
+    )(near_blocks, first, scale, feat, probes)
+
+
+def far_kernel(far, scale, part, rows_t, left, right, before, after, out, cols, panel, k0, k1):
     blocks = (cols.shape[0] - 1) // 2
     load_columns(cols, panel, [left, right], [before, after], weights(scale), blocks)
     out[...] = part[...]
@@ -202,10 +222,11 @@
         cols,
         panel,
         out,
+        (k0, k1),
     )
 
 
-def far_part(far, part, rows_t, left, right, scale, before, after, blocks):
+def far_part(far, scale, part, rows_t, left, right, before, after, blocks):
     half, leaf = before.shape
     block = leaf // blocks
     whole = pl.BlockSpec(memory_space=pltpu.VMEM)
@@ -213,58 +234,101 @@
         far_kernel,
         pltpu.VMEM((leaf, half), F32),
         grid_spec=pltpu.PrefetchScalarGridSpec(
-            num_scalar_prefetch=1,
+            num_scalar_prefetch=2,
             grid=(1,),
-            in_specs=[whole] * 7,
+            in_specs=[whole] * 6,
             out_specs=whole,
             scratch_shapes=[
                 pltpu.VMEM((2 * blocks + 1, 32, block), BF16),
                 pltpu.VMEM((2 * blocks + 1, half, block), BF16),
+                *[pltpu.VMEM((WIDE, block, block), BF16)] * 2,
             ],
         ),
-    )(far, part, rows_t, left, right, scale, before, after)
-
-
-def gram_kernel(me, own, other, out):
-    n = own.shape[1]
-
-    @pl.when(pl.program_id(0) == 0)
-    def _():
-        out[...] = jnp.zeros_like(out)
-
-    def product(a, b):
-        return dot16(a[0], b[0], 0, 0) + (dot16(a[0], b[1], 0, 0) + dot16(a[1], b[0], 0, 0))
-
-    mine = halves(own[...])
-    out[0:n] += product(mine, mine)
+    )(far, scale, part, rows_t, left, right, before, after)
+
+
+HALF = LANES // 2
+PACKED = HALF + ROWS
+
+
+def pack(block):
+    shape = (HALF, LANES)
+    row = lax.broadcasted_iota(jnp.int32, shape, 0)
+    col = lax.broadcasted_iota(jnp.int32, shape, 1) - HALF
+    bottom = block[HALF:, :]
+    top = pltpu.roll(block[:HALF, :], HALF, 1)
+    diagonal = jnp.sum(jnp.where(row == col, bottom, 0.0), 0, keepdims=True)
+    body = jnp.where((col >= 0) & (row >= col), top, bottom)
+    return body, jnp.broadcast_to(diagonal, TILE)
+
+
+def unpack(body, diagonal):
+    shape = (HALF, HALF)
+    row = lax.broadcasted_iota(jnp.int32, shape, 0)
+    col = lax.broadcasted_iota(jnp.int32, shape, 1)
+    side = body[:, :HALF]
+    fold = body[:, HALF:]
+    flip = fold.T
+    top = jnp.where(row >= col, fold, flip)
+    bottom = jnp.where(row < col, fold, flip)
+    bottom = jnp.where(row == col, diagonal[:1, HALF:], bottom)
+    return jnp.concatenate(
+        [jnp.concatenate([top, side.T], 1), jnp.concatenate([side, bottom], 1)], 0
+    )
+
+
+def product(a, b):
+    return dot16(a[0], b[0], 0, 0) + (dot16(a[0], b[1], 0, 0) + dot16(a[1], b[0], 0, 0))
+
+
+def own_kernel(own, out, high, low):
+    a0, a1 = halves(own[...])
+    high[...] = a0
+    low[...] = a1
+    out[:HALF], out[HALF:] = pack(product((a0, a1), (a0, a1)))
+
+
+def own_gram(own):
+    leaf, half = own.shape
+    return call(
+        own_kernel,
+        (
+            pltpu.VMEM((PACKED, half), F32),
+            pltpu.VMEM((leaf, half), BF16),
+            pltpu.VMEM((leaf, half), BF16),
+        ),
+    )(own)
+
+
+def gram_kernel(me, block, high, low, other, out, high_o, low_o):
+    b0, b1 = halves(other[...])
+    high_o[...] = b0
+    low_o[...] = b1
+    out[:PACKED] = block[...]
 
     @pl.when(me[0] == 0)
     def _():
-        out[n:] += product(halves(other[:, : n // 2]), halves(own[...]))
+        out[PACKED:] = product((b0[:, :HALF], b1[:, :HALF]), (high[...], low[...]))
 
     @pl.when(me[0] == 1)
     def _():
-        out[n:] += product(halves(own[:, n // 2 :]), halves(other[...]))
-
-
-def gram_blocks(me, own, other):
-    leaf, half = own.shape
-    steps = 4
-    height = half + half // 2
-    rows = pl.BlockSpec((leaf // steps, half), lambda i, me: (i, 0))
+        out[PACKED:] = product((high[:, HALF:], low[:, HALF:]), (b0, b1))
+
+
+def gram_blocks(me, block, high, low, other):
+    leaf, half = other.shape
+    whole = pl.BlockSpec(memory_space=pltpu.VMEM)
     return call(
         gram_kernel,
-        jax.ShapeDtypeStruct((height, half), F32),
+        (
+            jax.ShapeDtypeStruct((PACKED + HALF, half), F32),
+            pltpu.VMEM((leaf, half), BF16),
+            pltpu.VMEM((leaf, half), BF16),
+        ),
         grid_spec=pltpu.PrefetchScalarGridSpec(
-            num_scalar_prefetch=1,
-            grid=(steps,),
-            in_specs=[rows, rows],
-            out_specs=pl.BlockSpec((height, half), lambda i, me: (0, 0)),
-        ),
-    )(me, own, other)
-
-
-TILE = (ROWS, LANES)
+            num_scalar_prefetch=1, grid=(1,), in_specs=[whole] * 4, out_specs=[whole] * 3
+        ),
+    )(me, block, high, low, other)
 
 
 def row_of(x, k):
@@ -387,78 +451,72 @@
         straighten(ups, l, n)
 
 
-def factor_kernel(me, mine, theirs, transfer, weight, pieces, work, ups, invs):
+def factor_kernel(me, mine, theirs, own0, own1, other0, other1, transfer, basis, pieces, work, ups, invs, moved, rows, sems):
     n = LANES
-    height = n + n // 2
+    height = PACKED + HALF
     pieces[me[0]] = mine[...]
     pieces[1 - me[0]] = theirs[...]
 
     def gram(l, b):
         at = l * height
         if b == 1:
-            return jnp.concatenate([pieces[p, at + n : at + height, :] for p in range(2)], 0)
-        return pieces[b // 2, at : at + n, :]
+            return jnp.concatenate([pieces[p, at + PACKED : at + height, :] for p in range(2)], 0)
+        part = pieces.at[b // 2]
+        return unpack(part[at : at + HALF, :], part[at + HALF : at + PACKED, :])
 
     factor(gram, work, ups, invs)
     cols = pl.ds(pl.multiple_of(me[0] * n, n), n)
+    rest = pl.ds(pl.multiple_of((1 - me[0]) * n, n), n)
+    scale = math.sqrt(2**LEVELS * own0.shape[0])
+    weight = invs.at[LEVELS]
+    near0, near1 = halves(weight[cols, cols] * scale)
+    far0, far1 = halves(weight[cols, rest] * scale)
+    steps, size, _ = rows.shape
+    copies = []
+    for s in range(steps):
+        at = slice(s * size, (s + 1) * size)
+        a0, a1, b0, b1 = own0[at, :], own1[at, :], other0[at, :], other1[at, :]
+        small = dot16(a0, near1, 1, 1) + dot16(a1, near0, 1, 1)
+        small += dot16(b0, far1, 1, 1) + dot16(b1, far0, 1, 1)
+        rows[s] = small + (dot16(a0, near0, 1, 1) + dot16(b0, far0, 1, 1))
+        copies.append(pltpu.make_async_copy(rows.at[s], basis.at[pl.ds(s * size, size)], sems.at[s]))
+        copies[-1].start()
     for l in range(LEVELS):
-        transfer[l] = dot(ups[l], invs[l + 1, cols, :], 1, 1)
-    weight[...] = invs[LEVELS, cols, :]
-
-
-def factors(me, mine, theirs):
+        moved[l] = dot(ups[l], invs[l + 1, cols, :], 1, 1)
+        copies.append(pltpu.make_async_copy(moved.at[l], transfer.at[l], sems.at[steps + l]))
+        copies[-1].start()
+    for copy in copies:
+        copy.wait()
+
+
+def factors(me, mine, theirs, own, other):
     n = 2 * LANES
     count = LEVELS + 1
+    leaf, half = own[0].shape
+    steps = 6
     whole = pl.BlockSpec(memory_space=pltpu.VMEM)
     return call(
         factor_kernel,
         (
-            jax.ShapeDtypeStruct((LEVELS, n, LANES), F32),
-            jax.ShapeDtypeStruct((LANES, n), F32),
+            jax.ShapeDtypeStruct((LEVELS, n, half), F32),
+            jax.ShapeDtypeStruct((leaf, half), F32),
         ),
         grid_spec=pltpu.PrefetchScalarGridSpec(
             num_scalar_prefetch=1,
             grid=(1,),
-            in_specs=[whole] * 2,
-            out_specs=[whole] * 2,
+            in_specs=[whole] * 6,
+            out_specs=[pl.BlockSpec(memory_space=pl.ANY)] * 2,
             scratch_shapes=[
                 pltpu.VMEM((2, *mine.shape), F32),
                 pltpu.VMEM((count, LANES, LANES), F32),
                 pltpu.VMEM((count, n, n), F32),
                 pltpu.VMEM((count, n, n), F32),
+                pltpu.VMEM((LEVELS, n, half), F32),
+                pltpu.VMEM((steps, leaf // steps, half), F32),
+                pltpu.SemaphoreType.DMA((steps + LEVELS,)),
             ],
         ),
-    )(me, mine, theirs)
-
-
-def basis_kernel(me, own, other, weight, out):
-    n = LANES
-    scale = math.sqrt(2**LEVELS * own.shape[0] * pl.num_programs(0))
-    mine = pl.ds(pl.multiple_of(me[0] * n, n), n)
-    rest = pl.ds(pl.multiple_of((1 - me[0]) * n, n), n)
-    total = None
-    for ref, cols in ((own, mine), (other, rest)):
-        a0, a1 = halves(ref[...])
-        b0, b1 = halves(weight[:, cols] * scale)
-        part = dot16(a0, b0, 1, 1) + (dot16(a0, b1, 1, 1) + dot16(a1, b0, 1, 1))
-        total = part if total is None else total + part
-    out[...] = total
-
-
-def basis_rows(me, own, other, weight):
-    leaf, half = own.shape
-    steps = 4
-    rows = pl.BlockSpec((leaf // steps, half), lambda i, me: (i, 0))
-    return call(
-        basis_kernel,
-        jax.ShapeDtypeStruct((leaf, half), F32),
-        grid_spec=pltpu.PrefetchScalarGridSpec(
-            num_scalar_prefetch=1,
-            grid=(steps,),
-            in_specs=[rows, rows, pl.BlockSpec((half, 2 * half), lambda i, me: (0, 0))],
-            out_specs=rows,
-        ),
-    )(me, own, other, weight)
+    )(me, mine, theirs, *own, *other)
 
 
 def beside(array, shift):
@@ -478,25 +536,25 @@
 def body(features, probes, lengthscale, near_blocks, leaf_order):
     blocks = near_blocks.shape[0]
     me = lax.axis_index("probe").astype(jnp.int32)[None]
-    ids = near_blocks - (lax.axis_index("leaf") - 1) * blocks
-    scale = lengthscale[:, None]
+    first = ((lax.axis_index("leaf") - 1) * blocks).astype(jnp.int32)[None]
     probes_before = beside(probes, 1)
     probes_after = beside(probes, -1)
     ordered = order_features(features, leaf_order)
     before = beside(ordered, 1)
     after = beside(ordered, -1)
-    part, rows_t, far = near_part(ids, ordered, scale, probes)
-    own = far_part(far, part, rows_t, before, after, scale, probes_before, probes_after, blocks)
+    part, rows_t, far = near_part(near_blocks, first, lengthscale, ordered, probes)
+    own = far_part(
+        far, lengthscale, part, rows_t, before, after, probes_before, probes_after, blocks
+    )
     other = other_core(own)
-    gram = gram_blocks(me, own, other)
+    block, *own_pieces = own_gram(own)
+    gram, *other_pieces = gram_blocks(me, block, *own_pieces, other)
     grams = [gram]
     for depth in range(LEVELS):
         gram = gram + sibling(gram, depth)
         grams.append(gram)
     mine = jnp.concatenate(grams, 0)
-    transfer, weight = factors(me, mine, other_core(mine))
-    basis = basis_rows(me, own, other, weight)
-    return transfer, basis
+    return factors(me, mine, other_core(mine), own_pieces, other_pieces)
 
 
 def solution(mesh):

time: 121 us -> 110 us (0.909)
  Pallas kernels: 46.1 us -> 39.1 us
  waiting for transfers between devices: 31.2 us -> 27.4 us
    pallas_call x1, Pallas kernels: 10.8 us -> 7.98 us  [near_part(): call(near_kernel, (pltpu.VMEM((leaf, half), F32), pltpu.VMEM((leaf, 32),...]
    ppermute x4, waiting for transfers between devices: 26 us -> 23.3 us  [sibling(): lax.ppermute(array, 'leaf', [(i, i ^ 1 << bit) for i in range(lax.axis_si...]
    pallas_call x1, Pallas kernels: 12.5 us -> 10.1 us  [far_part(): call(far_kernel, pltpu.VMEM((leaf, half), F32), grid_spec=pltpu.PrefetchS...]
    pallas_call x3, Pallas kernels: 20.6 us -> 18.8 us  [the longest x1 17 us: factors(): call(factor_kernel, (jax.ShapeDtypeStruct((LEVELS, n, half), F32), jax.Sh...]
    unnamed x7 -> x11, local copies, waits for them, and re-layouts: 2.64 us -> 3.98 us
    ppermute x2, waiting for transfers between devices: 5.2 us -> 3.93 us  [other_core(): return lax.ppermute(array, 'probe', [(0, 1), (1, 0)])]
  transfers between devices with their start and end apart: 10 -> 10, of which waited for: 6 -> 7; matrix products, arithmetic and copies ran while one was open for 1% -> 0% of each run, Pallas kernels for 11% -> 10%
where the time goes in v3:
time: 110 us; the launch traced here: 109 us
  Pallas kernels  39.1 us (36%)
  starting transfers between devices  37.8 us (34%)
  waiting for transfers between devices  27.4 us (25%)
  local copies, waits for them, and re-layouts  3.98 us (4%)
    ppermute x4, starting transfers between devices, beside(): return lax.ppermute(array, 'leaf', pairs)  26.1 us
    ppermute x4, waiting for transfers between devices, sibling(): lax.ppermute(array, 'leaf', [(i, i ^ 1 << bit) for i in range(lax.axis_si...  23.3 us
    pallas_call x1, Pallas kernels, factors(): call(factor_kernel, (jax.ShapeDtypeStruct((LEVELS, n, half), F32), jax.Sh...  17 us
    pallas_call x1, Pallas kernels, far_part(): call(far_kernel, pltpu.VMEM((leaf, half), F32), grid_spec=pltpu.PrefetchS...  10.1 us
    pallas_call x1, Pallas kernels, near_part(): call(near_kernel, (pltpu.VMEM((leaf, half), F32), pltpu.VMEM((leaf, 32),...  7.98 us
    ppermute x4, starting transfers between devices, sibling(): lax.ppermute(array, 'leaf', [(i, i ^ 1 << bit) for i in range(lax.axis_si...  7.68 us
    ppermute x2, starting transfers between devices, other_core(): return lax.ppermute(array, 'probe', [(0, 1), (1, 0)])  4.02 us
    unnamed x11, local copies, waits for them, and re-layouts  3.98 us
  transfers between devices with their start and end apart: 10, of which 7 were waited for; matrix products, arithmetic and copies ran while one was open for 0% of the time, Pallas kernels for 10%

profile of v3, /device:TPU:6, one launch (start us, length us, event | category | flops | bytes accessed | tf_op | source)
XLA Modules:
  0.0 109.3 jit_solution(12623350370620921896)
XLA Ops:
  0.6 14.1 %collective-permute-start.3 = (bf16[128,3072]{1,0:T(8,128)(2,1)}, bf16[128,3072]{1,0:T(8,128)(2,1)S(1)}, u32[]{:S(2)}, u32[]{:S(2)}) collective-permute-start(bf16[128,3072]{1,0:T(8,128)(2,1)} %probes.1), channel_id=1, source_target_pairs={{2,0},{4,2},{6,4},{8,6},{10,8},{12,10},{14,12},{16,14},{18,16},{20... | collective-permute-start | bytes 2359304 | tf_op jit(solution)/shard_map/ppermute | solution.py:525
  14.8 1.9 %collective-permute-start.2 = (bf16[128,3072]{1,0:T(8,128)(2,1)}, bf16[128,3072]{1,0:T(8,128)(2,1)S(1)}, u32[]{:S(2)}, u32[]{:S(2)}) collective-permute-start(bf16[128,3072]{1,0:T(8,128)(2,1)} %probes.1), channel_id=1, source_target_pairs={{0,2},{2,4},{4,6},{6,8},{8,10},{10,12},{12,14},{14,16},{16,18},{18... | collective-permute-start | bytes 2359304 | tf_op jit(solution)/shard_map/ppermute | solution.py:525
  16.7 0.8 copy-done.1
  17.5 0.7 copy-done.2
  18.2 2.2 %shard_map.68.feat = bf16[8,3072]{1,0:T(8,128)(2,1)S(1)} custom-call(bf16[8,3072]{1,0:T(8,128)(2,1)S(1)} %copy-done.1, s32[1,3072]{1,0:T(1,128)S(1)} %copy-done.2), custom_call_target="tpu_custom_call" | custom-call | tf_op jit(solution)/shard_map/pallas_call | solution.py:73
  20.4 8.1 %collective-permute-start.1 = (bf16[8,3072]{1,0:T(8,128)(2,1)S(1)}, bf16[8,3072]{1,0:T(8,128)(2,1)S(1)}, u32[]{:S(2)}, u32[]{:S(2)}) collective-permute-start(bf16[8,3072]{1,0:T(8,128)(2,1)S(1)} %shard_map.68.feat), channel_id=1, source_target_pairs={{2,0},{4,2},{6,4},{8,6},{10,8},{12,10},{14,12},{16,14},{18,16},{20... | collective-permute-start | bytes 147464 | tf_op jit(solution)/shard_map/ppermute | solution.py:525
  28.5 1.9 %collective-permute-start = (bf16[8,3072]{1,0:T(8,128)(2,1)S(1)}, bf16[8,3072]{1,0:T(8,128)(2,1)S(1)}, u32[]{:S(2)}, u32[]{:S(2)}) collective-permute-start(bf16[8,3072]{1,0:T(8,128)(2,1)S(1)} %shard_map.68.feat), channel_id=1, source_target_pairs={{0,2},{2,4},{4,6},{6,8},{8,10},{10,12},{12,14},{14,16},{16,18},{18... | collective-permute-start | bytes 147464 | tf_op jit(solution)/shard_map/ppermute | solution.py:525
  30.5 0.0 copy-start
  30.5 1.1 %copy-done = bf16[128,3072]{1,0:T(8,128)(2,1)S(1)} copy-done((bf16[128,3072]{1,0:T(8,128)(2,1)S(1)}, bf16[128,3072]{1,0:T(8,128)(2,1)}, u32[]{:S(2)}) %copy-start) | copy-done | bytes 786456
  31.6 0.7 copy-done.3
  32.3 0.7 copy-done.4
  32.9 8.0 %shard_map.69 = (f32[3072,128]{1,0:T(8,128)S(1)}, bf16[3072,32]{1,0:T(8,128)(2,1)S(1)}, s32[160]{0:T(256)S(1)}) custom-call(s32[12,10]{1,0:T(8,128)S(1)} %copy-done.3, s32[1]{0:T(128)} %bitcast.1.first, f32[8]{0:T(128)S(1)} %copy-done.4, bf16[8,3072]{1,0:T(8,128)(2,1)S(1)} %shard_map.68.feat, bf16[128,3072]{1,0:T(8,128)(2,1)S(1)} %copy-done), custom_call_target="tpu_custom_call" | custom-call | tf_op jit(solution)/shard_map/pallas_call | solution.py:191
  40.9 0.0 collective-permute-done.1.right
  40.9 0.2 collective-permute-done.left
  41.1 0.0 collective-permute-done.3.after
  41.1 0.0 collective-permute-done.2.before
  41.1 10.1 %shard_map.70.own = f32[3072,128]{1,0:T(8,128)S(1)} custom-call(s32[160]{0:T(256)S(1)} %get-tuple-element.11.far, f32[8]{0:T(128)S(1)} %copy-done.4, f32[3072,128]{1,0:T(8,128)S(1)} %get-tuple-element.12.part, bf16[3072,32]{1,0:T(8,128)(2,1)S(1)} %get-tuple-element.13.rows_t, bf16[8,3072]{1,0:T(8,128)(2,1)S(1)} %collective-permute-done.left, ...), custom_call_target="tpu_custom_call" | custom-call | tf_op jit(solution)/shard_map/pallas_call | solution.py:233
  51.3 1.9 %collective-permute-start.4 = (f32[3072,128]{1,0:T(8,128)S(1)}, f32[3072,128]{1,0:T(8,128)S(1)}, u32[]{:S(2)}, u32[]{:S(2)}) collective-permute-start(f32[3072,128]{1,0:T(8,128)S(1)} %shard_map.70.own), channel_id=1, source_target_pairs={{0,1},{1,0},{2,3},{3,2},{4,5},{5,4},{6,7},{7,6},{8,9},{9,8},{10,11... | collective-permute-start | bytes 4718600 | tf_op jit(solution)/shard_map/ppermute | solution.py:533
  53.2 0.9 shard_map.71
  54.1 2.5 %collective-permute-done.4.other = f32[3072,128]{1,0:T(8,128)S(1)} collective-permute-done((f32[3072,128]{1,0:T(8,128)S(1)}, f32[3072,128]{1,0:T(8,128)S(1)}, u32[]{:S(2)}, u32[]{:S(2)}) %collective-permute-start.4) | collective-permute-done | bytes 1572896 | tf_op jit(solution)/shard_map/ppermute | solution.py:533
  56.6 1.0 shard_map.72
  57.6 1.9 %collective-permute-start.5 = (f32[136,128]{1,0:T(8,128)S(1)}, f32[136,128]{1,0:T(8,128)S(1)}, u32[]{:S(2)}, u32[]{:S(2)}) collective-permute-start(f32[136,128]{1,0:T(8,128)S(1)} %get-tuple-element.17), channel_id=1, source_target_pairs={{0,2},{2,0},{4,6},{6,4},{8,10},{10,8},{12,14},{14,12},{16,18},{18,... | collective-permute-start | bytes 208904 | tf_op jit(solution)/shard_map/ppermute | solution.py:529
  59.6 4.6 %collective-permute-done.5 = f32[136,128]{1,0:T(8,128)S(1)} collective-permute-done((f32[136,128]{1,0:T(8,128)S(1)}, f32[136,128]{1,0:T(8,128)S(1)}, u32[]{:S(2)}, u32[]{:S(2)}) %collective-permute-start.5) | collective-permute-done | bytes 69664 | tf_op jit(solution)/shard_map/ppermute | solution.py:529
  64.2 1.9 %collective-permute-start.6 = (f32[136,128]{1,0:T(8,128)S(1)}, f32[136,128]{1,0:T(8,128)S(1)}, u32[]{:S(2)}, u32[]{:S(2)}) collective-permute-start(f32[136,128]{1,0:T(8,128)S(1)} %get-tuple-element.25), channel_id=1, source_target_pairs={{0,4},{2,6},{4,0},{6,2},{8,12},{10,14},{12,8},{14,10},{16,20},{18,... | collective-permute-start | bytes 208904 | tf_op jit(solution)/shard_map/ppermute | solution.py:529
  66.1 6.2 %collective-permute-done.6 = f32[136,128]{1,0:T(8,128)S(1)} collective-permute-done((f32[136,128]{1,0:T(8,128)S(1)}, f32[136,128]{1,0:T(8,128)S(1)}, u32[]{:S(2)}, u32[]{:S(2)}) %collective-permute-start.6) | collective-permute-done | bytes 69664 | tf_op jit(solution)/shard_map/ppermute | solution.py:529
  72.3 1.9 %collective-permute-start.7 = (f32[136,128]{1,0:T(8,128)S(1)}, f32[136,128]{1,0:T(8,128)S(1)}, u32[]{:S(2)}, u32[]{:S(2)}) collective-permute-start(f32[136,128]{1,0:T(8,128)S(1)} %get-tuple-element.23), channel_id=1, source_target_pairs={{0,8},{2,10},{4,12},{6,14},{8,0},{10,2},{12,4},{14,6},{16,24},{18,... | collective-permute-start | bytes 208904 | tf_op jit(solution)/shard_map/ppermute | solution.py:529
  74.3 8.2 %collective-permute-done.7 = f32[136,128]{1,0:T(8,128)S(1)} collective-permute-done((f32[136,128]{1,0:T(8,128)S(1)}, f32[136,128]{1,0:T(8,128)S(1)}, u32[]{:S(2)}, u32[]{:S(2)}) %collective-permute-start.7) | collective-permute-done | bytes 69664 | tf_op jit(solution)/shard_map/ppermute | solution.py:529
  82.5 1.9 %collective-permute-start.8 = (f32[136,128]{1,0:T(8,128)S(1)}, f32[136,128]{1,0:T(8,128)S(1)}, u32[]{:S(2)}, u32[]{:S(2)}) collective-permute-start(f32[136,128]{1,0:T(8,128)S(1)} %get-tuple-element.21), channel_id=1, source_target_pairs={{0,16},{2,18},{4,20},{6,22},{8,24},{10,26},{12,28},{14,30},{16,0},... | collective-permute-start | bytes 208904 | tf_op jit(solution)/shard_map/ppermute | solution.py:529
  84.4 4.3 %collective-permute-done.8 = f32[136,128]{1,0:T(8,128)S(1)} collective-permute-done((f32[136,128]{1,0:T(8,128)S(1)}, f32[136,128]{1,0:T(8,128)S(1)}, u32[]{:S(2)}, u32[]{:S(2)}) %collective-permute-start.8) | collective-permute-done | bytes 69664 | tf_op jit(solution)/shard_map/ppermute | solution.py:529
  88.7 2.1 %collective-permute-start.9 = (f32[680,128]{1,0:T(8,128)S(1)}, f32[680,128]{1,0:T(8,128)S(1)}, u32[]{:S(2)}, u32[]{:S(2)}) collective-permute-start(f32[680,128]{1,0:T(8,128)S(1)} %add_dynamic-update-slice_fusion.mine), channel_id=1, source_target_pairs={{0,1},{1,0},{2,3},{3,2},{4,5},{5,4},{6,7},{7,6},{8,9},{9,8},{10,11... | collective-permute-start | bytes 1044488 | tf_op jit(solution)/shard_map/ppermute | solution.py:533
  90.8 1.4 %collective-permute-done.9.theirs = f32[680,128]{1,0:T(8,128)S(1)} collective-permute-done((f32[680,128]{1,0:T(8,128)S(1)}, f32[680,128]{1,0:T(8,128)S(1)}, u32[]{:S(2)}, u32[]{:S(2)}) %collective-permute-start.9) | collective-permute-done | bytes 348192 | tf_op jit(solution)/shard_map/ppermute | solution.py:533
  92.2 17.0 %shard_map.73 = (f32[4,256,128]{2,1,0:T(8,128)}, f32[3072,128]{1,0:T(8,128)}) custom-call(s32[1]{0:T(128)} %bitcast.me, f32[680,128]{1,0:T(8,128)S(1)} %add_dynamic-update-slice_fusion.mine, f32[680,128]{1,0:T(8,128)S(1)} %collective-permute-done.9.theirs, bf16[3072,128]{1,0:T(8,128)(2,1)S(1)} %get-tuple-element.15.high.own0, ...), custom_call_target="tpu_custom_call" | custom-call | tf_op jit(solution)/shard_map/pallas_call | solution.py:498
  (9 shorter events, 0.1 us)
Async XLA Ops:
  0.6 40.5 %collective-permute-start.3 = (bf16[128,3072]{1,0:T(8,128)(2,1)}, bf16[128,3072]{1,0:T(8,128)(2,1)S(1)}, u32[]{:S(2)}, u32[]{:S(2)}) collective-permute-start(bf16[128,3072]{1,0:T(8,128)(2,1)} %probes.1), channel_id=1, source_target_pairs={{2,0},{4,2},{6,4},{8,6},{10,8},{12,10},{14,12},{16,14},{18,16},{20... | collective-permute-start | bytes 2359304 | tf_op jit(solution)/shard_map/ppermute | solution.py:525
  14.8 26.4 %collective-permute-start.2 = (bf16[128,3072]{1,0:T(8,128)(2,1)}, bf16[128,3072]{1,0:T(8,128)(2,1)S(1)}, u32[]{:S(2)}, u32[]{:S(2)}) collective-permute-start(bf16[128,3072]{1,0:T(8,128)(2,1)} %probes.1), channel_id=1, source_target_pairs={{0,2},{2,4},{4,6},{6,8},{8,10},{10,12},{12,14},{14,16},{16,18},{18... | collective-permute-start | bytes 2359304 | tf_op jit(solution)/shard_map/ppermute | solution.py:525
  16.7 0.8 copy-start.1
  17.5 0.7 copy-start.2
  20.4 20.6 %collective-permute-start.1 = (bf16[8,3072]{1,0:T(8,128)(2,1)S(1)}, bf16[8,3072]{1,0:T(8,128)(2,1)S(1)}, u32[]{:S(2)}, u32[]{:S(2)}) collective-permute-start(bf16[8,3072]{1,0:T(8,128)(2,1)S(1)} %shard_map.68.feat), channel_id=1, source_target_pairs={{2,0},{4,2},{6,4},{8,6},{10,8},{12,10},{14,12},{16,14},{18,16},{20... | collective-permute-start | bytes 147464 | tf_op jit(solution)/shard_map/ppermute | solution.py:525
  28.5 12.6 %collective-permute-start = (bf16[8,3072]{1,0:T(8,128)(2,1)S(1)}, bf16[8,3072]{1,0:T(8,128)(2,1)S(1)}, u32[]{:S(2)}, u32[]{:S(2)}) collective-permute-start(bf16[8,3072]{1,0:T(8,128)(2,1)S(1)} %shard_map.68.feat), channel_id=1, source_target_pairs={{0,2},{2,4},{4,6},{6,8},{8,10},{10,12},{12,14},{14,16},{16,18},{18... | collective-permute-start | bytes 147464 | tf_op jit(solution)/shard_map/ppermute | solution.py:525
  30.5 1.1 %copy-start = (bf16[128,3072]{1,0:T(8,128)(2,1)S(1)}, bf16[128,3072]{1,0:T(8,128)(2,1)}, u32[]{:S(2)}) copy-start(bf16[128,3072]{1,0:T(8,128)(2,1)} %probes.1) | copy-start | bytes 2359300
  31.6 0.7 copy-start.3
  32.3 0.7 copy-start.4
  51.3 5.3 %collective-permute-start.4 = (f32[3072,128]{1,0:T(8,128)S(1)}, f32[3072,128]{1,0:T(8,128)S(1)}, u32[]{:S(2)}, u32[]{:S(2)}) collective-permute-start(f32[3072,128]{1,0:T(8,128)S(1)} %shard_map.70.own), channel_id=1, source_target_pairs={{0,1},{1,0},{2,3},{3,2},{4,5},{5,4},{6,7},{7,6},{8,9},{9,8},{10,11... | collective-permute-start | bytes 4718600 | tf_op jit(solution)/shard_map/ppermute | solution.py:533
  57.6 6.6 %collective-permute-start.5 = (f32[136,128]{1,0:T(8,128)S(1)}, f32[136,128]{1,0:T(8,128)S(1)}, u32[]{:S(2)}, u32[]{:S(2)}) collective-permute-start(f32[136,128]{1,0:T(8,128)S(1)} %get-tuple-element.17), channel_id=1, source_target_pairs={{0,2},{2,0},{4,6},{6,4},{8,10},{10,8},{12,14},{14,12},{16,18},{18,... | collective-permute-start | bytes 208904 | tf_op jit(solution)/shard_map/ppermute | solution.py:529
  64.2 8.1 %collective-permute-start.6 = (f32[136,128]{1,0:T(8,128)S(1)}, f32[136,128]{1,0:T(8,128)S(1)}, u32[]{:S(2)}, u32[]{:S(2)}) collective-permute-start(f32[136,128]{1,0:T(8,128)S(1)} %get-tuple-element.25), channel_id=1, source_target_pairs={{0,4},{2,6},{4,0},{6,2},{8,12},{10,14},{12,8},{14,10},{16,20},{18,... | collective-permute-start | bytes 208904 | tf_op jit(solution)/shard_map/ppermute | solution.py:529
  72.3 10.1 %collective-permute-start.7 = (f32[136,128]{1,0:T(8,128)S(1)}, f32[136,128]{1,0:T(8,128)S(1)}, u32[]{:S(2)}, u32[]{:S(2)}) collective-permute-start(f32[136,128]{1,0:T(8,128)S(1)} %get-tuple-element.23), channel_id=1, source_target_pairs={{0,8},{2,10},{4,12},{6,14},{8,0},{10,2},{12,4},{14,6},{16,24},{18,... | collective-permute-start | bytes 208904 | tf_op jit(solution)/shard_map/ppermute | solution.py:529
  82.5 6.2 %collective-permute-start.8 = (f32[136,128]{1,0:T(8,128)S(1)}, f32[136,128]{1,0:T(8,128)S(1)}, u32[]{:S(2)}, u32[]{:S(2)}) collective-permute-start(f32[136,128]{1,0:T(8,128)S(1)} %get-tuple-element.21), channel_id=1, source_target_pairs={{0,16},{2,18},{4,20},{6,22},{8,24},{10,26},{12,28},{14,30},{16,0},... | collective-permute-start | bytes 208904 | tf_op jit(solution)/shard_map/ppermute | solution.py:529
  88.7 3.6 %collective-permute-start.9 = (f32[680,128]{1,0:T(8,128)S(1)}, f32[680,128]{1,0:T(8,128)S(1)}, u32[]{:S(2)}, u32[]{:S(2)}) collective-permute-start(f32[680,128]{1,0:T(8,128)S(1)} %add_dynamic-update-slice_fusion.mine), channel_id=1, source_target_pairs={{0,1},{1,0},{2,3},{3,2},{4,5},{5,4},{6,7},{7,6},{8,9},{9,8},{10,11... | collective-permute-start | bytes 1044488 | tf_op jit(solution)/shard_map/ppermute | solution.py:533

commit v4 on v3

--- a/solution.py
+++ b/solution.py
@@ -52,15 +52,27 @@
     return hi, mid, rest - mid
 
 
-def order_kernel(feat, order, out):
+def in_hbm(array):
+    return pltpu.with_memory_space_constraint(array, pltpu.HBM)
+
+
+def order_kernel(feat_in, order_in, out, feat, order, sems):
+    copies = [
+        pltpu.make_async_copy(feat_in, feat, sems.at[0]),
+        pltpu.make_async_copy(order_in, order, sems.at[1]),
+    ]
+    for copy in copies:
+        copy.start()
+    for copy in copies:
+        copy.wait()
     chunks = feat.shape[1] // LANES
     pieces = [feat[:, c * LANES : (c + 1) * LANES].astype(F32) for c in range(chunks)]
 
     def one(q, carry):
         at = pl.multiple_of(q * LANES, LANES)
-        index = jnp.broadcast_to(order[:, pl.ds(at, LANES)], (ROWS, LANES))
+        index = jnp.broadcast_to(order[:, pl.ds(at, LANES)], TILE)
         low, high = index & (LANES - 1), index >> 7
-        total = jnp.zeros((ROWS, LANES), F32)
+        total = jnp.zeros(TILE, F32)
         for c in range(chunks):
             total = jnp.where(high == c, jnp.take_along_axis(pieces[c], low, axis=1), total)
         out[:, pl.ds(at, LANES)] = total.astype(BF16)
@@ -70,7 +82,18 @@
 
 
 def order_features(features, leaf_order):
-    return call(order_kernel, jax.ShapeDtypeStruct(features.shape, BF16))(features, leaf_order)
+    anywhere = pl.BlockSpec(memory_space=pltpu.HBM)
+    return call(
+        order_kernel,
+        jax.ShapeDtypeStruct(features.shape, BF16),
+        in_specs=[anywhere] * 2,
+        out_specs=pl.BlockSpec(memory_space=pltpu.VMEM),
+        scratch_shapes=[
+            pltpu.VMEM(features.shape, BF16),
+            pltpu.VMEM(leaf_order.shape, jnp.int32),
+            pltpu.SemaphoreType.DMA((2,)),
+        ],
+    )(in_hbm(features), in_hbm(leaf_order))
 
 
 SHIFT = 6
@@ -96,22 +119,19 @@
 
 def weights(scale):
     count = scale.shape[0]
-    row = lax.broadcasted_iota(jnp.int32, (count, 1), 0)
-    held = jnp.full((count, 1), scale[0], F32)
+    row = lax.broadcasted_iota(jnp.int32, (count, LANES), 0)
+    held = jnp.full((count, LANES), scale[0], F32)
     for f in range(1, count):
         held = jnp.where(row == f, scale[f], held)
     return (3.0 * LOG2_E * LOG2_E) / (held * held)
 
 
-def load_columns(cols, panel, feats, probes, weight, blocks):
-    leaf = feats[0].shape[1]
-    block = leaf // blocks
-    for n, (feat, probe) in enumerate(zip(feats, probes)):
+def load_columns(cols, panel, feats, weight, blocks):
+    block = feats[0].shape[1] // blocks
+    for n, feat in enumerate(feats):
         pieces = column_pieces(feat[...].astype(F32), weight)
         for b in range(blocks):
-            span = slice(b * block, (b + 1) * block)
-            cols[n * blocks + b] = pieces[:, span]
-            panel[n * blocks + b] = probe[:, span]
+            cols[n * blocks + b] = pieces[:, b * block : (b + 1) * block]
     last = len(feats) * blocks
     cols[last] = jnp.zeros(cols.shape[1:], BF16)
     panel[last] = jnp.zeros(panel.shape[1:], BF16)
@@ -150,9 +170,22 @@
         out[to, :] += part
 
 
-def near_kernel(near_blocks, first, scale, feat, probes, out, rows_t, far, tasks, cols, panel, k0, k1):
+def near_kernel(
+    first, listed_in, scale_in, feat, probes, out, rows_t, far, weight_out,
+    near_blocks, scale, tasks, cols, panel, k0, k1, sems,
+):
     blocks, near = near_blocks.shape
     block = feat.shape[1] // blocks
+    copies = [
+        pltpu.make_async_copy(listed_in, near_blocks, sems.at[0]),
+        pltpu.make_async_copy(scale_in, scale, sems.at[1]),
+    ]
+    for b in range(blocks):
+        source = probes.at[:, b * block : (b + 1) * block]
+        copies.append(pltpu.make_async_copy(source, panel.at[b], sems.at[2 + b]))
+    for copy in copies:
+        copy.start()
+    copies[0].wait()
 
     def scan(a, counts):
         mine, rest = counts
@@ -172,9 +205,13 @@
         far[rest + u] = 3 * blocks
     far[SLOTS - 1] = rest
 
-    weight = weights(scale)
+    copies[1].wait()
+    weight_out[...] = weights(scale)
+    weight = weight_out[:, :1]
     rows_t[...] = row_pieces(feat[...].astype(F32), weight)
-    load_columns(cols, panel, [feat], [probes], weight, blocks)
+    load_columns(cols, panel, [feat], weight, blocks)
+    for copy in copies[2:]:
+        copy.wait()
     here = lax.broadcasted_iota(jnp.int32, (block, block), 0)
     there = lax.broadcasted_iota(jnp.int32, (block, block), 1)
     nugget = jnp.where(here == there, NUGGET, 0.0).astype(BF16)
@@ -188,31 +225,40 @@
     blocks = near_blocks.shape[0]
     block = leaf // blocks
     whole = pl.BlockSpec(memory_space=pltpu.VMEM)
+    anywhere = pl.BlockSpec(memory_space=pltpu.HBM)
     return call(
         near_kernel,
         (
             pltpu.VMEM((leaf, half), F32),
             pltpu.VMEM((leaf, 32), BF16),
             jax.ShapeDtypeStruct((SLOTS,), jnp.int32),
+            pltpu.VMEM((ROWS, LANES), F32),
         ),
         grid_spec=pltpu.PrefetchScalarGridSpec(
-            num_scalar_prefetch=3,
+            num_scalar_prefetch=1,
             grid=(1,),
-            in_specs=[whole] * 2,
-            out_specs=[whole, whole, pl.BlockSpec(memory_space=pltpu.SMEM)],
+            in_specs=[anywhere, anywhere, whole, anywhere],
+            out_specs=[whole, whole, pl.BlockSpec(memory_space=pltpu.SMEM), whole],
             scratch_shapes=[
+                pltpu.SMEM(near_blocks.shape, jnp.int32),
+                pltpu.SMEM(scale.shape, F32),
                 pltpu.SMEM((SLOTS,), jnp.int32),
                 pltpu.VMEM((blocks + 1, 32, block), BF16),
                 pltpu.VMEM((blocks + 1, half, block), BF16),
                 *[pltpu.VMEM((WIDE, block, block), BF16)] * 2,
+                pltpu.SemaphoreType.DMA((2 + blocks,)),
             ],
         ),
-    )(near_blocks, first, scale, feat, probes)
-
-
-def far_kernel(far, scale, part, rows_t, left, right, before, after, out, cols, panel, k0, k1):
+    )(first, in_hbm(near_blocks), in_hbm(scale), feat, in_hbm(probes))
+
+
+def far_kernel(far, weight, part, rows_t, left, right, before, after, out, cols, panel, k0, k1):
     blocks = (cols.shape[0] - 1) // 2
-    load_columns(cols, panel, [left, right], [before, after], weights(scale), blocks)
+    load_columns(cols, panel, [left, right], weight[:, :1], blocks)
+    block = cols.shape[2]
+    for n, probe in enumerate((before, after)):
+        for b in range(blocks):
+            panel[n * blocks + b] = probe[:, b * block : (b + 1) * block]
     out[...] = part[...]
     run_tasks(
         far,
@@ -226,7 +272,7 @@
     )
 
 
-def far_part(far, scale, part, rows_t, left, right, before, after, blocks):
+def far_part(far, weight, part, rows_t, left, right, before, after, blocks):
     half, leaf = before.shape
     block = leaf // blocks
     whole = pl.BlockSpec(memory_space=pltpu.VMEM)
@@ -234,9 +280,9 @@
         far_kernel,
         pltpu.VMEM((leaf, half), F32),
         grid_spec=pltpu.PrefetchScalarGridSpec(
-            num_scalar_prefetch=2,
+            num_scalar_prefetch=1,
             grid=(1,),
-            in_specs=[whole] * 6,
+            in_specs=[whole] * 7,
             out_specs=whole,
             scratch_shapes=[
                 pltpu.VMEM((2 * blocks + 1, 32, block), BF16),
@@ -244,7 +290,7 @@
                 *[pltpu.VMEM((WIDE, block, block), BF16)] * 2,
             ],
         ),
-    )(far, scale, part, rows_t, left, right, before, after)
+    )(far, weight, part, rows_t, left, right, before, after)
 
 
 HALF = LANES // 2
@@ -300,10 +346,11 @@
     )(own)
 
 
-def gram_kernel(me, block, high, low, other, out, high_o, low_o):
+def gram_kernel(me, block, high, low, other, out, highs, lows):
+    n = LANES
     b0, b1 = halves(other[...])
-    high_o[...] = b0
-    low_o[...] = b1
+    highs[:, :n], highs[:, n:] = high[...], b0
+    lows[:, :n], lows[:, n:] = low[...], b1
     out[:PACKED] = block[...]
 
     @pl.when(me[0] == 0)
@@ -322,8 +369,8 @@
         gram_kernel,
         (
             jax.ShapeDtypeStruct((PACKED + HALF, half), F32),
-            pltpu.VMEM((leaf, half), BF16),
-            pltpu.VMEM((leaf, half), BF16),
+            pltpu.VMEM((leaf, 2 * half), BF16),
+            pltpu.VMEM((leaf, 2 * half), BF16),
         ),
         grid_spec=pltpu.PrefetchScalarGridSpec(
             num_scalar_prefetch=1, grid=(1,), in_specs=[whole] * 4, out_specs=[whole] * 3
@@ -342,12 +389,12 @@
     ]
 
 
-def outer_sum(a, b):
+def outer_pieces(a, b):
     a0, a1, a2 = thirds(a)
     b0, b1, b2 = thirds(b)
     left = jnp.concatenate([a0, a0, a1, a0, a1, a2], 0).astype(BF16)
     right = jnp.concatenate([b0, b1, b0, b2, b1, b0], 0).astype(BF16)
-    return dot16(left, right, 0, 0)
+    return left, right
 
 
 def eliminate(panels, nexts, at):
@@ -383,40 +430,36 @@
 def factor_block(work, ups, invs, base):
     count = range(work.shape[0])
     lane = lax.broadcasted_iota(jnp.int32, TILE, 1)
-    lane_all = lax.broadcasted_iota(jnp.int32, (LANES, LANES), 1)
     span = slice(base, base + LANES)
     pair = 2 * ROWS
-
-    def step(j, carry):
-        at = pl.multiple_of(j * pair, pair)
+    for at in range(0, LANES, pair):
         mid, end = at + ROWS, at + pair
-        both = [work[l, pl.ds(at, pair), :] for l in count]
+        both = [work[l, at:end, :] for l in count]
         first, low_first, second = eliminate(
             [b[:ROWS] for b in both], [b[ROWS:] for b in both], at
         )
         second, low_second, _ = eliminate(second, [], mid)
+        for l in count:
+            for x, low, p in ((first, low_first, at), (second, low_second, mid)):
+                to = slice(base + p, base + p + ROWS)
+                ups[l, to, span] = jnp.where(lane >= p + ROWS, x[l], low[l])
+                invs[l, to, span] = jnp.where(lane < p + ROWS, x[l], 0.0)
+        if end == LANES:
+            break
         lefts, rights = [], []
         for l in count:
-            lefts.append(
-                jnp.concatenate([jnp.where(lane >= end, x[l], 0.0) for x in (first, second)], 0)
-            )
+            lefts.append(jnp.concatenate([first[l], second[l]], 0))
             rights.append(
                 jnp.concatenate(
                     [jnp.where((lane >= mid) & (lane < end), 0.0, first[l]), second[l]], 0
                 )
             )
-        sums = [outer_sum(lefts[l], rights[l]) for l in count]
-        gone = (lane_all >= at) & (lane_all < end)
-        rests = [jnp.where(gone, 0.0, work[l]) - sums[l] for l in count]
+        pieces = [outer_pieces(lefts[l], rights[l]) for l in count]
+        col = lax.broadcasted_iota(jnp.int32, (LANES - end, LANES), 1)
+        gone = (col >= at) & (col < end)
+        sums = [dot16(pieces[l][0][:, end:], pieces[l][1], 0, 0) for l in count]
         for l in count:
-            for x, low, p in ((first, low_first, at), (second, low_second, mid)):
-                to = pl.ds(pl.multiple_of(base + p, ROWS), ROWS)
-                ups[l, to, span] = jnp.where(lane >= p + ROWS, x[l], low[l])
-                invs[l, to, span] = jnp.where(lane < p + ROWS, x[l], 0.0)
-            work[l] = rests[l]
-        return carry
-
-    lax.fori_loop(0, LANES // pair, step, 0)
+            work[l, end:, :] = jnp.where(gone, 0.0, work[l, end:, :]) - sums[l]
 
 
 def straighten(ups, l, base):
@@ -451,7 +494,9 @@
         straighten(ups, l, n)
 
 
-def factor_kernel(me, mine, theirs, own0, own1, other0, other1, transfer, basis, pieces, work, ups, invs, moved, rows, sems):
+def factor_kernel(
+    me, mine, theirs, highs, lows, transfer, basis, pieces, work, ups, invs, moved, rows, sems
+):
     n = LANES
     height = PACKED + HALF
     pieces[me[0]] = mine[...]
@@ -467,18 +512,16 @@
     factor(gram, work, ups, invs)
     cols = pl.ds(pl.multiple_of(me[0] * n, n), n)
     rest = pl.ds(pl.multiple_of((1 - me[0]) * n, n), n)
-    scale = math.sqrt(2**LEVELS * own0.shape[0])
+    scale = math.sqrt(2**LEVELS * highs.shape[0])
     weight = invs.at[LEVELS]
-    near0, near1 = halves(weight[cols, cols] * scale)
-    far0, far1 = halves(weight[cols, rest] * scale)
+    high, low = halves(jnp.concatenate([weight[cols, cols], weight[cols, rest]], 1) * scale)
+    both = jnp.concatenate([high, low], 0)
     steps, size, _ = rows.shape
     copies = []
     for s in range(steps):
         at = slice(s * size, (s + 1) * size)
-        a0, a1, b0, b1 = own0[at, :], own1[at, :], other0[at, :], other1[at, :]
-        small = dot16(a0, near1, 1, 1) + dot16(a1, near0, 1, 1)
-        small += dot16(b0, far1, 1, 1) + dot16(b1, far0, 1, 1)
-        rows[s] = small + (dot16(a0, near0, 1, 1) + dot16(b0, far0, 1, 1))
+        two = dot16(highs[at, :], both, 1, 1)
+        rows[s] = two[:, :n] + (two[:, n:] + dot16(lows[at, :], high, 1, 1))
         copies.append(pltpu.make_async_copy(rows.at[s], basis.at[pl.ds(s * size, size)], sems.at[s]))
         copies[-1].start()
     for l in range(LEVELS):
@@ -489,10 +532,10 @@
         copy.wait()
 
 
-def factors(me, mine, theirs, own, other):
+def factors(me, mine, theirs, highs, lows):
     n = 2 * LANES
     count = LEVELS + 1
-    leaf, half = own[0].shape
+    leaf, half = highs.shape[0], LANES
     steps = 6
     whole = pl.BlockSpec(memory_space=pltpu.VMEM)
     return call(
@@ -504,7 +547,7 @@
         grid_spec=pltpu.PrefetchScalarGridSpec(
             num_scalar_prefetch=1,
             grid=(1,),
-            in_specs=[whole] * 6,
+            in_specs=[whole] * 4,
             out_specs=[pl.BlockSpec(memory_space=pl.ANY)] * 2,
             scratch_shapes=[
                 pltpu.VMEM((2, *mine.shape), F32),
@@ -516,7 +559,7 @@
                 pltpu.SemaphoreType.DMA((steps + LEVELS,)),
             ],
         ),
-    )(me, mine, theirs, *own, *other)
+    )(me, mine, theirs, highs, lows)
 
 
 def beside(array, shift):
@@ -542,19 +585,19 @@
     ordered = order_features(features, leaf_order)
     before = beside(ordered, 1)
     after = beside(ordered, -1)
-    part, rows_t, far = near_part(near_blocks, first, lengthscale, ordered, probes)
+    part, rows_t, far, weight = near_part(near_blocks, first, lengthscale, ordered, probes)
     own = far_part(
-        far, lengthscale, part, rows_t, before, after, probes_before, probes_after, blocks
+        far, weight, part, rows_t, before, after, probes_before, probes_after, blocks
     )
     other = other_core(own)
-    block, *own_pieces = own_gram(own)
-    gram, *other_pieces = gram_blocks(me, block, *own_pieces, other)
+    block, high, low = own_gram(own)
+    gram, highs, lows = gram_blocks(me, block, high, low, other)
     grams = [gram]
     for depth in range(LEVELS):
         gram = gram + sibling(gram, depth)
         grams.append(gram)
     mine = jnp.concatenate(grams, 0)
-    return factors(me, mine, other_core(mine), own_pieces, other_pieces)
+    return factors(me, mine, other_core(mine), highs, lows)
 
 
 def solution(mesh):

time: 110 us -> 110 us (level)
  local copies, waits for them, and re-layouts: 3.98 us -> 0.01 us
  waiting for transfers between devices: 27.4 us -> 30 us
    unnamed x11 -> x1, local copies, waits for them, and re-layouts: 3.98 us -> 0.01 us
    ppermute x4, waiting for transfers between devices: 0.2 us -> 2.86 us  [beside(): return lax.ppermute(array, 'leaf', pairs)]
    pallas_call x1, Pallas kernels: 17 us -> 15.6 us  [factors(): call(factor_kernel, (jax.ShapeDtypeStruct((LEVELS, n, half), F32), jax.Sh...]
  transfers between devices with their start and end apart: 10 -> 10, of which waited for: 7 -> 7; matrix products, arithmetic and copies ran while one was open for 0% -> 0% of each run, Pallas kernels for 10% -> 11%
where the time goes in v4:
time: 110 us; the launch traced here: 108 us
  Pallas kernels  39.6 us (36%)
  starting transfers between devices  37.8 us (34%)
  waiting for transfers between devices  30 us (27%)
    ppermute x4, starting transfers between devices, beside(): return lax.ppermute(array, 'leaf', pairs)  26.1 us
    ppermute x4, waiting for transfers between devices, sibling(): lax.ppermute(array, 'leaf', [(i, i ^ 1 << bit) for i in range(lax.axis_si...  23.3 us
    pallas_call x1, Pallas kernels, factors(): call(factor_kernel, (jax.ShapeDtypeStruct((LEVELS, n, half), F32), jax.Sh...  15.6 us
    pallas_call x1, Pallas kernels, far_part(): call(far_kernel, pltpu.VMEM((leaf, half), F32), grid_spec=pltpu.PrefetchS...  10.2 us
    pallas_call x1, Pallas kernels, near_part(): call(near_kernel, (pltpu.VMEM((leaf, half), F32), pltpu.VMEM((leaf, 32),...  8.5 us
    ppermute x4, starting transfers between devices, sibling(): lax.ppermute(array, 'leaf', [(i, i ^ 1 << bit) for i in range(lax.axis_si...  7.68 us
    ppermute x2, starting transfers between devices, other_core(): return lax.ppermute(array, 'probe', [(0, 1), (1, 0)])  4.02 us
    ppermute x2, waiting for transfers between devices, other_core(): return lax.ppermute(array, 'probe', [(0, 1), (1, 0)])  3.91 us
  transfers between devices with their start and end apart: 10, of which 7 were waited for; matrix products, arithmetic and copies ran while one was open for 0% of the time, Pallas kernels for 11%

profile of v4, /device:TPU:6, one launch (start us, length us, event | category | flops | bytes accessed | tf_op | source)
XLA Modules:
  0.0 108.4 jit_solution(17052604503965194518)
XLA Ops:
  0.6 14.1 %collective-permute-start.3 = (bf16[128,3072]{1,0:T(8,128)(2,1)}, bf16[128,3072]{1,0:T(8,128)(2,1)S(1)}, u32[]{:S(2)}, u32[]{:S(2)}) collective-permute-start(bf16[128,3072]{1,0:T(8,128)(2,1)} %probes.1), channel_id=1, source_target_pairs={{2,0},{4,2},{6,4},{8,6},{10,8},{12,10},{14,12},{16,14},{18,16},{20... | collective-permute-start | bytes 2359304 | tf_op jit(solution)/shard_map/ppermute | solution.py:568
  14.8 1.9 %collective-permute-start.2 = (bf16[128,3072]{1,0:T(8,128)(2,1)}, bf16[128,3072]{1,0:T(8,128)(2,1)S(1)}, u32[]{:S(2)}, u32[]{:S(2)}) collective-permute-start(bf16[128,3072]{1,0:T(8,128)(2,1)} %probes.1), channel_id=1, source_target_pairs={{0,2},{2,4},{4,6},{6,8},{8,10},{10,12},{12,14},{14,16},{16,18},{18... | collective-permute-start | bytes 2359304 | tf_op jit(solution)/shard_map/ppermute | solution.py:568
  16.7 3.0 %shard_map.68.feat = bf16[8,3072]{1,0:T(8,128)(2,1)S(1)} custom-call(bf16[8,3072]{1,0:T(8,128)(2,1)} %feat_in.1, s32[1,3072]{1,0:T(1,128)} %order_in.1), custom_call_target="tpu_custom_call" | custom-call | tf_op jit(solution)/shard_map/pallas_call | solution.py:86
  19.7 8.1 %collective-permute-start.1 = (bf16[8,3072]{1,0:T(8,128)(2,1)S(1)}, bf16[8,3072]{1,0:T(8,128)(2,1)S(1)}, u32[]{:S(2)}, u32[]{:S(2)}) collective-permute-start(bf16[8,3072]{1,0:T(8,128)(2,1)S(1)} %shard_map.68.feat), channel_id=1, source_target_pairs={{2,0},{4,2},{6,4},{8,6},{10,8},{12,10},{14,12},{16,14},{18,16},{20... | collective-permute-start | bytes 147464 | tf_op jit(solution)/shard_map/ppermute | solution.py:568
  27.8 1.9 %collective-permute-start = (bf16[8,3072]{1,0:T(8,128)(2,1)S(1)}, bf16[8,3072]{1,0:T(8,128)(2,1)S(1)}, u32[]{:S(2)}, u32[]{:S(2)}) collective-permute-start(bf16[8,3072]{1,0:T(8,128)(2,1)S(1)} %shard_map.68.feat), channel_id=1, source_target_pairs={{0,2},{2,4},{4,6},{6,8},{8,10},{10,12},{12,14},{14,16},{16,18},{18... | collective-permute-start | bytes 147464 | tf_op jit(solution)/shard_map/ppermute | solution.py:568
  29.8 8.5 %shard_map.69 = (f32[3072,128]{1,0:T(8,128)S(1)}, bf16[3072,32]{1,0:T(8,128)(2,1)S(1)}, s32[160]{0:T(256)S(1)}, f32[8,128]{1,0:T(8,128)S(1)}) custom-call(s32[1]{0:T(128)} %bitcast.1.first, s32[12,10]{1,0:T(8,128)} %listed_in.1, f32[8]{0:T(128)} %scale_in.1, bf16[8,3072]{1,0:T(8,128)(2,1)S(1)} %shard_map.68.feat, bf16[128,3072]{1,0:T(8,128)(2,1)} %probes.1), custom_call_target="tpu_custom_call" | custom-call | tf_op jit(solution)/shard_map/pallas_call | solution.py:229
  38.3 0.0 collective-permute-done.1.right
  38.3 2.8 %collective-permute-done.left = bf16[8,3072]{1,0:T(8,128)(2,1)S(1)} collective-permute-done((bf16[8,3072]{1,0:T(8,128)(2,1)S(1)}, bf16[8,3072]{1,0:T(8,128)(2,1)S(1)}, u32[]{:S(2)}, u32[]{:S(2)}) %collective-permute-start) | collective-permute-done | bytes 49184 | tf_op jit(solution)/shard_map/ppermute | solution.py:568
  41.1 0.0 collective-permute-done.3.after
  41.1 0.0 collective-permute-done.2.before
  41.1 10.2 %shard_map.70.own = f32[3072,128]{1,0:T(8,128)S(1)} custom-call(s32[160]{0:T(256)S(1)} %get-tuple-element.12.far, f32[8,128]{1,0:T(8,128)S(1)} %get-tuple-element.13.weight, f32[3072,128]{1,0:T(8,128)S(1)} %get-tuple-element.14.part, bf16[3072,32]{1,0:T(8,128)(2,1)S(1)} %get-tuple-element.15.rows_t, bf16[8,3072]{1,0:T(8,128)(2,1)S(1)} %collective-permute-done.left, ...), custom_call_target="tpu_custom_call" | custom-call | tf_op jit(solution)/shard_map/pallas_call | solution.py:279
  51.4 1.9 %collective-permute-start.4 = (f32[3072,128]{1,0:T(8,128)S(1)}, f32[3072,128]{1,0:T(8,128)S(1)}, u32[]{:S(2)}, u32[]{:S(2)}) collective-permute-start(f32[3072,128]{1,0:T(8,128)S(1)} %shard_map.70.own), channel_id=1, source_target_pairs={{0,1},{1,0},{2,3},{3,2},{4,5},{5,4},{6,7},{7,6},{8,9},{9,8},{10,11... | collective-permute-start | bytes 4718600 | tf_op jit(solution)/shard_map/ppermute | solution.py:576
  53.3 0.9 shard_map.71
  54.2 2.5 %collective-permute-done.4.other = f32[3072,128]{1,0:T(8,128)S(1)} collective-permute-done((f32[3072,128]{1,0:T(8,128)S(1)}, f32[3072,128]{1,0:T(8,128)S(1)}, u32[]{:S(2)}, u32[]{:S(2)}) %collective-permute-start.4) | collective-permute-done | bytes 1572896 | tf_op jit(solution)/shard_map/ppermute | solution.py:576
  56.7 1.3 %shard_map.72 = (f32[136,128]{1,0:T(8,128)S(1)}, bf16[3072,256]{1,0:T(8,128)(2,1)S(1)}, bf16[3072,256]{1,0:T(8,128)(2,1)S(1)}) custom-call(s32[1]{0:T(128)} %bitcast.me, f32[72,128]{1,0:T(8,128)S(1)} %get-tuple-element.16.block, bf16[3072,128]{1,0:T(8,128)(2,1)S(1)} %get-tuple-element.17.high, bf16[3072,128]{1,0:T(8,128)(2,1)S(1)} %get-tuple-element.18.low, ...), custom_call_target="tpu_custom_call" | custom-call | tf_op jit(solution)/shard_map/pallas_call | solution.py:368
  58.0 1.9 %collective-permute-start.5 = (f32[136,128]{1,0:T(8,128)S(1)}, f32[136,128]{1,0:T(8,128)S(1)}, u32[]{:S(2)}, u32[]{:S(2)}) collective-permute-start(f32[136,128]{1,0:T(8,128)S(1)} %get-tuple-element.19), channel_id=1, source_target_pairs={{0,2},{2,0},{4,6},{6,4},{8,10},{10,8},{12,14},{14,12},{16,18},{18,... | collective-permute-start | bytes 208904 | tf_op jit(solution)/shard_map/ppermute | solution.py:572
  60.0 4.6 %collective-permute-done.5 = f32[136,128]{1,0:T(8,128)S(1)} collective-permute-done((f32[136,128]{1,0:T(8,128)S(1)}, f32[136,128]{1,0:T(8,128)S(1)}, u32[]{:S(2)}, u32[]{:S(2)}) %collective-permute-start.5) | collective-permute-done | bytes 69664 | tf_op jit(solution)/shard_map/ppermute | solution.py:572
  64.6 1.9 %collective-permute-start.6 = (f32[136,128]{1,0:T(8,128)S(1)}, f32[136,128]{1,0:T(8,128)S(1)}, u32[]{:S(2)}, u32[]{:S(2)}) collective-permute-start(f32[136,128]{1,0:T(8,128)S(1)} %get-tuple-element.27), channel_id=1, source_target_pairs={{0,4},{2,6},{4,0},{6,2},{8,12},{10,14},{12,8},{14,10},{16,20},{18,... | collective-permute-start | bytes 208904 | tf_op jit(solution)/shard_map/ppermute | solution.py:572
  66.5 6.2 %collective-permute-done.6 = f32[136,128]{1,0:T(8,128)S(1)} collective-permute-done((f32[136,128]{1,0:T(8,128)S(1)}, f32[136,128]{1,0:T(8,128)S(1)}, u32[]{:S(2)}, u32[]{:S(2)}) %collective-permute-start.6) | collective-permute-done | bytes 69664 | tf_op jit(solution)/shard_map/ppermute | solution.py:572
  72.7 1.9 %collective-permute-start.7 = (f32[136,128]{1,0:T(8,128)S(1)}, f32[136,128]{1,0:T(8,128)S(1)}, u32[]{:S(2)}, u32[]{:S(2)}) collective-permute-start(f32[136,128]{1,0:T(8,128)S(1)} %get-tuple-element.25), channel_id=1, source_target_pairs={{0,8},{2,10},{4,12},{6,14},{8,0},{10,2},{12,4},{14,6},{16,24},{18,... | collective-permute-start | bytes 208904 | tf_op jit(solution)/shard_map/ppermute | solution.py:572
  74.7 8.2 %collective-permute-done.7 = f32[136,128]{1,0:T(8,128)S(1)} collective-permute-done((f32[136,128]{1,0:T(8,128)S(1)}, f32[136,128]{1,0:T(8,128)S(1)}, u32[]{:S(2)}, u32[]{:S(2)}) %collective-permute-start.7) | collective-permute-done | bytes 69664 | tf_op jit(solution)/shard_map/ppermute | solution.py:572
  82.9 1.9 %collective-permute-start.8 = (f32[136,128]{1,0:T(8,128)S(1)}, f32[136,128]{1,0:T(8,128)S(1)}, u32[]{:S(2)}, u32[]{:S(2)}) collective-permute-start(f32[136,128]{1,0:T(8,128)S(1)} %get-tuple-element.23), channel_id=1, source_target_pairs={{0,16},{2,18},{4,20},{6,22},{8,24},{10,26},{12,28},{14,30},{16,0},... | collective-permute-start | bytes 208904 | tf_op jit(solution)/shard_map/ppermute | solution.py:572
  84.8 4.3 %collective-permute-done.8 = f32[136,128]{1,0:T(8,128)S(1)} collective-permute-done((f32[136,128]{1,0:T(8,128)S(1)}, f32[136,128]{1,0:T(8,128)S(1)}, u32[]{:S(2)}, u32[]{:S(2)}) %collective-permute-start.8) | collective-permute-done | bytes 69664 | tf_op jit(solution)/shard_map/ppermute | solution.py:572
  89.1 2.1 %collective-permute-start.9 = (f32[680,128]{1,0:T(8,128)S(1)}, f32[680,128]{1,0:T(8,128)S(1)}, u32[]{:S(2)}, u32[]{:S(2)}) collective-permute-start(f32[680,128]{1,0:T(8,128)S(1)} %add_dynamic-update-slice_fusion.mine), channel_id=1, source_target_pairs={{0,1},{1,0},{2,3},{3,2},{4,5},{5,4},{6,7},{7,6},{8,9},{9,8},{10,11... | collective-permute-start | bytes 1044488 | tf_op jit(solution)/shard_map/ppermute | solution.py:576
  91.2 1.4 %collective-permute-done.9.theirs = f32[680,128]{1,0:T(8,128)S(1)} collective-permute-done((f32[680,128]{1,0:T(8,128)S(1)}, f32[680,128]{1,0:T(8,128)S(1)}, u32[]{:S(2)}, u32[]{:S(2)}) %collective-permute-start.9) | collective-permute-done | bytes 348192 | tf_op jit(solution)/shard_map/ppermute | solution.py:576
  92.6 15.6 %shard_map.73 = (f32[4,256,128]{2,1,0:T(8,128)}, f32[3072,128]{1,0:T(8,128)}) custom-call(s32[1]{0:T(128)} %bitcast.me, f32[680,128]{1,0:T(8,128)S(1)} %add_dynamic-update-slice_fusion.mine, f32[680,128]{1,0:T(8,128)S(1)} %collective-permute-done.9.theirs, bf16[3072,256]{1,0:T(8,128)(2,1)S(1)} %get-tuple-element.20.highs, ...), custom_call_target="tpu_custom_call" | custom-call | tf_op jit(solution)/shard_map/pallas_call | solution.py:541
  (5 shorter events, 0.1 us)
Async XLA Ops:
  0.6 40.5 %collective-permute-start.3 = (bf16[128,3072]{1,0:T(8,128)(2,1)}, bf16[128,3072]{1,0:T(8,128)(2,1)S(1)}, u32[]{:S(2)}, u32[]{:S(2)}) collective-permute-start(bf16[128,3072]{1,0:T(8,128)(2,1)} %probes.1), channel_id=1, source_target_pairs={{2,0},{4,2},{6,4},{8,6},{10,8},{12,10},{14,12},{16,14},{18,16},{20... | collective-permute-start | bytes 2359304 | tf_op jit(solution)/shard_map/ppermute | solution.py:568
  14.8 26.4 %collective-permute-start.2 = (bf16[128,3072]{1,0:T(8,128)(2,1)}, bf16[128,3072]{1,0:T(8,128)(2,1)S(1)}, u32[]{:S(2)}, u32[]{:S(2)}) collective-permute-start(bf16[128,3072]{1,0:T(8,128)(2,1)} %probes.1), channel_id=1, source_target_pairs={{0,2},{2,4},{4,6},{6,8},{8,10},{10,12},{12,14},{14,16},{16,18},{18... | collective-permute-start | bytes 2359304 | tf_op jit(solution)/shard_map/ppermute | solution.py:568
  19.7 18.6 %collective-permute-start.1 = (bf16[8,3072]{1,0:T(8,128)(2,1)S(1)}, bf16[8,3072]{1,0:T(8,128)(2,1)S(1)}, u32[]{:S(2)}, u32[]{:S(2)}) collective-permute-start(bf16[8,3072]{1,0:T(8,128)(2,1)S(1)} %shard_map.68.feat), channel_id=1, source_target_pairs={{2,0},{4,2},{6,4},{8,6},{10,8},{12,10},{14,12},{16,14},{18,16},{20... | collective-permute-start | bytes 147464 | tf_op jit(solution)/shard_map/ppermute | solution.py:568
  27.8 13.3 %collective-permute-start = (bf16[8,3072]{1,0:T(8,128)(2,1)S(1)}, bf16[8,3072]{1,0:T(8,128)(2,1)S(1)}, u32[]{:S(2)}, u32[]{:S(2)}) collective-permute-start(bf16[8,3072]{1,0:T(8,128)(2,1)S(1)} %shard_map.68.feat), channel_id=1, source_target_pairs={{0,2},{2,4},{4,6},{6,8},{8,10},{10,12},{12,14},{14,16},{16,18},{18... | collective-permute-start | bytes 147464 | tf_op jit(solution)/shard_map/ppermute | solution.py:568
  51.4 5.3 %collective-permute-start.4 = (f32[3072,128]{1,0:T(8,128)S(1)}, f32[3072,128]{1,0:T(8,128)S(1)}, u32[]{:S(2)}, u32[]{:S(2)}) collective-permute-start(f32[3072,128]{1,0:T(8,128)S(1)} %shard_map.70.own), channel_id=1, source_target_pairs={{0,1},{1,0},{2,3},{3,2},{4,5},{5,4},{6,7},{7,6},{8,9},{9,8},{10,11... | collective-permute-start | bytes 4718600 | tf_op jit(solution)/shard_map/ppermute | solution.py:576
  58.0 6.6 %collective-permute-start.5 = (f32[136,128]{1,0:T(8,128)S(1)}, f32[136,128]{1,0:T(8,128)S(1)}, u32[]{:S(2)}, u32[]{:S(2)}) collective-permute-start(f32[136,128]{1,0:T(8,128)S(1)} %get-tuple-element.19), channel_id=1, source_target_pairs={{0,2},{2,0},{4,6},{6,4},{8,10},{10,8},{12,14},{14,12},{16,18},{18,... | collective-permute-start | bytes 208904 | tf_op jit(solution)/shard_map/ppermute | solution.py:572
  64.6 8.1 %collective-permute-start.6 = (f32[136,128]{1,0:T(8,128)S(1)}, f32[136,128]{1,0:T(8,128)S(1)}, u32[]{:S(2)}, u32[]{:S(2)}) collective-permute-start(f32[136,128]{1,0:T(8,128)S(1)} %get-tuple-element.27), channel_id=1, source_target_pairs={{0,4},{2,6},{4,0},{6,2},{8,12},{10,14},{12,8},{14,10},{16,20},{18,... | collective-permute-start | bytes 208904 | tf_op jit(solution)/shard_map/ppermute | solution.py:572
  72.7 10.1 %collective-permute-start.7 = (f32[136,128]{1,0:T(8,128)S(1)}, f32[136,128]{1,0:T(8,128)S(1)}, u32[]{:S(2)}, u32[]{:S(2)}) collective-permute-start(f32[136,128]{1,0:T(8,128)S(1)} %get-tuple-element.25), channel_id=1, source_target_pairs={{0,8},{2,10},{4,12},{6,14},{8,0},{10,2},{12,4},{14,6},{16,24},{18,... | collective-permute-start | bytes 208904 | tf_op jit(solution)/shard_map/ppermute | solution.py:572
  82.9 6.2 %collective-permute-start.8 = (f32[136,128]{1,0:T(8,128)S(1)}, f32[136,128]{1,0:T(8,128)S(1)}, u32[]{:S(2)}, u32[]{:S(2)}) collective-permute-start(f32[136,128]{1,0:T(8,128)S(1)} %get-tuple-element.23), channel_id=1, source_target_pairs={{0,16},{2,18},{4,20},{6,22},{8,24},{10,26},{12,28},{14,30},{16,0},... | collective-permute-start | bytes 208904 | tf_op jit(solution)/shard_map/ppermute | solution.py:572
  89.1 3.6 %collective-permute-start.9 = (f32[680,128]{1,0:T(8,128)S(1)}, f32[680,128]{1,0:T(8,128)S(1)}, u32[]{:S(2)}, u32[]{:S(2)}) collective-permute-start(f32[680,128]{1,0:T(8,128)S(1)} %add_dynamic-update-slice_fusion.mine), channel_id=1, source_target_pairs={{0,1},{1,0},{2,3},{3,2},{4,5},{5,4},{6,7},{7,6},{8,9},{9,8},{10,11... | collective-permute-start | bytes 1044488 | tf_op jit(solution)/shard_map/ppermute | solution.py:576

commit v5 on v4

--- a/solution.py
+++ b/solution.py
@@ -329,8 +329,8 @@
 
 def own_kernel(own, out, high, low):
     a0, a1 = halves(own[...])
-    high[...] = a0
-    low[...] = a1
+    high[:, :LANES] = a0
+    low[:, :LANES] = a1
     out[:HALF], out[HALF:] = pack(product((a0, a1), (a0, a1)))
 
 
@@ -340,8 +340,8 @@
         own_kernel,
         (
             pltpu.VMEM((PACKED, half), F32),
-            pltpu.VMEM((leaf, half), BF16),
-            pltpu.VMEM((leaf, half), BF16),
+            pltpu.VMEM((leaf, 2 * half), BF16),
+            pltpu.VMEM((leaf, 2 * half), BF16),
         ),
     )(own)
 
@@ -349,17 +349,18 @@
 def gram_kernel(me, block, high, low, other, out, highs, lows):
     n = LANES
     b0, b1 = halves(other[...])
-    highs[:, :n], highs[:, n:] = high[...], b0
-    lows[:, :n], lows[:, n:] = low[...], b1
+    a0, a1 = high.at[:, :n], low.at[:, :n]
+    highs[:, n:] = b0
+    lows[:, n:] = b1
     out[:PACKED] = block[...]
 
     @pl.when(me[0] == 0)
     def _():
-        out[PACKED:] = product((b0[:, :HALF], b1[:, :HALF]), (high[...], low[...]))
+        out[PACKED:] = product((b0[:, :HALF], b1[:, :HALF]), (a0[...], a1[...]))
 
     @pl.when(me[0] == 1)
     def _():
-        out[PACKED:] = product((high[:, HALF:], low[:, HALF:]), (b0, b1))
+        out[PACKED:] = product((high[:, HALF:n], low[:, HALF:n]), (b0, b1))
 
 
 def gram_blocks(me, block, high, low, other):
@@ -375,6 +376,7 @@
         grid_spec=pltpu.PrefetchScalarGridSpec(
             num_scalar_prefetch=1, grid=(1,), in_specs=[whole] * 4, out_specs=[whole] * 3
         ),
+        input_output_aliases={2: 1, 3: 2},
     )(me, block, high, low, other)
 
 
@@ -568,8 +570,8 @@
     return lax.ppermute(array, "leaf", pairs)
 
 
-def sibling(array, bit):
-    return lax.ppermute(array, "leaf", [(i, i ^ 1 << bit) for i in range(lax.axis_size("leaf"))])
+def sibling(array, flip):
+    return lax.ppermute(array, "leaf", [(i, i ^ flip) for i in range(lax.axis_size("leaf"))])
 
 
 def other_core(array):
@@ -583,9 +585,10 @@
     probes_before = beside(probes, 1)
     probes_after = beside(probes, -1)
     ordered = order_features(features, leaf_order)
-    before = beside(ordered, 1)
-    after = beside(ordered, -1)
     part, rows_t, far, weight = near_part(near_blocks, first, lengthscale, ordered, probes)
+    sent, part = lax.optimization_barrier((ordered, part))
+    before = beside(sent, 1)
+    after = beside(sent, -1)
     own = far_part(
         far, weight, part, rows_t, before, after, probes_before, probes_after, blocks
     )
@@ -593,8 +596,8 @@
     block, high, low = own_gram(own)
     gram, highs, lows = gram_blocks(me, block, high, low, other)
     grams = [gram]
-    for depth in range(LEVELS):
-        gram = gram + sibling(gram, depth)
+    for flip in (1, 2, 7, 8):
+        gram = gram + sibling(gram, flip)
         grams.append(gram)
     mine = jnp.concatenate(grams, 0)
     return factors(me, mine, other_core(mine), highs, lows)

time: 110 us -> 113 us (1.027)
  waiting for transfers between devices: 30 us -> 33.1 us
    ppermute x4, waiting for transfers between devices: 2.86 us -> 8.27 us  [beside(): return lax.ppermute(array, 'leaf', pairs)]
    ppermute x4, waiting for transfers between devices: 23.3 us -> 21 us  [sibling(): lax.ppermute(array, 'leaf', [(i, i ^ flip) for i in range(lax.axis_size('...]
  transfers between devices with their start and end apart: 10 -> 10, of which waited for: 7 -> 7; matrix products, arithmetic and copies ran while one was open for 0% -> 0% of each run, Pallas kernels for 11% -> 12%
where the time goes in v5:
time: 113 us; the launch traced here: 111 us
  Pallas kernels  39.4 us (35%)
  starting transfers between devices  37.8 us (33%)
  waiting for transfers between devices  33.1 us (29%)
    ppermute x4, starting transfers between devices, beside(): return lax.ppermute(array, 'leaf', pairs)  26.1 us
    ppermute x4, waiting for transfers between devices, sibling(): lax.ppermute(array, 'leaf', [(i, i ^ flip) for i in range(lax.axis_size('...  21 us
    pallas_call x1, Pallas kernels, factors(): call(factor_kernel, (jax.ShapeDtypeStruct((LEVELS, n, half), F32), jax.Sh...  15.6 us
    pallas_call x1, Pallas kernels, near_part(): call(near_kernel, (pltpu.VMEM((leaf, half), F32), pltpu.VMEM((leaf, 32),...  9.4 us
    pallas_call x1, Pallas kernels, far_part(): call(far_kernel, pltpu.VMEM((leaf, half), F32), grid_spec=pltpu.PrefetchS...  9.33 us
    ppermute x4, waiting for transfers between devices, beside(): return lax.ppermute(array, 'leaf', pairs)  8.27 us
    ppermute x4, starting transfers between devices, sibling(): lax.ppermute(array, 'leaf', [(i, i ^ flip) for i in range(lax.axis_size('...  7.68 us
    ppermute x2, starting transfers between devices, other_core(): return lax.ppermute(array, 'probe', [(0, 1), (1, 0)])  4.02 us
  transfers between devices with their start and end apart: 10, of which 7 were waited for; matrix products, arithmetic and copies ran while one was open for 0% of the time, Pallas kernels for 12%

profile of v5, /device:TPU:6, one launch (start us, length us, event | category | flops | bytes accessed | tf_op | source)
XLA Modules:
  0.0 111.3 jit_solution(3611387253436562317)
XLA Ops:
  0.6 14.1 %collective-permute-start.3 = (bf16[128,3072]{1,0:T(8,128)(2,1)}, bf16[128,3072]{1,0:T(8,128)(2,1)S(1)}, u32[]{:S(2)}, u32[]{:S(2)}) collective-permute-start(bf16[128,3072]{1,0:T(8,128)(2,1)} %probes.1), channel_id=1, source_target_pairs={{2,0},{4,2},{6,4},{8,6},{10,8},{12,10},{14,12},{16,14},{18,16},{20... | collective-permute-start | bytes 2359304 | tf_op jit(solution)/shard_map/ppermute | solution.py:570
  14.8 1.9 %collective-permute-start.2 = (bf16[128,3072]{1,0:T(8,128)(2,1)}, bf16[128,3072]{1,0:T(8,128)(2,1)S(1)}, u32[]{:S(2)}, u32[]{:S(2)}) collective-permute-start(bf16[128,3072]{1,0:T(8,128)(2,1)} %probes.1), channel_id=1, source_target_pairs={{0,2},{2,4},{4,6},{6,8},{8,10},{10,12},{12,14},{14,16},{16,18},{18... | collective-permute-start | bytes 2359304 | tf_op jit(solution)/shard_map/ppermute | solution.py:570
  16.7 3.0 %shard_map.68.feat = bf16[8,3072]{1,0:T(8,128)(2,1)S(1)} custom-call(bf16[8,3072]{1,0:T(8,128)(2,1)} %feat_in.1, s32[1,3072]{1,0:T(1,128)} %order_in.1), custom_call_target="tpu_custom_call" | custom-call | tf_op jit(solution)/shard_map/pallas_call | solution.py:86
  19.7 9.4 %shard_map.69 = (f32[3072,128]{1,0:T(8,128)S(1)}, bf16[3072,32]{1,0:T(8,128)(2,1)S(1)}, s32[160]{0:T(256)S(1)}, f32[8,128]{1,0:T(8,128)S(1)}) custom-call(s32[1]{0:T(128)} %bitcast.1.first, s32[12,10]{1,0:T(8,128)} %listed_in.1, f32[8]{0:T(128)} %scale_in.1, bf16[8,3072]{1,0:T(8,128)(2,1)S(1)} %shard_map.68.feat, bf16[128,3072]{1,0:T(8,128)(2,1)} %probes.1), custom_call_target="tpu_custom_call" | custom-call | tf_op jit(solution)/shard_map/pallas_call | solution.py:229
  29.1 8.1 %collective-permute-start.1 = (bf16[8,3072]{1,0:T(8,128)(2,1)S(1)}, bf16[8,3072]{1,0:T(8,128)(2,1)S(1)}, u32[]{:S(2)}, u32[]{:S(2)}) collective-permute-start(bf16[8,3072]{1,0:T(8,128)(2,1)S(1)} %shard_map.68.feat), channel_id=1, source_target_pairs={{2,0},{4,2},{6,4},{8,6},{10,8},{12,10},{14,12},{16,14},{18,16},{20... | collective-permute-start | bytes 147464 | tf_op jit(solution)/shard_map/ppermute | solution.py:570
  37.3 1.9 %collective-permute-start = (bf16[8,3072]{1,0:T(8,128)(2,1)S(1)}, bf16[8,3072]{1,0:T(8,128)(2,1)S(1)}, u32[]{:S(2)}, u32[]{:S(2)}) collective-permute-start(bf16[8,3072]{1,0:T(8,128)(2,1)S(1)} %shard_map.68.feat), channel_id=1, source_target_pairs={{0,2},{2,4},{4,6},{6,8},{8,10},{10,12},{12,14},{14,16},{16,18},{18... | collective-permute-start | bytes 147464 | tf_op jit(solution)/shard_map/ppermute | solution.py:570
  39.2 0.0 collective-permute-done.1.right
  39.2 8.3 %collective-permute-done.left = bf16[8,3072]{1,0:T(8,128)(2,1)S(1)} collective-permute-done((bf16[8,3072]{1,0:T(8,128)(2,1)S(1)}, bf16[8,3072]{1,0:T(8,128)(2,1)S(1)}, u32[]{:S(2)}, u32[]{:S(2)}) %collective-permute-start) | collective-permute-done | bytes 49184 | tf_op jit(solution)/shard_map/ppermute | solution.py:570
  47.5 0.0 collective-permute-done.3.after
  47.5 0.0 collective-permute-done.2.before
  47.5 9.3 %shard_map.70.own = f32[3072,128]{1,0:T(8,128)S(1)} custom-call(s32[160]{0:T(256)S(1)} %get-tuple-element.14.far, f32[8,128]{1,0:T(8,128)S(1)} %get-tuple-element.15.weight, f32[3072,128]{1,0:T(8,128)S(1)} %get-tuple-element.17.part, bf16[3072,32]{1,0:T(8,128)(2,1)S(1)} %get-tuple-element.18.rows_t, bf16[8,3072]{1,0:T(8,128)(2,1)S(1)} %collective-permute-done.left, ...), custom_call_target="tpu_custom_call" | custom-call | tf_op jit(solution)/shard_map/pallas_call | solution.py:279
  56.8 1.9 %collective-permute-start.4 = (f32[3072,128]{1,0:T(8,128)S(1)}, f32[3072,128]{1,0:T(8,128)S(1)}, u32[]{:S(2)}, u32[]{:S(2)}) collective-permute-start(f32[3072,128]{1,0:T(8,128)S(1)} %shard_map.70.own), channel_id=1, source_target_pairs={{0,1},{1,0},{2,3},{3,2},{4,5},{5,4},{6,7},{7,6},{8,9},{9,8},{10,11... | collective-permute-start | bytes 4718600 | tf_op jit(solution)/shard_map/ppermute | solution.py:578
  58.7 1.0 shard_map.71
  59.7 2.4 %collective-permute-done.4.other = f32[3072,128]{1,0:T(8,128)S(1)} collective-permute-done((f32[3072,128]{1,0:T(8,128)S(1)}, f32[3072,128]{1,0:T(8,128)S(1)}, u32[]{:S(2)}, u32[]{:S(2)}) %collective-permute-start.4) | collective-permute-done | bytes 1572896 | tf_op jit(solution)/shard_map/ppermute | solution.py:578
  62.1 1.1 shard_map.72
  63.2 1.9 %collective-permute-start.5 = (f32[136,128]{1,0:T(8,128)S(1)}, f32[136,128]{1,0:T(8,128)S(1)}, u32[]{:S(2)}, u32[]{:S(2)}) collective-permute-start(f32[136,128]{1,0:T(8,128)S(1)} %get-tuple-element.23), channel_id=1, source_target_pairs={{0,2},{2,0},{4,6},{6,4},{8,10},{10,8},{12,14},{14,12},{16,18},{18,... | collective-permute-start | bytes 208904 | tf_op jit(solution)/shard_map/ppermute | solution.py:574
  65.2 4.6 %collective-permute-done.5 = f32[136,128]{1,0:T(8,128)S(1)} collective-permute-done((f32[136,128]{1,0:T(8,128)S(1)}, f32[136,128]{1,0:T(8,128)S(1)}, u32[]{:S(2)}, u32[]{:S(2)}) %collective-permute-start.5) | collective-permute-done | bytes 69664 | tf_op jit(solution)/shard_map/ppermute | solution.py:574
  69.8 1.9 %collective-permute-start.6 = (f32[136,128]{1,0:T(8,128)S(1)}, f32[136,128]{1,0:T(8,128)S(1)}, u32[]{:S(2)}, u32[]{:S(2)}) collective-permute-start(f32[136,128]{1,0:T(8,128)S(1)} %get-tuple-element.31), channel_id=1, source_target_pairs={{0,4},{2,6},{4,0},{6,2},{8,12},{10,14},{12,8},{14,10},{16,20},{18,... | collective-permute-start | bytes 208904 | tf_op jit(solution)/shard_map/ppermute | solution.py:574
  71.7 6.2 %collective-permute-done.6 = f32[136,128]{1,0:T(8,128)S(1)} collective-permute-done((f32[136,128]{1,0:T(8,128)S(1)}, f32[136,128]{1,0:T(8,128)S(1)}, u32[]{:S(2)}, u32[]{:S(2)}) %collective-permute-start.6) | collective-permute-done | bytes 69664 | tf_op jit(solution)/shard_map/ppermute | solution.py:574
  77.9 1.9 %collective-permute-start.7 = (f32[136,128]{1,0:T(8,128)S(1)}, f32[136,128]{1,0:T(8,128)S(1)}, u32[]{:S(2)}, u32[]{:S(2)}) collective-permute-start(f32[136,128]{1,0:T(8,128)S(1)} %get-tuple-element.29), channel_id=1, source_target_pairs={{0,14},{2,12},{4,10},{6,8},{8,6},{10,4},{12,2},{14,0},{16,30},{18,... | collective-permute-start | bytes 208904 | tf_op jit(solution)/shard_map/ppermute | solution.py:574
  79.8 5.9 %collective-permute-done.7 = f32[136,128]{1,0:T(8,128)S(1)} collective-permute-done((f32[136,128]{1,0:T(8,128)S(1)}, f32[136,128]{1,0:T(8,128)S(1)}, u32[]{:S(2)}, u32[]{:S(2)}) %collective-permute-start.7) | collective-permute-done | bytes 69664 | tf_op jit(solution)/shard_map/ppermute | solution.py:574
  85.8 1.9 %collective-permute-start.8 = (f32[136,128]{1,0:T(8,128)S(1)}, f32[136,128]{1,0:T(8,128)S(1)}, u32[]{:S(2)}, u32[]{:S(2)}) collective-permute-start(f32[136,128]{1,0:T(8,128)S(1)} %get-tuple-element.27), channel_id=1, source_target_pairs={{0,16},{2,18},{4,20},{6,22},{8,24},{10,26},{12,28},{14,30},{16,0},... | collective-permute-start | bytes 208904 | tf_op jit(solution)/shard_map/ppermute | solution.py:574
  87.7 4.3 %collective-permute-done.8 = f32[136,128]{1,0:T(8,128)S(1)} collective-permute-done((f32[136,128]{1,0:T(8,128)S(1)}, f32[136,128]{1,0:T(8,128)S(1)}, u32[]{:S(2)}, u32[]{:S(2)}) %collective-permute-start.8) | collective-permute-done | bytes 69664 | tf_op jit(solution)/shard_map/ppermute | solution.py:574
  92.0 2.1 %collective-permute-start.9 = (f32[680,128]{1,0:T(8,128)S(1)}, f32[680,128]{1,0:T(8,128)S(1)}, u32[]{:S(2)}, u32[]{:S(2)}) collective-permute-start(f32[680,128]{1,0:T(8,128)S(1)} %add_dynamic-update-slice_fusion.mine), channel_id=1, source_target_pairs={{0,1},{1,0},{2,3},{3,2},{4,5},{5,4},{6,7},{7,6},{8,9},{9,8},{10,11... | collective-permute-start | bytes 1044488 | tf_op jit(solution)/shard_map/ppermute | solution.py:578
  94.1 1.4 %collective-permute-done.9.theirs = f32[680,128]{1,0:T(8,128)S(1)} collective-permute-done((f32[680,128]{1,0:T(8,128)S(1)}, f32[680,128]{1,0:T(8,128)S(1)}, u32[]{:S(2)}, u32[]{:S(2)}) %collective-permute-start.9) | collective-permute-done | bytes 348192 | tf_op jit(solution)/shard_map/ppermute | solution.py:578
  95.5 15.6 %shard_map.73 = (f32[4,256,128]{2,1,0:T(8,128)}, f32[3072,128]{1,0:T(8,128)}) custom-call(s32[1]{0:T(128)} %bitcast.me, f32[680,128]{1,0:T(8,128)S(1)} %add_dynamic-update-slice_fusion.mine, f32[680,128]{1,0:T(8,128)S(1)} %collective-permute-done.9.theirs, bf16[3072,256]{1,0:T(8,128)(2,1)S(1)} %get-tuple-element.24.highs, ...), custom_call_target="tpu_custom_call" | custom-call | tf_op jit(solution)/shard_map/pallas_call | solution.py:543
  (5 shorter events, 0.1 us)
Async XLA Ops:
  0.6 46.8 %collective-permute-start.3 = (bf16[128,3072]{1,0:T(8,128)(2,1)}, bf16[128,3072]{1,0:T(8,128)(2,1)S(1)}, u32[]{:S(2)}, u32[]{:S(2)}) collective-permute-start(bf16[128,3072]{1,0:T(8,128)(2,1)} %probes.1), channel_id=1, source_target_pairs={{2,0},{4,2},{6,4},{8,6},{10,8},{12,10},{14,12},{16,14},{18,16},{20... | collective-permute-start | bytes 2359304 | tf_op jit(solution)/shard_map/ppermute | solution.py:570
  14.8 32.7 %collective-permute-start.2 = (bf16[128,3072]{1,0:T(8,128)(2,1)}, bf16[128,3072]{1,0:T(8,128)(2,1)S(1)}, u32[]{:S(2)}, u32[]{:S(2)}) collective-permute-start(bf16[128,3072]{1,0:T(8,128)(2,1)} %probes.1), channel_id=1, source_target_pairs={{0,2},{2,4},{4,6},{6,8},{8,10},{10,12},{12,14},{14,16},{16,18},{18... | collective-permute-start | bytes 2359304 | tf_op jit(solution)/shard_map/ppermute | solution.py:570
  29.1 10.1 %collective-permute-start.1 = (bf16[8,3072]{1,0:T(8,128)(2,1)S(1)}, bf16[8,3072]{1,0:T(8,128)(2,1)S(1)}, u32[]{:S(2)}, u32[]{:S(2)}) collective-permute-start(bf16[8,3072]{1,0:T(8,128)(2,1)S(1)} %shard_map.68.feat), channel_id=1, source_target_pairs={{2,0},{4,2},{6,4},{8,6},{10,8},{12,10},{14,12},{16,14},{18,16},{20... | collective-permute-start | bytes 147464 | tf_op jit(solution)/shard_map/ppermute | solution.py:570
  37.3 10.2 %collective-permute-start = (bf16[8,3072]{1,0:T(8,128)(2,1)S(1)}, bf16[8,3072]{1,0:T(8,128)(2,1)S(1)}, u32[]{:S(2)}, u32[]{:S(2)}) collective-permute-start(bf16[8,3072]{1,0:T(8,128)(2,1)S(1)} %shard_map.68.feat), channel_id=1, source_target_pairs={{0,2},{2,4},{4,6},{6,8},{8,10},{10,12},{12,14},{14,16},{16,18},{18... | collective-permute-start | bytes 147464 | tf_op jit(solution)/shard_map/ppermute | solution.py:570
  56.8 5.3 %collective-permute-start.4 = (f32[3072,128]{1,0:T(8,128)S(1)}, f32[3072,128]{1,0:T(8,128)S(1)}, u32[]{:S(2)}, u32[]{:S(2)}) collective-permute-start(f32[3072,128]{1,0:T(8,128)S(1)} %shard_map.70.own), channel_id=1, source_target_pairs={{0,1},{1,0},{2,3},{3,2},{4,5},{5,4},{6,7},{7,6},{8,9},{9,8},{10,11... | collective-permute-start | bytes 4718600 | tf_op jit(solution)/shard_map/ppermute | solution.py:578
  63.2 6.6 %collective-permute-start.5 = (f32[136,128]{1,0:T(8,128)S(1)}, f32[136,128]{1,0:T(8,128)S(1)}, u32[]{:S(2)}, u32[]{:S(2)}) collective-permute-start(f32[136,128]{1,0:T(8,128)S(1)} %get-tuple-element.23), channel_id=1, source_target_pairs={{0,2},{2,0},{4,6},{6,4},{8,10},{10,8},{12,14},{14,12},{16,18},{18,... | collective-permute-start | bytes 208904 | tf_op jit(solution)/shard_map/ppermute | solution.py:574
  69.8 8.1 %collective-permute-start.6 = (f32[136,128]{1,0:T(8,128)S(1)}, f32[136,128]{1,0:T(8,128)S(1)}, u32[]{:S(2)}, u32[]{:S(2)}) collective-permute-start(f32[136,128]{1,0:T(8,128)S(1)} %get-tuple-element.31), channel_id=1, source_target_pairs={{0,4},{2,6},{4,0},{6,2},{8,12},{10,14},{12,8},{14,10},{16,20},{18,... | collective-permute-start | bytes 208904 | tf_op jit(solution)/shard_map/ppermute | solution.py:574
  77.9 7.8 %collective-permute-start.7 = (f32[136,128]{1,0:T(8,128)S(1)}, f32[136,128]{1,0:T(8,128)S(1)}, u32[]{:S(2)}, u32[]{:S(2)}) collective-permute-start(f32[136,128]{1,0:T(8,128)S(1)} %get-tuple-element.29), channel_id=1, source_target_pairs={{0,14},{2,12},{4,10},{6,8},{8,6},{10,4},{12,2},{14,0},{16,30},{18,... | collective-permute-start | bytes 208904 | tf_op jit(solution)/shard_map/ppermute | solution.py:574
  85.8 6.2 %collective-permute-start.8 = (f32[136,128]{1,0:T(8,128)S(1)}, f32[136,128]{1,0:T(8,128)S(1)}, u32[]{:S(2)}, u32[]{:S(2)}) collective-permute-start(f32[136,128]{1,0:T(8,128)S(1)} %get-tuple-element.27), channel_id=1, source_target_pairs={{0,16},{2,18},{4,20},{6,22},{8,24},{10,26},{12,28},{14,30},{16,0},... | collective-permute-start | bytes 208904 | tf_op jit(solution)/shard_map/ppermute | solution.py:574
  92.0 3.6 %collective-permute-start.9 = (f32[680,128]{1,0:T(8,128)S(1)}, f32[680,128]{1,0:T(8,128)S(1)}, u32[]{:S(2)}, u32[]{:S(2)}) collective-permute-start(f32[680,128]{1,0:T(8,128)S(1)} %add_dynamic-update-slice_fusion.mine), channel_id=1, source_target_pairs={{0,1},{1,0},{2,3},{3,2},{4,5},{5,4},{6,7},{7,6},{8,9},{9,8},{10,11... | collective-permute-start | bytes 1044488 | tf_op jit(solution)/shard_map/ppermute | solution.py:578

commit v6 on v5

--- a/solution.py
+++ b/solution.py
@@ -78,7 +78,7 @@
         out[:, pl.ds(at, LANES)] = total.astype(BF16)
         return carry
 
-    lax.fori_loop(0, chunks, one, 0)
+    lax.fori_loop(0, chunks, one, 0, unroll=chunks)
 
 
 def order_features(features, leaf_order):
@@ -585,10 +585,9 @@
     probes_before = beside(probes, 1)
     probes_after = beside(probes, -1)
     ordered = order_features(features, leaf_order)
+    before = beside(ordered, 1)
+    after = beside(ordered, -1)
     part, rows_t, far, weight = near_part(near_blocks, first, lengthscale, ordered, probes)
-    sent, part = lax.optimization_barrier((ordered, part))
-    before = beside(sent, 1)
-    after = beside(sent, -1)
     own = far_part(
         far, weight, part, rows_t, before, after, probes_before, probes_after, blocks
     )

time: 113 us -> 107 us (0.947)
  waiting for transfers between devices: 33.1 us -> 29.4 us
  Pallas kernels: 39.4 us -> 36.8 us
    ppermute x4, waiting for transfers between devices: 8.27 us -> 4.58 us  [beside(): return lax.ppermute(array, 'leaf', pairs)]
    pallas_call x1, Pallas kernels: 2.99 us -> 1.27 us  [order_features(): call(order_kernel, jax.ShapeDtypeStruct(features.shape, BF16), in_specs=[...]
  transfers between devices with their start and end apart: 10 -> 10, of which waited for: 7 -> 7; matrix products, arithmetic and copies ran while one was open for 0% -> 0% of each run, Pallas kernels for 12% -> 10%
where the time goes in v6:
time: 107 us; the launch traced here: 105 us
  starting transfers between devices  37.8 us (35%)
  Pallas kernels  36.8 us (34%)
  waiting for transfers between devices  29.4 us (27%)
    ppermute x4, starting transfers between devices, beside(): return lax.ppermute(array, 'leaf', pairs)  26.1 us
    ppermute x4, waiting for transfers between devices, sibling(): lax.ppermute(array, 'leaf', [(i, i ^ flip) for i in range(lax.axis_size('...  21 us
    pallas_call x1, Pallas kernels, factors(): call(factor_kernel, (jax.ShapeDtypeStruct((LEVELS, n, half), F32), jax.Sh...  15.6 us
    pallas_call x1, Pallas kernels, far_part(): call(far_kernel, pltpu.VMEM((leaf, half), F32), grid_spec=pltpu.PrefetchS...  9.32 us
    pallas_call x1, Pallas kernels, near_part(): call(near_kernel, (pltpu.VMEM((leaf, half), F32), pltpu.VMEM((leaf, 32),...  8.5 us
    ppermute x4, starting transfers between devices, sibling(): lax.ppermute(array, 'leaf', [(i, i ^ flip) for i in range(lax.axis_size('...  7.68 us
    ppermute x4, waiting for transfers between devices, beside(): return lax.ppermute(array, 'leaf', pairs)  4.58 us
    ppermute x2, starting transfers between devices, other_core(): return lax.ppermute(array, 'probe', [(0, 1), (1, 0)])  4.02 us
  transfers between devices with their start and end apart: 10, of which 7 were waited for; matrix products, arithmetic and copies ran while one was open for 0% of the time, Pallas kernels for 10%

profile of v6, /device:TPU:6, one launch (start us, length us, event | category | flops | bytes accessed | tf_op | source)
XLA Modules:
  0.0 105.0 jit_solution(1877896656783475508)
XLA Ops:
  0.6 14.1 %collective-permute-start.3 = (bf16[128,3072]{1,0:T(8,128)(2,1)}, bf16[128,3072]{1,0:T(8,128)(2,1)S(1)}, u32[]{:S(2)}, u32[]{:S(2)}) collective-permute-start(bf16[128,3072]{1,0:T(8,128)(2,1)} %probes.1), channel_id=1, source_target_pairs={{2,0},{4,2},{6,4},{8,6},{10,8},{12,10},{14,12},{16,14},{18,16},{20... | collective-permute-start | bytes 2359304 | tf_op jit(solution)/shard_map/ppermute | solution.py:570
  14.8 1.9 %collective-permute-start.2 = (bf16[128,3072]{1,0:T(8,128)(2,1)}, bf16[128,3072]{1,0:T(8,128)(2,1)S(1)}, u32[]{:S(2)}, u32[]{:S(2)}) collective-permute-start(bf16[128,3072]{1,0:T(8,128)(2,1)} %probes.1), channel_id=1, source_target_pairs={{0,2},{2,4},{4,6},{6,8},{8,10},{10,12},{12,14},{14,16},{16,18},{18... | collective-permute-start | bytes 2359304 | tf_op jit(solution)/shard_map/ppermute | solution.py:570
  16.7 1.3 %shard_map.68.feat = bf16[8,3072]{1,0:T(8,128)(2,1)S(1)} custom-call(bf16[8,3072]{1,0:T(8,128)(2,1)} %feat_in.1, s32[1,3072]{1,0:T(1,128)} %order_in.1), custom_call_target="tpu_custom_call" | custom-call | tf_op jit(solution)/shard_map/pallas_call | solution.py:86
  18.0 8.1 %collective-permute-start.1 = (bf16[8,3072]{1,0:T(8,128)(2,1)S(1)}, bf16[8,3072]{1,0:T(8,128)(2,1)S(1)}, u32[]{:S(2)}, u32[]{:S(2)}) collective-permute-start(bf16[8,3072]{1,0:T(8,128)(2,1)S(1)} %shard_map.68.feat), channel_id=1, source_target_pairs={{2,0},{4,2},{6,4},{8,6},{10,8},{12,10},{14,12},{16,14},{18,16},{20... | collective-permute-start | bytes 147464 | tf_op jit(solution)/shard_map/ppermute | solution.py:570
  26.1 1.9 %collective-permute-start = (bf16[8,3072]{1,0:T(8,128)(2,1)S(1)}, bf16[8,3072]{1,0:T(8,128)(2,1)S(1)}, u32[]{:S(2)}, u32[]{:S(2)}) collective-permute-start(bf16[8,3072]{1,0:T(8,128)(2,1)S(1)} %shard_map.68.feat), channel_id=1, source_target_pairs={{0,2},{2,4},{4,6},{6,8},{8,10},{10,12},{12,14},{14,16},{16,18},{18... | collective-permute-start | bytes 147464 | tf_op jit(solution)/shard_map/ppermute | solution.py:570
  28.0 8.5 %shard_map.69 = (f32[3072,128]{1,0:T(8,128)S(1)}, bf16[3072,32]{1,0:T(8,128)(2,1)S(1)}, s32[160]{0:T(256)S(1)}, f32[8,128]{1,0:T(8,128)S(1)}) custom-call(s32[1]{0:T(128)} %bitcast.1.first, s32[12,10]{1,0:T(8,128)} %listed_in.1, f32[8]{0:T(128)} %scale_in.1, bf16[8,3072]{1,0:T(8,128)(2,1)S(1)} %shard_map.68.feat, bf16[128,3072]{1,0:T(8,128)(2,1)} %probes.1), custom_call_target="tpu_custom_call" | custom-call | tf_op jit(solution)/shard_map/pallas_call | solution.py:229
  36.6 0.0 collective-permute-done.1.right
  36.6 4.6 %collective-permute-done.left = bf16[8,3072]{1,0:T(8,128)(2,1)S(1)} collective-permute-done((bf16[8,3072]{1,0:T(8,128)(2,1)S(1)}, bf16[8,3072]{1,0:T(8,128)(2,1)S(1)}, u32[]{:S(2)}, u32[]{:S(2)}) %collective-permute-start) | collective-permute-done | bytes 49184 | tf_op jit(solution)/shard_map/ppermute | solution.py:570
  41.1 0.0 collective-permute-done.3.after
  41.1 0.0 collective-permute-done.2.before
  41.1 9.3 %shard_map.70.own = f32[3072,128]{1,0:T(8,128)S(1)} custom-call(s32[160]{0:T(256)S(1)} %get-tuple-element.12.far, f32[8,128]{1,0:T(8,128)S(1)} %get-tuple-element.13.weight, f32[3072,128]{1,0:T(8,128)S(1)} %get-tuple-element.14.part, bf16[3072,32]{1,0:T(8,128)(2,1)S(1)} %get-tuple-element.15.rows_t, bf16[8,3072]{1,0:T(8,128)(2,1)S(1)} %collective-permute-done.left, ...), custom_call_target="tpu_custom_call" | custom-call | tf_op jit(solution)/shard_map/pallas_call | solution.py:279
  50.5 1.9 %collective-permute-start.4 = (f32[3072,128]{1,0:T(8,128)S(1)}, f32[3072,128]{1,0:T(8,128)S(1)}, u32[]{:S(2)}, u32[]{:S(2)}) collective-permute-start(f32[3072,128]{1,0:T(8,128)S(1)} %shard_map.70.own), channel_id=1, source_target_pairs={{0,1},{1,0},{2,3},{3,2},{4,5},{5,4},{6,7},{7,6},{8,9},{9,8},{10,11... | collective-permute-start | bytes 4718600 | tf_op jit(solution)/shard_map/ppermute | solution.py:578
  52.4 1.0 shard_map.71
  53.4 2.4 %collective-permute-done.4.other = f32[3072,128]{1,0:T(8,128)S(1)} collective-permute-done((f32[3072,128]{1,0:T(8,128)S(1)}, f32[3072,128]{1,0:T(8,128)S(1)}, u32[]{:S(2)}, u32[]{:S(2)}) %collective-permute-start.4) | collective-permute-done | bytes 1572896 | tf_op jit(solution)/shard_map/ppermute | solution.py:578
  55.8 1.1 %shard_map.72 = (f32[136,128]{1,0:T(8,128)S(1)}, bf16[3072,256]{1,0:T(8,128)(2,1)S(1)}, bf16[3072,256]{1,0:T(8,128)(2,1)S(1)}) custom-call(s32[1]{0:T(128)} %bitcast.me, f32[72,128]{1,0:T(8,128)S(1)} %get-tuple-element.16.block, bf16[3072,256]{1,0:T(8,128)(2,1)S(1)} %get-tuple-element.17.high, ...), custom_call_target="tpu_custom_call", output_to_operand_aliasing={{1}: (2, {}), {2}: (3, {})} | custom-call | tf_op jit(solution)/shard_map/pallas_call | solution.py:369
  56.9 1.9 %collective-permute-start.5 = (f32[136,128]{1,0:T(8,128)S(1)}, f32[136,128]{1,0:T(8,128)S(1)}, u32[]{:S(2)}, u32[]{:S(2)}) collective-permute-start(f32[136,128]{1,0:T(8,128)S(1)} %get-tuple-element.19), channel_id=1, source_target_pairs={{0,2},{2,0},{4,6},{6,4},{8,10},{10,8},{12,14},{14,12},{16,18},{18,... | collective-permute-start | bytes 208904 | tf_op jit(solution)/shard_map/ppermute | solution.py:574
  58.8 4.6 %collective-permute-done.5 = f32[136,128]{1,0:T(8,128)S(1)} collective-permute-done((f32[136,128]{1,0:T(8,128)S(1)}, f32[136,128]{1,0:T(8,128)S(1)}, u32[]{:S(2)}, u32[]{:S(2)}) %collective-permute-start.5) | collective-permute-done | bytes 69664 | tf_op jit(solution)/shard_map/ppermute | solution.py:574
  63.5 1.9 %collective-permute-start.6 = (f32[136,128]{1,0:T(8,128)S(1)}, f32[136,128]{1,0:T(8,128)S(1)}, u32[]{:S(2)}, u32[]{:S(2)}) collective-permute-start(f32[136,128]{1,0:T(8,128)S(1)} %get-tuple-element.27), channel_id=1, source_target_pairs={{0,4},{2,6},{4,0},{6,2},{8,12},{10,14},{12,8},{14,10},{16,20},{18,... | collective-permute-start | bytes 208904 | tf_op jit(solution)/shard_map/ppermute | solution.py:574
  65.4 6.2 %collective-permute-done.6 = f32[136,128]{1,0:T(8,128)S(1)} collective-permute-done((f32[136,128]{1,0:T(8,128)S(1)}, f32[136,128]{1,0:T(8,128)S(1)}, u32[]{:S(2)}, u32[]{:S(2)}) %collective-permute-start.6) | collective-permute-done | bytes 69664 | tf_op jit(solution)/shard_map/ppermute | solution.py:574
  71.6 1.9 %collective-permute-start.7 = (f32[136,128]{1,0:T(8,128)S(1)}, f32[136,128]{1,0:T(8,128)S(1)}, u32[]{:S(2)}, u32[]{:S(2)}) collective-permute-start(f32[136,128]{1,0:T(8,128)S(1)} %get-tuple-element.25), channel_id=1, source_target_pairs={{0,14},{2,12},{4,10},{6,8},{8,6},{10,4},{12,2},{14,0},{16,30},{18,... | collective-permute-start | bytes 208904 | tf_op jit(solution)/shard_map/ppermute | solution.py:574
  73.5 5.9 %collective-permute-done.7 = f32[136,128]{1,0:T(8,128)S(1)} collective-permute-done((f32[136,128]{1,0:T(8,128)S(1)}, f32[136,128]{1,0:T(8,128)S(1)}, u32[]{:S(2)}, u32[]{:S(2)}) %collective-permute-start.7) | collective-permute-done | bytes 69664 | tf_op jit(solution)/shard_map/ppermute | solution.py:574
  79.4 1.9 %collective-permute-start.8 = (f32[136,128]{1,0:T(8,128)S(1)}, f32[136,128]{1,0:T(8,128)S(1)}, u32[]{:S(2)}, u32[]{:S(2)}) collective-permute-start(f32[136,128]{1,0:T(8,128)S(1)} %get-tuple-element.23), channel_id=1, source_target_pairs={{0,16},{2,18},{4,20},{6,22},{8,24},{10,26},{12,28},{14,30},{16,0},... | collective-permute-start | bytes 208904 | tf_op jit(solution)/shard_map/ppermute | solution.py:574
  81.4 4.3 %collective-permute-done.8 = f32[136,128]{1,0:T(8,128)S(1)} collective-permute-done((f32[136,128]{1,0:T(8,128)S(1)}, f32[136,128]{1,0:T(8,128)S(1)}, u32[]{:S(2)}, u32[]{:S(2)}) %collective-permute-start.8) | collective-permute-done | bytes 69664 | tf_op jit(solution)/shard_map/ppermute | solution.py:574
  85.7 2.1 %collective-permute-start.9 = (f32[680,128]{1,0:T(8,128)S(1)}, f32[680,128]{1,0:T(8,128)S(1)}, u32[]{:S(2)}, u32[]{:S(2)}) collective-permute-start(f32[680,128]{1,0:T(8,128)S(1)} %add_dynamic-update-slice_fusion.mine), channel_id=1, source_target_pairs={{0,1},{1,0},{2,3},{3,2},{4,5},{5,4},{6,7},{7,6},{8,9},{9,8},{10,11... | collective-permute-start | bytes 1044488 | tf_op jit(solution)/shard_map/ppermute | solution.py:578
  87.8 1.4 %collective-permute-done.9.theirs = f32[680,128]{1,0:T(8,128)S(1)} collective-permute-done((f32[680,128]{1,0:T(8,128)S(1)}, f32[680,128]{1,0:T(8,128)S(1)}, u32[]{:S(2)}, u32[]{:S(2)}) %collective-permute-start.9) | collective-permute-done | bytes 348192 | tf_op jit(solution)/shard_map/ppermute | solution.py:578
  89.2 15.6 %shard_map.73 = (f32[4,256,128]{2,1,0:T(8,128)}, f32[3072,128]{1,0:T(8,128)}) custom-call(s32[1]{0:T(128)} %bitcast.me, f32[680,128]{1,0:T(8,128)S(1)} %add_dynamic-update-slice_fusion.mine, f32[680,128]{1,0:T(8,128)S(1)} %collective-permute-done.9.theirs, bf16[3072,256]{1,0:T(8,128)(2,1)S(1)} %get-tuple-element.20.highs, ...), custom_call_target="tpu_custom_call" | custom-call | tf_op jit(solution)/shard_map/pallas_call | solution.py:543
  (5 shorter events, 0.1 us)
Async XLA Ops:
  0.6 40.5 %collective-permute-start.3 = (bf16[128,3072]{1,0:T(8,128)(2,1)}, bf16[128,3072]{1,0:T(8,128)(2,1)S(1)}, u32[]{:S(2)}, u32[]{:S(2)}) collective-permute-start(bf16[128,3072]{1,0:T(8,128)(2,1)} %probes.1), channel_id=1, source_target_pairs={{2,0},{4,2},{6,4},{8,6},{10,8},{12,10},{14,12},{16,14},{18,16},{20... | collective-permute-start | bytes 2359304 | tf_op jit(solution)/shard_map/ppermute | solution.py:570
  14.8 26.4 %collective-permute-start.2 = (bf16[128,3072]{1,0:T(8,128)(2,1)}, bf16[128,3072]{1,0:T(8,128)(2,1)S(1)}, u32[]{:S(2)}, u32[]{:S(2)}) collective-permute-start(bf16[128,3072]{1,0:T(8,128)(2,1)} %probes.1), channel_id=1, source_target_pairs={{0,2},{2,4},{4,6},{6,8},{8,10},{10,12},{12,14},{14,16},{16,18},{18... | collective-permute-start | bytes 2359304 | tf_op jit(solution)/shard_map/ppermute | solution.py:570
  18.0 18.6 %collective-permute-start.1 = (bf16[8,3072]{1,0:T(8,128)(2,1)S(1)}, bf16[8,3072]{1,0:T(8,128)(2,1)S(1)}, u32[]{:S(2)}, u32[]{:S(2)}) collective-permute-start(bf16[8,3072]{1,0:T(8,128)(2,1)S(1)} %shard_map.68.feat), channel_id=1, source_target_pairs={{2,0},{4,2},{6,4},{8,6},{10,8},{12,10},{14,12},{16,14},{18,16},{20... | collective-permute-start | bytes 147464 | tf_op jit(solution)/shard_map/ppermute | solution.py:570
  26.1 15.0 %collective-permute-start = (bf16[8,3072]{1,0:T(8,128)(2,1)S(1)}, bf16[8,3072]{1,0:T(8,128)(2,1)S(1)}, u32[]{:S(2)}, u32[]{:S(2)}) collective-permute-start(bf16[8,3072]{1,0:T(8,128)(2,1)S(1)} %shard_map.68.feat), channel_id=1, source_target_pairs={{0,2},{2,4},{4,6},{6,8},{8,10},{10,12},{12,14},{14,16},{16,18},{18... | collective-permute-start | bytes 147464 | tf_op jit(solution)/shard_map/ppermute | solution.py:570
  50.5 5.3 %collective-permute-start.4 = (f32[3072,128]{1,0:T(8,128)S(1)}, f32[3072,128]{1,0:T(8,128)S(1)}, u32[]{:S(2)}, u32[]{:S(2)}) collective-permute-start(f32[3072,128]{1,0:T(8,128)S(1)} %shard_map.70.own), channel_id=1, source_target_pairs={{0,1},{1,0},{2,3},{3,2},{4,5},{5,4},{6,7},{7,6},{8,9},{9,8},{10,11... | collective-permute-start | bytes 4718600 | tf_op jit(solution)/shard_map/ppermute | solution.py:578
  56.9 6.6 %collective-permute-start.5 = (f32[136,128]{1,0:T(8,128)S(1)}, f32[136,128]{1,0:T(8,128)S(1)}, u32[]{:S(2)}, u32[]{:S(2)}) collective-permute-start(f32[136,128]{1,0:T(8,128)S(1)} %get-tuple-element.19), channel_id=1, source_target_pairs={{0,2},{2,0},{4,6},{6,4},{8,10},{10,8},{12,14},{14,12},{16,18},{18,... | collective-permute-start | bytes 208904 | tf_op jit(solution)/shard_map/ppermute | solution.py:574
  63.5 8.1 %collective-permute-start.6 = (f32[136,128]{1,0:T(8,128)S(1)}, f32[136,128]{1,0:T(8,128)S(1)}, u32[]{:S(2)}, u32[]{:S(2)}) collective-permute-start(f32[136,128]{1,0:T(8,128)S(1)} %get-tuple-element.27), channel_id=1, source_target_pairs={{0,4},{2,6},{4,0},{6,2},{8,12},{10,14},{12,8},{14,10},{16,20},{18,... | collective-permute-start | bytes 208904 | tf_op jit(solution)/shard_map/ppermute | solution.py:574
  71.6 7.8 %collective-permute-start.7 = (f32[136,128]{1,0:T(8,128)S(1)}, f32[136,128]{1,0:T(8,128)S(1)}, u32[]{:S(2)}, u32[]{:S(2)}) collective-permute-start(f32[136,128]{1,0:T(8,128)S(1)} %get-tuple-element.25), channel_id=1, source_target_pairs={{0,14},{2,12},{4,10},{6,8},{8,6},{10,4},{12,2},{14,0},{16,30},{18,... | collective-permute-start | bytes 208904 | tf_op jit(solution)/shard_map/ppermute | solution.py:574
  79.4 6.2 %collective-permute-start.8 = (f32[136,128]{1,0:T(8,128)S(1)}, f32[136,128]{1,0:T(8,128)S(1)}, u32[]{:S(2)}, u32[]{:S(2)}) collective-permute-start(f32[136,128]{1,0:T(8,128)S(1)} %get-tuple-element.23), channel_id=1, source_target_pairs={{0,16},{2,18},{4,20},{6,22},{8,24},{10,26},{12,28},{14,30},{16,0},... | collective-permute-start | bytes 208904 | tf_op jit(solution)/shard_map/ppermute | solution.py:574
  85.7 3.6 %collective-permute-start.9 = (f32[680,128]{1,0:T(8,128)S(1)}, f32[680,128]{1,0:T(8,128)S(1)}, u32[]{:S(2)}, u32[]{:S(2)}) collective-permute-start(f32[680,128]{1,0:T(8,128)S(1)} %add_dynamic-update-slice_fusion.mine), channel_id=1, source_target_pairs={{0,1},{1,0},{2,3},{3,2},{4,5},{5,4},{6,7},{7,6},{8,9},{9,8},{10,11... | collective-permute-start | bytes 1044488 | tf_op jit(solution)/shard_map/ppermute | solution.py:578

commit v7 on v6

--- a/solution.py
+++ b/solution.py
@@ -56,7 +56,10 @@
     return pltpu.with_memory_space_constraint(array, pltpu.HBM)
 
 
-def order_kernel(feat_in, order_in, out, feat, order, sems):
+def order_kernel(feat_in, order_in, probes_in, out, feat, order, sems):
+    rows = probes_in.shape[0]
+    moved = pltpu.make_async_copy(probes_in, out.at[:rows], sems.at[2])
+    moved.start()
     copies = [
         pltpu.make_async_copy(feat_in, feat, sems.at[0]),
         pltpu.make_async_copy(order_in, order, sems.at[1]),
@@ -75,25 +78,26 @@
         total = jnp.zeros(TILE, F32)
         for c in range(chunks):
             total = jnp.where(high == c, jnp.take_along_axis(pieces[c], low, axis=1), total)
-        out[:, pl.ds(at, LANES)] = total.astype(BF16)
+        out[rows:, pl.ds(at, LANES)] = total.astype(BF16)
         return carry
 
     lax.fori_loop(0, chunks, one, 0, unroll=chunks)
-
-
-def order_features(features, leaf_order):
+    moved.wait()
+
+
+def order_features(features, leaf_order, probes):
     anywhere = pl.BlockSpec(memory_space=pltpu.HBM)
     return call(
         order_kernel,
-        jax.ShapeDtypeStruct(features.shape, BF16),
-        in_specs=[anywhere] * 2,
+        jax.ShapeDtypeStruct((probes.shape[0] + features.shape[0], features.shape[1]), BF16),
+        in_specs=[anywhere] * 3,
         out_specs=pl.BlockSpec(memory_space=pltpu.VMEM),
         scratch_shapes=[
             pltpu.VMEM(features.shape, BF16),
             pltpu.VMEM(leaf_order.shape, jnp.int32),
-            pltpu.SemaphoreType.DMA((2,)),
+            pltpu.SemaphoreType.DMA((3,)),
         ],
-    )(in_hbm(features), in_hbm(leaf_order))
+    )(in_hbm(features), in_hbm(leaf_order), in_hbm(probes))
 
 
 SHIFT = 6
@@ -171,10 +175,11 @@
 
 
 def near_kernel(
-    first, listed_in, scale_in, feat, probes, out, rows_t, far, weight_out,
+    first, listed_in, scale_in, stack, probes, out, rows_t, far, weight_out,
     near_blocks, scale, tasks, cols, panel, k0, k1, sems,
 ):
     blocks, near = near_blocks.shape
+    feat = stack.at[probes.shape[0] :]
     block = feat.shape[1] // blocks
     copies = [
         pltpu.make_async_copy(listed_in, near_blocks, sems.at[0]),
@@ -252,13 +257,15 @@
     )(first, in_hbm(near_blocks), in_hbm(scale), feat, in_hbm(probes))
 
 
-def far_kernel(far, weight, part, rows_t, left, right, before, after, out, cols, panel, k0, k1):
+def far_kernel(far, weight, part, rows_t, before, after, out, cols, panel, k0, k1):
     blocks = (cols.shape[0] - 1) // 2
+    rows = panel.shape[1]
+    left, right = before.at[rows:], after.at[rows:]
     load_columns(cols, panel, [left, right], weight[:, :1], blocks)
     block = cols.shape[2]
     for n, probe in enumerate((before, after)):
         for b in range(blocks):
-            panel[n * blocks + b] = probe[:, b * block : (b + 1) * block]
+            panel[n * blocks + b] = probe[:rows, b * block : (b + 1) * block]
     out[...] = part[...]
     run_tasks(
         far,
@@ -272,8 +279,8 @@
     )
 
 
-def far_part(far, weight, part, rows_t, left, right, before, after, blocks):
-    half, leaf = before.shape
+def far_part(far, weight, part, rows_t, before, after, blocks):
+    leaf, half = part.shape
     block = leaf // blocks
     whole = pl.BlockSpec(memory_space=pltpu.VMEM)
     return call(
@@ -282,7 +289,7 @@
         grid_spec=pltpu.PrefetchScalarGridSpec(
             num_scalar_prefetch=1,
             grid=(1,),
-            in_specs=[whole] * 7,
+            in_specs=[whole] * 5,
             out_specs=whole,
             scratch_shapes=[
                 pltpu.VMEM((2 * blocks + 1, 32, block), BF16),
@@ -290,7 +297,7 @@
                 *[pltpu.VMEM((WIDE, block, block), BF16)] * 2,
             ],
         ),
-    )(far, weight, part, rows_t, left, right, before, after)
+    )(far, weight, part, rows_t, before, after)
 
 
 HALF = LANES // 2
@@ -582,15 +589,11 @@
     blocks = near_blocks.shape[0]
     me = lax.axis_index("probe").astype(jnp.int32)[None]
     first = ((lax.axis_index("leaf") - 1) * blocks).astype(jnp.int32)[None]
-    probes_before = beside(probes, 1)
-    probes_after = beside(probes, -1)
-    ordered = order_features(features, leaf_order)
-    before = beside(ordered, 1)
-    after = beside(ordered, -1)
-    part, rows_t, far, weight = near_part(near_blocks, first, lengthscale, ordered, probes)
-    own = far_part(
-        far, weight, part, rows_t, before, after, probes_before, probes_after, blocks
-    )
+    stack = order_features(features, leaf_order, probes)
+    before = beside(stack, 1)
+    after = beside(stack, -1)
+    part, rows_t, far, weight = near_part(near_blocks, first, lengthscale, stack, probes)
+    own = far_part(far, weight, part, rows_t, before, after, blocks)
     other = other_core(own)
     block, high, low = own_gram(own)
     gram, highs, lows = gram_blocks(me, block, high, low, other)

time: 107 us -> 108 us (level); the launches traced: 105 us -> 107 us
  waiting for transfers between devices: 29.4 us -> 40.5 us
  starting transfers between devices: 37.8 us -> 27.7 us
  Pallas kernels: 36.8 us -> 38 us
    ppermute x4 -> x2, waiting for transfers between devices: 4.58 us -> 15.7 us  [beside(): return lax.ppermute(array, 'leaf', pairs)]
    ppermute x4 -> x2, starting transfers between devices: 26.1 us -> 16 us  [beside(): return lax.ppermute(array, 'leaf', pairs)]
  transfers between devices with their start and end apart: 10 -> 8, of which waited for: 7 -> 8; matrix products, arithmetic and copies ran while one was open for 0% -> 0% of each run, Pallas kernels for 10% -> 9%
where the time goes in v7:
time: 108 us; the launch traced here: 107 us
  waiting for transfers between devices  40.5 us (38%)
  Pallas kernels  38 us (35%)
  starting transfers between devices  27.7 us (26%)
    ppermute x4, waiting for transfers between devices, sibling(): lax.ppermute(array, 'leaf', [(i, i ^ flip) for i in range(lax.axis_size('...  21 us
    ppermute x2, starting transfers between devices, beside(): return lax.ppermute(array, 'leaf', pairs)  16 us
    ppermute x2, waiting for transfers between devices, beside(): return lax.ppermute(array, 'leaf', pairs)  15.7 us
    pallas_call x1, Pallas kernels, factors(): call(factor_kernel, (jax.ShapeDtypeStruct((LEVELS, n, half), F32), jax.Sh...  15.6 us
    pallas_call x1, Pallas kernels, far_part(): call(far_kernel, pltpu.VMEM((leaf, half), F32), grid_spec=pltpu.PrefetchS...  10.2 us
    pallas_call x1, Pallas kernels, near_part(): call(near_kernel, (pltpu.VMEM((leaf, half), F32), pltpu.VMEM((leaf, 32),...  8.5 us
    ppermute x4, starting transfers between devices, sibling(): lax.ppermute(array, 'leaf', [(i, i ^ flip) for i in range(lax.axis_size('...  7.68 us
    ppermute x2, starting transfers between devices, other_core(): return lax.ppermute(array, 'probe', [(0, 1), (1, 0)])  4.02 us
  transfers between devices with their start and end apart: 8, of which 8 were waited for; matrix products, arithmetic and copies ran while one was open for 0% of the time, Pallas kernels for 9%

profile of v7, /device:TPU:6, one launch (start us, length us, event | category | flops | bytes accessed | tf_op | source)
XLA Modules:
  0.0 107.2 jit_solution(8776922132442506395)
XLA Ops:
  0.6 1.6 %shard_map.68.stack = bf16[136,3072]{1,0:T(8,128)(2,1)S(1)} custom-call(bf16[8,3072]{1,0:T(8,128)(2,1)} %feat_in.1, s32[1,3072]{1,0:T(1,128)} %order_in.1, bf16[128,3072]{1,0:T(8,128)(2,1)} %probes.1), custom_call_target="tpu_custom_call" | custom-call | tf_op jit(solution)/shard_map/pallas_call | solution.py:90
  2.2 14.1 %collective-permute-start.1 = (bf16[136,3072]{1,0:T(8,128)(2,1)S(1)}, bf16[136,3072]{1,0:T(8,128)(2,1)S(1)}, u32[]{:S(2)}, u32[]{:S(2)}) collective-permute-start(bf16[136,3072]{1,0:T(8,128)(2,1)S(1)} %shard_map.68.stack), channel_id=1, source_target_pairs={{2,0},{4,2},{6,4},{8,6},{10,8},{12,10},{14,12},{16,14},{18,16},{20... | collective-permute-start | bytes 2506760 | tf_op jit(solution)/shard_map/ppermute | solution.py:577
  16.3 1.9 %collective-permute-start = (bf16[136,3072]{1,0:T(8,128)(2,1)S(1)}, bf16[136,3072]{1,0:T(8,128)(2,1)S(1)}, u32[]{:S(2)}, u32[]{:S(2)}) collective-permute-start(bf16[136,3072]{1,0:T(8,128)(2,1)S(1)} %shard_map.68.stack), channel_id=1, source_target_pairs={{0,2},{2,4},{4,6},{6,8},{8,10},{10,12},{12,14},{14,16},{16,18},{18... | collective-permute-start | bytes 2506760 | tf_op jit(solution)/shard_map/ppermute | solution.py:577
  18.3 8.5 %shard_map.69 = (f32[3072,128]{1,0:T(8,128)S(1)}, bf16[3072,32]{1,0:T(8,128)(2,1)S(1)}, s32[160]{0:T(256)S(1)}, f32[8,128]{1,0:T(8,128)S(1)}) custom-call(s32[1]{0:T(128)} %bitcast.1.first, s32[12,10]{1,0:T(8,128)} %listed_in.1, f32[8]{0:T(128)} %scale_in.1, bf16[136,3072]{1,0:T(8,128)(2,1)S(1)} %shard_map.68.stack, bf16[128,3072]{1,0:T(8,128)(2,1)} %probes.1), custom_call_target="tpu_custom_call" | custom-call | tf_op jit(solution)/shard_map/pallas_call | solution.py:234
  26.8 7.4 %collective-permute-done.1.after = bf16[136,3072]{1,0:T(8,128)(2,1)S(1)} collective-permute-done((bf16[136,3072]{1,0:T(8,128)(2,1)S(1)}, bf16[136,3072]{1,0:T(8,128)(2,1)S(1)}, u32[]{:S(2)}, u32[]{:S(2)}) %collective-permute-start.1) | collective-permute-done | bytes 835616 | tf_op jit(solution)/shard_map/ppermute | solution.py:577
  34.2 8.3 %collective-permute-done.before = bf16[136,3072]{1,0:T(8,128)(2,1)S(1)} collective-permute-done((bf16[136,3072]{1,0:T(8,128)(2,1)S(1)}, bf16[136,3072]{1,0:T(8,128)(2,1)S(1)}, u32[]{:S(2)}, u32[]{:S(2)}) %collective-permute-start) | collective-permute-done | bytes 835616 | tf_op jit(solution)/shard_map/ppermute | solution.py:577
  42.5 10.2 %shard_map.70.own = f32[3072,128]{1,0:T(8,128)S(1)} custom-call(s32[160]{0:T(256)S(1)} %get-tuple-element.12.far, f32[8,128]{1,0:T(8,128)S(1)} %get-tuple-element.13.weight, f32[3072,128]{1,0:T(8,128)S(1)} %get-tuple-element.14.part, bf16[3072,32]{1,0:T(8,128)(2,1)S(1)} %get-tuple-element.15.rows_t, bf16[136,3072]{1,0:T(8,128)(2,1)S(1)} %collective-permute-done.before, ...), custom_call_target="tpu_custom_call" | custom-call | tf_op jit(solution)/shard_map/pallas_call | solution.py:286
  52.7 1.9 %collective-permute-start.2 = (f32[3072,128]{1,0:T(8,128)S(1)}, f32[3072,128]{1,0:T(8,128)S(1)}, u32[]{:S(2)}, u32[]{:S(2)}) collective-permute-start(f32[3072,128]{1,0:T(8,128)S(1)} %shard_map.70.own), channel_id=1, source_target_pairs={{0,1},{1,0},{2,3},{3,2},{4,5},{5,4},{6,7},{7,6},{8,9},{9,8},{10,11... | collective-permute-start | bytes 4718600 | tf_op jit(solution)/shard_map/ppermute | solution.py:585
  54.7 1.0 shard_map.71
  55.7 2.4 %collective-permute-done.2.other = f32[3072,128]{1,0:T(8,128)S(1)} collective-permute-done((f32[3072,128]{1,0:T(8,128)S(1)}, f32[3072,128]{1,0:T(8,128)S(1)}, u32[]{:S(2)}, u32[]{:S(2)}) %collective-permute-start.2) | collective-permute-done | bytes 1572896 | tf_op jit(solution)/shard_map/ppermute | solution.py:585
  58.0 1.1 %shard_map.72 = (f32[136,128]{1,0:T(8,128)S(1)}, bf16[3072,256]{1,0:T(8,128)(2,1)S(1)}, bf16[3072,256]{1,0:T(8,128)(2,1)S(1)}) custom-call(s32[1]{0:T(128)} %bitcast.me, f32[72,128]{1,0:T(8,128)S(1)} %get-tuple-element.16.block, bf16[3072,256]{1,0:T(8,128)(2,1)S(1)} %get-tuple-element.17.high, ...), custom_call_target="tpu_custom_call", output_to_operand_aliasing={{1}: (2, {}), {2}: (3, {})} | custom-call | tf_op jit(solution)/shard_map/pallas_call | solution.py:376
  59.1 1.9 %collective-permute-start.3 = (f32[136,128]{1,0:T(8,128)S(1)}, f32[136,128]{1,0:T(8,128)S(1)}, u32[]{:S(2)}, u32[]{:S(2)}) collective-permute-start(f32[136,128]{1,0:T(8,128)S(1)} %get-tuple-element.19), channel_id=1, source_target_pairs={{0,2},{2,0},{4,6},{6,4},{8,10},{10,8},{12,14},{14,12},{16,18},{18,... | collective-permute-start | bytes 208904 | tf_op jit(solution)/shard_map/ppermute | solution.py:581
  61.1 4.6 %collective-permute-done.3 = f32[136,128]{1,0:T(8,128)S(1)} collective-permute-done((f32[136,128]{1,0:T(8,128)S(1)}, f32[136,128]{1,0:T(8,128)S(1)}, u32[]{:S(2)}, u32[]{:S(2)}) %collective-permute-start.3) | collective-permute-done | bytes 69664 | tf_op jit(solution)/shard_map/ppermute | solution.py:581
  65.7 1.9 %collective-permute-start.4 = (f32[136,128]{1,0:T(8,128)S(1)}, f32[136,128]{1,0:T(8,128)S(1)}, u32[]{:S(2)}, u32[]{:S(2)}) collective-permute-start(f32[136,128]{1,0:T(8,128)S(1)} %get-tuple-element.27), channel_id=1, source_target_pairs={{0,4},{2,6},{4,0},{6,2},{8,12},{10,14},{12,8},{14,10},{16,20},{18,... | collective-permute-start | bytes 208904 | tf_op jit(solution)/shard_map/ppermute | solution.py:581
  67.7 6.2 %collective-permute-done.4 = f32[136,128]{1,0:T(8,128)S(1)} collective-permute-done((f32[136,128]{1,0:T(8,128)S(1)}, f32[136,128]{1,0:T(8,128)S(1)}, u32[]{:S(2)}, u32[]{:S(2)}) %collective-permute-start.4) | collective-permute-done | bytes 69664 | tf_op jit(solution)/shard_map/ppermute | solution.py:581
  73.9 1.9 %collective-permute-start.5 = (f32[136,128]{1,0:T(8,128)S(1)}, f32[136,128]{1,0:T(8,128)S(1)}, u32[]{:S(2)}, u32[]{:S(2)}) collective-permute-start(f32[136,128]{1,0:T(8,128)S(1)} %get-tuple-element.25), channel_id=1, source_target_pairs={{0,14},{2,12},{4,10},{6,8},{8,6},{10,4},{12,2},{14,0},{16,30},{18,... | collective-permute-start | bytes 208904 | tf_op jit(solution)/shard_map/ppermute | solution.py:581
  75.8 5.9 %collective-permute-done.5 = f32[136,128]{1,0:T(8,128)S(1)} collective-permute-done((f32[136,128]{1,0:T(8,128)S(1)}, f32[136,128]{1,0:T(8,128)S(1)}, u32[]{:S(2)}, u32[]{:S(2)}) %collective-permute-start.5) | collective-permute-done | bytes 69664 | tf_op jit(solution)/shard_map/ppermute | solution.py:581
  81.7 1.9 %collective-permute-start.6 = (f32[136,128]{1,0:T(8,128)S(1)}, f32[136,128]{1,0:T(8,128)S(1)}, u32[]{:S(2)}, u32[]{:S(2)}) collective-permute-start(f32[136,128]{1,0:T(8,128)S(1)} %get-tuple-element.23), channel_id=1, source_target_pairs={{0,16},{2,18},{4,20},{6,22},{8,24},{10,26},{12,28},{14,30},{16,0},... | collective-permute-start | bytes 208904 | tf_op jit(solution)/shard_map/ppermute | solution.py:581
  83.6 4.3 %collective-permute-done.6 = f32[136,128]{1,0:T(8,128)S(1)} collective-permute-done((f32[136,128]{1,0:T(8,128)S(1)}, f32[136,128]{1,0:T(8,128)S(1)}, u32[]{:S(2)}, u32[]{:S(2)}) %collective-permute-start.6) | collective-permute-done | bytes 69664 | tf_op jit(solution)/shard_map/ppermute | solution.py:581
  87.9 2.1 %collective-permute-start.7 = (f32[680,128]{1,0:T(8,128)S(1)}, f32[680,128]{1,0:T(8,128)S(1)}, u32[]{:S(2)}, u32[]{:S(2)}) collective-permute-start(f32[680,128]{1,0:T(8,128)S(1)} %add_dynamic-update-slice_fusion.mine), channel_id=1, source_target_pairs={{0,1},{1,0},{2,3},{3,2},{4,5},{5,4},{6,7},{7,6},{8,9},{9,8},{10,11... | collective-permute-start | bytes 1044488 | tf_op jit(solution)/shard_map/ppermute | solution.py:585
  90.0 1.4 %collective-permute-done.7.theirs = f32[680,128]{1,0:T(8,128)S(1)} collective-permute-done((f32[680,128]{1,0:T(8,128)S(1)}, f32[680,128]{1,0:T(8,128)S(1)}, u32[]{:S(2)}, u32[]{:S(2)}) %collective-permute-start.7) | collective-permute-done | bytes 348192 | tf_op jit(solution)/shard_map/ppermute | solution.py:585
  91.5 15.6 %shard_map.73 = (f32[4,256,128]{2,1,0:T(8,128)}, f32[3072,128]{1,0:T(8,128)}) custom-call(s32[1]{0:T(128)} %bitcast.me, f32[680,128]{1,0:T(8,128)S(1)} %add_dynamic-update-slice_fusion.mine, f32[680,128]{1,0:T(8,128)S(1)} %collective-permute-done.7.theirs, bf16[3072,256]{1,0:T(8,128)(2,1)S(1)} %get-tuple-element.20.highs, ...), custom_call_target="tpu_custom_call" | custom-call | tf_op jit(solution)/shard_map/pallas_call | solution.py:550
  (5 shorter events, 0.1 us)
Async XLA Ops:
  2.2 32.0 %collective-permute-start.1 = (bf16[136,3072]{1,0:T(8,128)(2,1)S(1)}, bf16[136,3072]{1,0:T(8,128)(2,1)S(1)}, u32[]{:S(2)}, u32[]{:S(2)}) collective-permute-start(bf16[136,3072]{1,0:T(8,128)(2,1)S(1)} %shard_map.68.stack), channel_id=1, source_target_pairs={{2,0},{4,2},{6,4},{8,6},{10,8},{12,10},{14,12},{16,14},{18,16},{20... | collective-permute-start | bytes 2506760 | tf_op jit(solution)/shard_map/ppermute | solution.py:577
  16.3 26.2 %collective-permute-start = (bf16[136,3072]{1,0:T(8,128)(2,1)S(1)}, bf16[136,3072]{1,0:T(8,128)(2,1)S(1)}, u32[]{:S(2)}, u32[]{:S(2)}) collective-permute-start(bf16[136,3072]{1,0:T(8,128)(2,1)S(1)} %shard_map.68.stack), channel_id=1, source_target_pairs={{0,2},{2,4},{4,6},{6,8},{8,10},{10,12},{12,14},{14,16},{16,18},{18... | collective-permute-start | bytes 2506760 | tf_op jit(solution)/shard_map/ppermute | solution.py:577
  52.7 5.3 %collective-permute-start.2 = (f32[3072,128]{1,0:T(8,128)S(1)}, f32[3072,128]{1,0:T(8,128)S(1)}, u32[]{:S(2)}, u32[]{:S(2)}) collective-permute-start(f32[3072,128]{1,0:T(8,128)S(1)} %shard_map.70.own), channel_id=1, source_target_pairs={{0,1},{1,0},{2,3},{3,2},{4,5},{5,4},{6,7},{7,6},{8,9},{9,8},{10,11... | collective-permute-start | bytes 4718600 | tf_op jit(solution)/shard_map/ppermute | solution.py:585
  59.1 6.6 %collective-permute-start.3 = (f32[136,128]{1,0:T(8,128)S(1)}, f32[136,128]{1,0:T(8,128)S(1)}, u32[]{:S(2)}, u32[]{:S(2)}) collective-permute-start(f32[136,128]{1,0:T(8,128)S(1)} %get-tuple-element.19), channel_id=1, source_target_pairs={{0,2},{2,0},{4,6},{6,4},{8,10},{10,8},{12,14},{14,12},{16,18},{18,... | collective-permute-start | bytes 208904 | tf_op jit(solution)/shard_map/ppermute | solution.py:581
  65.7 8.1 %collective-permute-start.4 = (f32[136,128]{1,0:T(8,128)S(1)}, f32[136,128]{1,0:T(8,128)S(1)}, u32[]{:S(2)}, u32[]{:S(2)}) collective-permute-start(f32[136,128]{1,0:T(8,128)S(1)} %get-tuple-element.27), channel_id=1, source_target_pairs={{0,4},{2,6},{4,0},{6,2},{8,12},{10,14},{12,8},{14,10},{16,20},{18,... | collective-permute-start | bytes 208904 | tf_op jit(solution)/shard_map/ppermute | solution.py:581
  73.9 7.8 %collective-permute-start.5 = (f32[136,128]{1,0:T(8,128)S(1)}, f32[136,128]{1,0:T(8,128)S(1)}, u32[]{:S(2)}, u32[]{:S(2)}) collective-permute-start(f32[136,128]{1,0:T(8,128)S(1)} %get-tuple-element.25), channel_id=1, source_target_pairs={{0,14},{2,12},{4,10},{6,8},{8,6},{10,4},{12,2},{14,0},{16,30},{18,... | collective-permute-start | bytes 208904 | tf_op jit(solution)/shard_map/ppermute | solution.py:581
  81.7 6.2 %collective-permute-start.6 = (f32[136,128]{1,0:T(8,128)S(1)}, f32[136,128]{1,0:T(8,128)S(1)}, u32[]{:S(2)}, u32[]{:S(2)}) collective-permute-start(f32[136,128]{1,0:T(8,128)S(1)} %get-tuple-element.23), channel_id=1, source_target_pairs={{0,16},{2,18},{4,20},{6,22},{8,24},{10,26},{12,28},{14,30},{16,0},... | collective-permute-start | bytes 208904 | tf_op jit(solution)/shard_map/ppermute | solution.py:581
  87.9 3.6 %collective-permute-start.7 = (f32[680,128]{1,0:T(8,128)S(1)}, f32[680,128]{1,0:T(8,128)S(1)}, u32[]{:S(2)}, u32[]{:S(2)}) collective-permute-start(f32[680,128]{1,0:T(8,128)S(1)} %add_dynamic-update-slice_fusion.mine), channel_id=1, source_target_pairs={{0,1},{1,0},{2,3},{3,2},{4,5},{5,4},{6,7},{7,6},{8,9},{9,8},{10,11... | collective-permute-start | bytes 1044488 | tf_op jit(solution)/shard_map/ppermute | solution.py:585
